TPU v7x, 1024 devices: a whole 4x8x16 slice. The times are simulated.
1024 devices in a mesh: frame: 64 (over x, z_lo, core), head: 16 (over z_hi, y).
Axes of the slice: x: 4, y: 8, z: 16 (z_hi: 2, z_lo: 8; z = z_hi * 8 + z_lo), core: 2. Of those that a mesh axis runs over, the one named last changes fastest.
Arguments:
- queries: bfloat16 [32768, 4096], P('frame', 'head'), may hold values from -500 to 500
- keys: bfloat16 [32768, 4096], P('frame', 'head'), may hold values from -20 to 20
- values: bfloat16 [32768, 4096], P('frame', 'head'), may hold values from -6 to 6
- cotangent: bfloat16 [32768, 4096], P('frame', 'head'), may hold values from -6 to 6
- kept: int32 [64, 6], replicated, may hold values from 0 to 3
Outputs:
- attended: bfloat16 [32768, 4096], P('frame', 'head')
- grad_queries: bfloat16 [32768, 4096], P('frame', 'head')
- grad_keys: bfloat16 [32768, 4096], P('frame', 'head')
- grad_values: bfloat16 [32768, 4096], P('frame', 'head')
All inputs are finite; a program needn't handle non-finite values.
Results may differ from a plain program's by a relative error of at most 0.024.
The roundings to bfloat16 on the way count: a program that leaves them out, or rounds other values in their place, can miss the bound.
Values may be sent and summed in bfloat16 or wider, within the bound.
No kernel may reach another device: no remote copies, remote signals or barrier semaphores. Data moves between devices by JAX's collectives and lax.ppermute only.
A program may use at most 32 MiB of HBM per device.

v0:
```python
import math

import jax
import jax.numpy as jnp
from jax import lax
from jax.sharding import PartitionSpec as P

HD = 128
BS = 128
LEVELS = 3


masked_score = -1e30
norm_eps = 1e-06


def from_behind(block, axis, distance):
    devices = range(lax.axis_size(axis))
    route = [(i - distance, i) for i in devices if i - distance in devices]
    return lax.ppermute(block, axis, route)


def attend_local(q_rows, k_rows, v_rows, d_rows, key_mask):
    factor = 1.0 / math.sqrt(q_rows.shape[2])
    scores = jnp.einsum("qhd,khd->hqk", q_rows, k_rows, preferred_element_type=jnp.float32) * factor
    scores = jnp.where(key_mask[None, None, :], scores, masked_score)
    top_score = jnp.max(scores, axis=2, keepdims=True)
    weights = jnp.exp(scores - top_score)
    probs = weights / jnp.sum(weights, axis=2, keepdims=True)
    probs_low = probs.astype(jnp.bfloat16)
    attended = jnp.einsum(
        "hqk,khd->qhd", probs_low, v_rows, preferred_element_type=jnp.float32
    ).astype(jnp.bfloat16)
    dprobs = jnp.einsum("qhd,khd->hqk", d_rows, v_rows, preferred_element_type=jnp.float32)
    inner = jnp.sum(d_rows.astype(jnp.float32) * attended.astype(jnp.float32), axis=2)
    dscores_low = (probs * (dprobs - jnp.transpose(inner)[:, :, None])).astype(jnp.bfloat16)
    grad_q = (
        factor * jnp.einsum("hqk,khd->qhd", dscores_low, k_rows, preferred_element_type=jnp.float32)
    ).astype(jnp.bfloat16)
    grad_k = factor * jnp.einsum(
        "hqk,qhd->khd", dscores_low, q_rows, preferred_element_type=jnp.float32
    )
    grad_v = jnp.einsum("hqk,qhd->khd", probs_low, d_rows, preferred_element_type=jnp.float32)
    return (attended, grad_q, grad_k, grad_v)


def slot_offset(slot_idx):
    level_idx = slot_idx // 2
    return 2**level_idx if slot_idx % 2 == 0 else -(2**level_idx)


def square_sums(rows):
    floats = rows.astype(jnp.float32)
    return jnp.sum(floats * floats, axis=1)


def normalize(rows, total, width_all):
    scale = lax.rsqrt(total / width_all + norm_eps)
    return (rows.astype(jnp.float32) * scale[:, None]).astype(jnp.bfloat16)


def on_device(queries, keys, values, cotangent, kept):
    frames = lax.axis_size("frame")
    frame_idx = lax.axis_index("frame")
    tokens = queries.shape[0]
    width = queries.shape[1]
    width_all = width * lax.axis_size("head")
    q_total, k_total = lax.psum((square_sums(queries), square_sums(keys)), "head")
    q_flat = normalize(queries, q_total, width_all)
    k_flat = normalize(keys, k_total, width_all)
    heads_dev = width // HD
    slot_count = 2 * LEVELS
    far_keys = [None] * slot_count
    far_values = [None] * slot_count
    live_flags = [None] * slot_count
    for slot_idx in range(slot_count):
        offset = slot_offset(slot_idx)
        whole_k, whole_v = from_behind((k_flat, values), "frame", -offset)
        wanted = kept[frame_idx, slot_idx] * BS
        got_k = lax.dynamic_slice_in_dim(whole_k, wanted, BS, 0)
        got_v = lax.dynamic_slice_in_dim(whole_v, wanted, BS, 0)
        far_keys[slot_idx] = got_k
        far_values[slot_idx] = got_v
        target = frame_idx + offset
        live_flags[slot_idx] = jnp.logical_and(target >= 0, target < frames)
    all_k = jnp.concatenate([k_flat] + far_keys, axis=0).reshape(-1, heads_dev, HD)
    all_v = jnp.concatenate([values] + far_values, axis=0).reshape(-1, heads_dev, HD)
    key_mask = jnp.concatenate(
        [jnp.ones((tokens,), dtype=bool)] + [jnp.broadcast_to(flag, (BS,)) for flag in live_flags]
    )
    local_shape = (tokens, heads_dev, HD)
    q_three = q_flat.reshape(local_shape)
    d_three = cotangent.reshape(local_shape)
    pieces_att = []
    pieces_q = []
    pieces_k = []
    pieces_v = []
    for head_idx in range(heads_dev):
        picked = slice(head_idx, head_idx + 1)
        one_att, one_q, one_k, one_v = attend_local(
            q_three[:, picked], all_k[:, picked], all_v[:, picked], d_three[:, picked], key_mask
        )
        pieces_att.append(one_att)
        pieces_q.append(one_q)
        pieces_k.append(one_k)
        pieces_v.append(one_v)
    attended = jnp.concatenate(pieces_att, axis=1).reshape(tokens, width)
    grad_q = jnp.concatenate(pieces_q, axis=1).reshape(tokens, width)
    grad_k = jnp.concatenate(pieces_k, axis=1).reshape(-1, width)
    grad_v = jnp.concatenate(pieces_v, axis=1).reshape(-1, width)
    own_k = grad_k[:tokens]
    own_v = grad_v[:tokens]
    for slot_idx in range(slot_count):
        offset = slot_offset(slot_idx)
        row_start = tokens + slot_idx * BS
        part_k = grad_k[row_start : row_start + BS]
        part_v = grad_v[row_start : row_start + BS]
        back_k, back_v = (
            from_behind(part_k.astype(jnp.bfloat16), "frame", offset).astype(part_k.dtype),
            from_behind(part_v.astype(jnp.bfloat16), "frame", offset).astype(part_v.dtype),
        )
        sender = jnp.clip(frame_idx - offset, 0, frames - 1)
        block_start = kept[sender, slot_idx] * BS
        current_k = lax.dynamic_slice_in_dim(own_k, block_start, BS, 0)
        current_v = lax.dynamic_slice_in_dim(own_v, block_start, BS, 0)
        own_k = lax.dynamic_update_slice_in_dim(own_k, current_k + back_k, block_start, 0)
        own_v = lax.dynamic_update_slice_in_dim(own_v, current_v + back_v, block_start, 0)
    return (attended, grad_q, own_k.astype(jnp.bfloat16), own_v.astype(jnp.bfloat16))


def solution(mesh):
    return jax.shard_map(
        on_device,
        mesh=mesh,
        in_specs=(
            P("frame", "head"),
            P("frame", "head"),
            P("frame", "head"),
            P("frame", "head"),
            P(),
        ),
        out_specs=(P("frame", "head"), P("frame", "head"), P("frame", "head"), P("frame", "head")),
        check_vma=False,
    )
```

profile of v0, /device:TPU:4, one launch (start us, length us, event | category | flops | bytes accessed | tf_op | source)
XLA Modules:
  0.0 268.5 jit_solution(11081352096260713396)
XLA Ops:
  0.7 1.1 copy.59
  1.9 1.1 copy.61
  3.1 85.8 %all-reduce = (f32[512]{0:T(512)S(1)}, f32[512]{0:T(512)S(1)}) all-reduce(f32[512]{0:T(512)S(1)} %fusion.28, f32[512]{0:T(512)S(1)} %fusion.26), channel_id=1, replica_groups=mesh['frame'=64,'head'=16] {'head'}, use_global_device_ids=true, to_apply=%region_3.0 | all-reduce | flops 1024 | bytes 8192 | tf_op jit(solution)/shard_map/psum | solution.py:68
  89.0 1.9 collective-permute-start.6
  90.9 2.4 collective-permute-start.7
  93.3 8.9 %collective-permute-start.8 = (bf16[512,256]{0,1:T(8,128)(2,1)S(1)}, bf16[512,256]{0,1:T(8,128)(2,1)}, u32[]{:S(2)}, u32[]{:S(2)}) collective-permute-start(bf16[512,256]{0,1:T(8,128)(2,1)S(1)} %get-tuple-element.21), channel_id=1, source_target_pairs={{32,0},{48,16},{64,32},{80,48},{96,64},{112,80},{128,96},{144,112}... | collective-permute-start | bytes 786440 | tf_op jit(solution)/shard_map/ppermute | solution.py:20
  102.2 1.9 collective-permute-start.9
  104.2 3.1 %collective-permute-start.10 = (bf16[512,256]{0,1:T(8,128)(2,1)S(1)}, bf16[512,256]{0,1:T(8,128)(2,1)S(1)}, u32[]{:S(2)}, u32[]{:S(2)}) collective-permute-start(bf16[512,256]{0,1:T(8,128)(2,1)S(1)} %get-tuple-element.21), channel_id=1, source_target_pairs={{64,0},{80,16},{96,32},{112,48},{128,64},{144,80},{160,96},{176,11... | collective-permute-start | bytes 786440 | tf_op jit(solution)/shard_map/ppermute | solution.py:20
  117.9 3.6 %collective-permute-start.11 = (bf16[512,256]{0,1:T(8,128)(2,1)S(1)}, bf16[512,256]{0,1:T(8,128)(2,1)S(1)}, u32[]{:S(2)}, u32[]{:S(2)}) collective-permute-start(bf16[512,256]{0,1:T(8,128)(2,1)S(1)} %get-tuple-element.21), channel_id=1, source_target_pairs={{0,64},{16,80},{32,96},{48,112},{64,128},{80,144},{96,160},{112,17... | collective-permute-start | bytes 786440 | tf_op jit(solution)/shard_map/ppermute | solution.py:20
  122.4 17.7 %collective-permute-start = (bf16[512,256]{0,1:T(8,128)(2,1)S(1)}, bf16[512,256]{0,1:T(8,128)(2,1)S(1)}, u32[]{:S(2)}, u32[]{:S(2)}) collective-permute-start(bf16[512,256]{0,1:T(8,128)(2,1)S(1)} %copy.57), channel_id=1, source_target_pairs={{16,0},{32,16},{48,32},{64,48},{80,64},{96,80},{112,96},{128,112},... | collective-permute-start | bytes 786440 | tf_op jit(solution)/shard_map/ppermute | solution.py:20
  141.0 1.9 collective-permute-start.1
  143.8 2.3 collective-permute-start.2
  146.2 3.5 %collective-permute-start.3 = (bf16[512,256]{0,1:T(8,128)(2,1)S(1)}, bf16[512,256]{0,1:T(8,128)(2,1)S(1)}, u32[]{:S(2)}, u32[]{:S(2)}) collective-permute-start(bf16[512,256]{0,1:T(8,128)(2,1)S(1)} %copy.57), channel_id=1, source_target_pairs={{0,32},{16,48},{32,64},{48,80},{64,96},{80,112},{96,128},{112,144}... | collective-permute-start | bytes 786440 | tf_op jit(solution)/shard_map/ppermute | solution.py:20
  149.8 1.9 collective-permute-start.4
  156.0 4.8 %collective-permute-start.5 = (bf16[512,256]{0,1:T(8,128)(2,1)S(1)}, bf16[512,256]{0,1:T(8,128)(2,1)S(1)}, u32[]{:S(2)}, u32[]{:S(2)}) collective-permute-start(bf16[512,256]{0,1:T(8,128)(2,1)S(1)} %copy.57), channel_id=1, source_target_pairs={{0,64},{16,80},{32,96},{48,112},{64,128},{80,144},{96,160},{112,17... | collective-permute-start | bytes 786440 | tf_op jit(solution)/shard_map/ppermute | solution.py:20
  161.0 1.2 collective-permute-done.3
  162.3 4.1 %collective-permute-done.4 = bf16[512,256]{0,1:T(8,128)(2,1)S(1)} collective-permute-done((bf16[512,256]{0,1:T(8,128)(2,1)S(1)}, bf16[512,256]{0,1:T(8,128)(2,1)S(1)}, u32[]{:S(2)}, u32[]{:S(2)}) %collective-permute-start.4) | collective-permute-done | bytes 262176 | tf_op jit(solution)/shard_map/ppermute | solution.py:20
  166.5 13.6 %collective-permute-done.5 = bf16[512,256]{0,1:T(8,128)(2,1)S(1)} collective-permute-done((bf16[512,256]{0,1:T(8,128)(2,1)S(1)}, bf16[512,256]{0,1:T(8,128)(2,1)S(1)}, u32[]{:S(2)}, u32[]{:S(2)}) %collective-permute-start.5) | collective-permute-done | bytes 262176 | tf_op jit(solution)/shard_map/ppermute | solution.py:20
  185.3 3.3 %collective-permute-start.18 = (bf16[128,256]{1,0:T(8,128)(2,1)}, bf16[128,256]{1,0:T(8,128)(2,1)S(1)}, u32[]{:S(2)}, u32[]{:S(2)}) collective-permute-start(bf16[128,256]{1,0:T(8,128)(2,1)} %copy.78), channel_id=1, source_target_pairs={{0,16},{16,32},{32,48},{48,64},{64,80},{80,96},{96,112},{112,128},... | collective-permute-start | bytes 196616 | tf_op jit(solution)/shard_map/ppermute | solution.py:20
  189.5 9.8 %collective-permute-start.19 = (bf16[128,256]{1,0:T(8,128)(2,1)}, bf16[128,256]{1,0:T(8,128)(2,1)S(1)}, u32[]{:S(2)}, u32[]{:S(2)}) collective-permute-start(bf16[128,256]{1,0:T(8,128)(2,1)} %copy.80), channel_id=1, source_target_pairs={{16,0},{32,16},{48,32},{64,48},{80,64},{96,80},{112,96},{128,112},... | collective-permute-start | bytes 196616 | tf_op jit(solution)/shard_map/ppermute | solution.py:20
  200.0 1.9 collective-permute-start.20
  202.7 11.4 %collective-permute-start.21 = (bf16[128,256]{1,0:T(8,128)(2,1)}, bf16[128,256]{1,0:T(8,128)(2,1)S(1)}, u32[]{:S(2)}, u32[]{:S(2)}) collective-permute-start(bf16[128,256]{1,0:T(8,128)(2,1)} %copy.82), channel_id=1, source_target_pairs={{32,0},{48,16},{64,32},{80,48},{96,64},{112,80},{128,96},{144,112}... | collective-permute-start | bytes 196616 | tf_op jit(solution)/shard_map/ppermute | solution.py:20
  214.8 1.9 collective-permute-start.22
  219.6 1.9 collective-permute-start.12
  221.6 11.4 %collective-permute-done.12 = bf16[128,256]{1,0:T(8,128)(2,1)S(1)} collective-permute-done((bf16[128,256]{1,0:T(8,128)(2,1)S(1)}, bf16[128,256]{1,0:T(8,128)(2,1)S(1)}, u32[]{:S(2)}, u32[]{:S(2)}) %collective-permute-start.12) | collective-permute-done | bytes 65568 | tf_op jit(solution)/shard_map/ppermute | solution.py:20
  233.0 2.7 %collective-permute-start.23 = (bf16[128,256]{1,0:T(8,128)(2,1)S(1)}, bf16[128,256]{1,0:T(8,128)(2,1)S(1)}, u32[]{:S(2)}, u32[]{:S(2)}) collective-permute-start(bf16[128,256]{1,0:T(8,128)(2,1)S(1)} %copy.84), channel_id=1, source_target_pairs={{64,0},{80,16},{96,32},{112,48},{128,64},{144,80},{160,96},{176,11... | collective-permute-start | bytes 196616 | tf_op jit(solution)/shard_map/ppermute | solution.py:20
  235.7 1.9 collective-permute-start.13
  237.7 1.9 collective-permute-done.13
  239.6 1.9 collective-permute-start.14
  241.5 11.4 %collective-permute-start.15 = (bf16[128,256]{1,0:T(8,128)(2,1)S(1)}, bf16[128,256]{1,0:T(8,128)(2,1)S(1)}, u32[]{:S(2)}, u32[]{:S(2)}) collective-permute-start(bf16[128,256]{1,0:T(8,128)(2,1)S(1)} %copy.74), channel_id=1, source_target_pairs={{32,0},{48,16},{64,32},{80,48},{96,64},{112,80},{128,96},{144,112}... | collective-permute-start | bytes 196616 | tf_op jit(solution)/shard_map/ppermute | solution.py:20
  253.4 1.9 collective-permute-start.16
  255.3 10.5 %collective-permute-start.17 = (bf16[128,256]{1,0:T(8,128)(2,1)S(1)}, bf16[128,256]{1,0:T(8,128)(2,1)S(1)}, u32[]{:S(2)}, u32[]{:S(2)}) collective-permute-start(bf16[128,256]{1,0:T(8,128)(2,1)S(1)} %copy.76), channel_id=1, source_target_pairs={{64,0},{80,16},{96,32},{112,48},{128,64},{144,80},{160,96},{176,11... | collective-permute-start | bytes 196616 | tf_op jit(solution)/shard_map/ppermute | solution.py:20
  (115 shorter events, 24.3 us)
Async XLA Ops:
  0.6 106.7 %copy-start = (bf16[512,256]{1,0:T(8,128)(2,1)S(1)}, bf16[512,256]{1,0:T(8,128)(2,1)}, u32[]{:S(2)}) copy-start(bf16[512,256]{1,0:T(8,128)(2,1)} %param.7) | copy-start | bytes 786436
  0.6 106.9 %copy-start.2 = (s32[64,6]{0,1:T(8,128)S(1)}, s32[64,6]{0,1:T(8,128)}, u32[]{:S(2)}) copy-start(s32[64,6]{0,1:T(8,128)} %param.9) | copy-start | bytes 4612
  0.7 115.3 %copy-start.1 = (bf16[512,256]{1,0:T(8,128)(2,1)S(1)}, bf16[512,256]{1,0:T(8,128)(2,1)}, u32[]{:S(2)}) copy-start(bf16[512,256]{1,0:T(8,128)(2,1)} %param.8) | copy-start | bytes 786436
  89.0 28.9 %collective-permute-start.6 = (bf16[512,256]{0,1:T(8,128)(2,1)S(1)}, bf16[512,256]{0,1:T(8,128)(2,1)}, u32[]{:S(2)}, u32[]{:S(2)}) collective-permute-start(bf16[512,256]{0,1:T(8,128)(2,1)S(1)} %get-tuple-element.21), channel_id=1, source_target_pairs={{16,0},{32,16},{48,32},{64,48},{80,64},{96,80},{112,96},{128,112},... | collective-permute-start | bytes 786440 | tf_op jit(solution)/shard_map/ppermute | solution.py:20
  90.9 31.5 %collective-permute-start.7 = (bf16[512,256]{0,1:T(8,128)(2,1)S(1)}, bf16[512,256]{0,1:T(8,128)(2,1)}, u32[]{:S(2)}, u32[]{:S(2)}) collective-permute-start(bf16[512,256]{0,1:T(8,128)(2,1)S(1)} %get-tuple-element.21), channel_id=1, source_target_pairs={{0,16},{16,32},{32,48},{48,64},{64,80},{80,96},{96,112},{112,128},... | collective-permute-start | bytes 786440 | tf_op jit(solution)/shard_map/ppermute | solution.py:20
  93.3 47.7 %collective-permute-start.8 = (bf16[512,256]{0,1:T(8,128)(2,1)S(1)}, bf16[512,256]{0,1:T(8,128)(2,1)}, u32[]{:S(2)}, u32[]{:S(2)}) collective-permute-start(bf16[512,256]{0,1:T(8,128)(2,1)S(1)} %get-tuple-element.21), channel_id=1, source_target_pairs={{32,0},{48,16},{64,32},{80,48},{96,64},{112,80},{128,96},{144,112}... | collective-permute-start | bytes 786440 | tf_op jit(solution)/shard_map/ppermute | solution.py:20
  102.2 41.6 %collective-permute-start.9 = (bf16[512,256]{0,1:T(8,128)(2,1)S(1)}, bf16[512,256]{0,1:T(8,128)(2,1)S(1)}, u32[]{:S(2)}, u32[]{:S(2)}) collective-permute-start(bf16[512,256]{0,1:T(8,128)(2,1)S(1)} %get-tuple-element.21), channel_id=1, source_target_pairs={{0,32},{16,48},{32,64},{48,80},{64,96},{80,112},{96,128},{112,144}... | collective-permute-start | bytes 786440 | tf_op jit(solution)/shard_map/ppermute | solution.py:20
  104.2 42.0 %collective-permute-start.10 = (bf16[512,256]{0,1:T(8,128)(2,1)S(1)}, bf16[512,256]{0,1:T(8,128)(2,1)S(1)}, u32[]{:S(2)}, u32[]{:S(2)}) collective-permute-start(bf16[512,256]{0,1:T(8,128)(2,1)S(1)} %get-tuple-element.21), channel_id=1, source_target_pairs={{64,0},{80,16},{96,32},{112,48},{128,64},{144,80},{160,96},{176,11... | collective-permute-start | bytes 786440 | tf_op jit(solution)/shard_map/ppermute | solution.py:20
  117.9 31.9 %collective-permute-start.11 = (bf16[512,256]{0,1:T(8,128)(2,1)S(1)}, bf16[512,256]{0,1:T(8,128)(2,1)S(1)}, u32[]{:S(2)}, u32[]{:S(2)}) collective-permute-start(bf16[512,256]{0,1:T(8,128)(2,1)S(1)} %get-tuple-element.21), channel_id=1, source_target_pairs={{0,64},{16,80},{32,96},{48,112},{64,128},{80,144},{96,160},{112,17... | collective-permute-start | bytes 786440 | tf_op jit(solution)/shard_map/ppermute | solution.py:20
  122.4 33.6 %collective-permute-start = (bf16[512,256]{0,1:T(8,128)(2,1)S(1)}, bf16[512,256]{0,1:T(8,128)(2,1)S(1)}, u32[]{:S(2)}, u32[]{:S(2)}) collective-permute-start(bf16[512,256]{0,1:T(8,128)(2,1)S(1)} %copy.57), channel_id=1, source_target_pairs={{16,0},{32,16},{48,32},{64,48},{80,64},{96,80},{112,96},{128,112},... | collective-permute-start | bytes 786440 | tf_op jit(solution)/shard_map/ppermute | solution.py:20
  141.0 19.9 %collective-permute-start.1 = (bf16[512,256]{0,1:T(8,128)(2,1)S(1)}, bf16[512,256]{0,1:T(8,128)(2,1)S(1)}, u32[]{:S(2)}, u32[]{:S(2)}) collective-permute-start(bf16[512,256]{0,1:T(8,128)(2,1)S(1)} %copy.57), channel_id=1, source_target_pairs={{0,16},{16,32},{32,48},{48,64},{64,80},{80,96},{96,112},{112,128},... | collective-permute-start | bytes 786440 | tf_op jit(solution)/shard_map/ppermute | solution.py:20
  143.8 17.1 %collective-permute-start.2 = (bf16[512,256]{0,1:T(8,128)(2,1)S(1)}, bf16[512,256]{0,1:T(8,128)(2,1)S(1)}, u32[]{:S(2)}, u32[]{:S(2)}) collective-permute-start(bf16[512,256]{0,1:T(8,128)(2,1)S(1)} %copy.57), channel_id=1, source_target_pairs={{32,0},{48,16},{64,32},{80,48},{96,64},{112,80},{128,96},{144,112}... | collective-permute-start | bytes 786440 | tf_op jit(solution)/shard_map/ppermute | solution.py:20
  146.2 16.0 %collective-permute-start.3 = (bf16[512,256]{0,1:T(8,128)(2,1)S(1)}, bf16[512,256]{0,1:T(8,128)(2,1)S(1)}, u32[]{:S(2)}, u32[]{:S(2)}) collective-permute-start(bf16[512,256]{0,1:T(8,128)(2,1)S(1)} %copy.57), channel_id=1, source_target_pairs={{0,32},{16,48},{32,64},{48,80},{64,96},{80,112},{96,128},{112,144}... | collective-permute-start | bytes 786440 | tf_op jit(solution)/shard_map/ppermute | solution.py:20
  149.8 16.6 %collective-permute-start.4 = (bf16[512,256]{0,1:T(8,128)(2,1)S(1)}, bf16[512,256]{0,1:T(8,128)(2,1)S(1)}, u32[]{:S(2)}, u32[]{:S(2)}) collective-permute-start(bf16[512,256]{0,1:T(8,128)(2,1)S(1)} %copy.57), channel_id=1, source_target_pairs={{64,0},{80,16},{96,32},{112,48},{128,64},{144,80},{160,96},{176,11... | collective-permute-start | bytes 786440 | tf_op jit(solution)/shard_map/ppermute | solution.py:20
  156.0 24.1 %collective-permute-start.5 = (bf16[512,256]{0,1:T(8,128)(2,1)S(1)}, bf16[512,256]{0,1:T(8,128)(2,1)S(1)}, u32[]{:S(2)}, u32[]{:S(2)}) collective-permute-start(bf16[512,256]{0,1:T(8,128)(2,1)S(1)} %copy.57), channel_id=1, source_target_pairs={{0,64},{16,80},{32,96},{48,112},{64,128},{80,144},{96,160},{112,17... | collective-permute-start | bytes 786440 | tf_op jit(solution)/shard_map/ppermute | solution.py:20
  185.3 34.3 %collective-permute-start.18 = (bf16[128,256]{1,0:T(8,128)(2,1)}, bf16[128,256]{1,0:T(8,128)(2,1)S(1)}, u32[]{:S(2)}, u32[]{:S(2)}) collective-permute-start(bf16[128,256]{1,0:T(8,128)(2,1)} %copy.78), channel_id=1, source_target_pairs={{0,16},{16,32},{32,48},{48,64},{64,80},{80,96},{96,112},{112,128},... | collective-permute-start | bytes 196616 | tf_op jit(solution)/shard_map/ppermute | solution.py:20
  189.5 46.2 %collective-permute-start.19 = (bf16[128,256]{1,0:T(8,128)(2,1)}, bf16[128,256]{1,0:T(8,128)(2,1)S(1)}, u32[]{:S(2)}, u32[]{:S(2)}) collective-permute-start(bf16[128,256]{1,0:T(8,128)(2,1)} %copy.80), channel_id=1, source_target_pairs={{16,0},{32,16},{48,32},{64,48},{80,64},{96,80},{112,96},{128,112},... | collective-permute-start | bytes 196616 | tf_op jit(solution)/shard_map/ppermute | solution.py:20
  200.0 41.5 %collective-permute-start.20 = (bf16[128,256]{1,0:T(8,128)(2,1)}, bf16[128,256]{1,0:T(8,128)(2,1)S(1)}, u32[]{:S(2)}, u32[]{:S(2)}) collective-permute-start(bf16[128,256]{1,0:T(8,128)(2,1)} %copy.81), channel_id=1, source_target_pairs={{0,32},{16,48},{32,64},{48,80},{64,96},{80,112},{96,128},{112,144}... | collective-permute-start | bytes 196616 | tf_op jit(solution)/shard_map/ppermute | solution.py:20
  202.7 52.7 %collective-permute-start.21 = (bf16[128,256]{1,0:T(8,128)(2,1)}, bf16[128,256]{1,0:T(8,128)(2,1)S(1)}, u32[]{:S(2)}, u32[]{:S(2)}) collective-permute-start(bf16[128,256]{1,0:T(8,128)(2,1)} %copy.82), channel_id=1, source_target_pairs={{32,0},{48,16},{64,32},{80,48},{96,64},{112,80},{128,96},{144,112}... | collective-permute-start | bytes 196616 | tf_op jit(solution)/shard_map/ppermute | solution.py:20
  214.8 51.1 %collective-permute-start.22 = (bf16[128,256]{1,0:T(8,128)(2,1)}, bf16[128,256]{1,0:T(8,128)(2,1)S(1)}, u32[]{:S(2)}, u32[]{:S(2)}) collective-permute-start(bf16[128,256]{1,0:T(8,128)(2,1)} %copy.83), channel_id=1, source_target_pairs={{0,64},{16,80},{32,96},{48,112},{64,128},{80,144},{96,160},{112,17... | collective-permute-start | bytes 196616 | tf_op jit(solution)/shard_map/ppermute | solution.py:20
  219.6 13.4 %collective-permute-start.12 = (bf16[128,256]{1,0:T(8,128)(2,1)S(1)}, bf16[128,256]{1,0:T(8,128)(2,1)S(1)}, u32[]{:S(2)}, u32[]{:S(2)}) collective-permute-start(bf16[128,256]{1,0:T(8,128)(2,1)S(1)} %copy.70), channel_id=1, source_target_pairs={{0,16},{16,32},{32,48},{48,64},{64,80},{80,96},{96,112},{112,128},... | collective-permute-start | bytes 196616 | tf_op jit(solution)/shard_map/ppermute | solution.py:20
  233.0 33.3 %collective-permute-start.23 = (bf16[128,256]{1,0:T(8,128)(2,1)S(1)}, bf16[128,256]{1,0:T(8,128)(2,1)S(1)}, u32[]{:S(2)}, u32[]{:S(2)}) collective-permute-start(bf16[128,256]{1,0:T(8,128)(2,1)S(1)} %copy.84), channel_id=1, source_target_pairs={{64,0},{80,16},{96,32},{112,48},{128,64},{144,80},{160,96},{176,11... | collective-permute-start | bytes 196616 | tf_op jit(solution)/shard_map/ppermute | solution.py:20
  235.7 3.8 %collective-permute-start.13 = (bf16[128,256]{1,0:T(8,128)(2,1)S(1)}, bf16[128,256]{1,0:T(8,128)(2,1)S(1)}, u32[]{:S(2)}, u32[]{:S(2)}) collective-permute-start(bf16[128,256]{1,0:T(8,128)(2,1)S(1)} %copy.72), channel_id=1, source_target_pairs={{16,0},{32,16},{48,32},{64,48},{80,64},{96,80},{112,96},{128,112},... | collective-permute-start | bytes 196616 | tf_op jit(solution)/shard_map/ppermute | solution.py:20
  239.6 13.8 %collective-permute-start.14 = (bf16[128,256]{1,0:T(8,128)(2,1)S(1)}, bf16[128,256]{1,0:T(8,128)(2,1)S(1)}, u32[]{:S(2)}, u32[]{:S(2)}) collective-permute-start(bf16[128,256]{1,0:T(8,128)(2,1)S(1)} %copy.73), channel_id=1, source_target_pairs={{0,32},{16,48},{32,64},{48,80},{64,96},{80,112},{96,128},{112,144}... | collective-permute-start | bytes 196616 | tf_op jit(solution)/shard_map/ppermute | solution.py:20
  241.5 24.4 %collective-permute-start.15 = (bf16[128,256]{1,0:T(8,128)(2,1)S(1)}, bf16[128,256]{1,0:T(8,128)(2,1)S(1)}, u32[]{:S(2)}, u32[]{:S(2)}) collective-permute-start(bf16[128,256]{1,0:T(8,128)(2,1)S(1)} %copy.74), channel_id=1, source_target_pairs={{32,0},{48,16},{64,32},{80,48},{96,64},{112,80},{128,96},{144,112}... | collective-permute-start | bytes 196616 | tf_op jit(solution)/shard_map/ppermute | solution.py:20
  253.4 12.8 %collective-permute-start.16 = (bf16[128,256]{1,0:T(8,128)(2,1)S(1)}, bf16[128,256]{1,0:T(8,128)(2,1)S(1)}, u32[]{:S(2)}, u32[]{:S(2)}) collective-permute-start(bf16[128,256]{1,0:T(8,128)(2,1)S(1)} %copy.75), channel_id=1, source_target_pairs={{0,64},{16,80},{32,96},{48,112},{64,128},{80,144},{96,160},{112,17... | collective-permute-start | bytes 196616 | tf_op jit(solution)/shard_map/ppermute | solution.py:20
  255.3 12.4 %collective-permute-start.17 = (bf16[128,256]{1,0:T(8,128)(2,1)S(1)}, bf16[128,256]{1,0:T(8,128)(2,1)S(1)}, u32[]{:S(2)}, u32[]{:S(2)}) collective-permute-start(bf16[128,256]{1,0:T(8,128)(2,1)S(1)} %copy.76), channel_id=1, source_target_pairs={{64,0},{80,16},{96,32},{112,48},{128,64},{144,80},{160,96},{176,11... | collective-permute-start | bytes 196616 | tf_op jit(solution)/shard_map/ppermute | solution.py:20
where the time goes:
time: 270 us; the launch traced here: 269 us
  starting transfers between devices  115 us (43%)
  blocking collectives  85.8 us (32%)
  waiting for transfers between devices  33.6 us (12%)
  local copies, waits for them, and re-layouts  14.5 us (5%)
  between operations  9.17 us (3%)
  matrix products  6.09 us (2%)
  other arithmetic  4.6 us (2%)
    ppermute x24, starting transfers between devices, from_behind(): return lax.ppermute(block, axis, route)  115 us
    psum x1, blocking collectives, on_device(): lax.psum((square_sums(queries), square_sums(keys)), 'head')  85.8 us
    ppermute x24, waiting for transfers between devices, from_behind(): return lax.ppermute(block, axis, route)  33.6 us
    unnamed x29, local copies, waits for them, and re-layouts  8.45 us
  transfers between devices with their start and end apart: 24, of which 8 were waited for; matrix products, arithmetic and copies ran while one was open for 6% of the time, Pallas kernels for 0%

commit v1 on v0

v1 whole, which is shorter than its diff:
```python
import functools
import math

import jax
import jax.numpy as jnp
from jax import lax
from jax.experimental import pallas as pl
from jax.experimental.pallas import tpu as pltpu
from jax.sharding import PartitionSpec as P

HD = 128
BS = 128
EXCHANGES = ((1, False), (4, True), (4, False), (2, True), (2, False), (1, True))

masked_score = -1e30
norm_eps = 1e-06

VMEM = pl.BlockSpec(memory_space=pltpu.VMEM)
SMEM = pl.BlockSpec(memory_space=pltpu.SMEM)


def params(mib):
    return pltpu.CompilerParams(vmem_limit_bytes=mib << 20)


def route(distance, shifted, frames):
    pairs = []
    for low in range(frames - distance):
        if ((low // distance) % 2 == 1) == shifted:
            pairs += [(low, low + distance), (low + distance, low)]
    return pairs


def partner(frame, distance, shifted):
    up = ((frame // distance) % 2 == 1) == shifted
    level = int(math.log2(distance))
    offset = jnp.where(up, distance, -distance)
    slot = jnp.where(up, 2 * level + 1, 2 * level)
    return offset, slot


def block_start(kept_ref, frame, frames, distance, shifted):
    offset, slot = partner(frame, distance, shifted)
    other = jnp.clip(frame + offset, 0, frames - 1)
    return pl.multiple_of(kept_ref[other, slot] * BS, BS)


def is_live(frame, frames, distance, shifted):
    offset, _ = partner(frame, distance, shifted)
    other = frame + offset
    return jnp.logical_and(other >= 0, other < frames)


def sums_kernel(q_ref, k_ref, out_ref):
    rows = []
    for ref in (q_ref, k_ref):
        for start in range(0, ref.shape[0], 128):
            total = jnp.zeros((128, 128), jnp.float32)
            for column in range(0, ref.shape[1], 128):
                part = ref[start : start + 128, column : column + 128].astype(jnp.float32)
                total += part * part
            rows.append(jnp.sum(total.T, axis=0, keepdims=True))
    packed = jnp.concatenate(rows, axis=0)
    for copy in range(out_ref.shape[0]):
        out_ref[copy] = packed


def norm_kernel(frames, width_all, frame_ref, kept_ref, sums_ref, q_ref, k_ref, v_ref, qn_ref, kn_ref, *block_refs):
    frame = frame_ref[0]
    width = q_ref.shape[1]
    total = sums_ref[0]
    for part in range(1, sums_ref.shape[0]):
        total += sums_ref[part]
    scale = lax.rsqrt(total / width_all + norm_eps)
    row = 0
    for ref, out in ((q_ref, qn_ref), (k_ref, kn_ref)):
        for start in range(0, ref.shape[0], 128):
            by_row = jnp.broadcast_to(scale[row : row + 1, :], (128, 128)).T
            row += 1
            for column in range(0, width, 128):
                part = ref[start : start + 128, column : column + 128].astype(jnp.float32)
                out[start : start + 128, column : column + 128] = (part * by_row).astype(jnp.bfloat16)
    for (distance, shifted), block in zip(EXCHANGES, block_refs):
        rows = pl.ds(block_start(kept_ref, frame, frames, distance, shifted), BS)
        block[:, :width] = kn_ref[rows, :]
        block[:, width:] = v_ref[rows, :]


def attend_kernel(frames, frame_ref, q_ref, k_ref, v_ref, d_ref, *refs):
    far_refs = refs[:6]
    att_ref, gq_ref, gk_ref, gv_ref = refs[6:10]
    back_refs = refs[10:16]
    k_all, v_all, p_all, s_all = refs[16:]
    frame = frame_ref[0]
    tokens, width = q_ref.shape
    factor = 1.0 / math.sqrt(HD)
    k_all[:tokens] = k_ref[...]
    v_all[:tokens] = v_ref[...]
    for slot, far in enumerate(far_refs):
        rows = slice(tokens + slot * BS, tokens + (slot + 1) * BS)
        k_all[rows] = far[:, :width]
        v_all[rows] = far[:, width:]
    live = [is_live(frame, frames, distance, shifted) for distance, shifted in EXCHANGES]
    total_keys = k_all.shape[0]
    chunk = 256
    contract_last = (((1,), (1,)), ((), ()))
    contract_first = (((0,), (0,)), ((), ()))
    f32 = jnp.float32
    column = lax.broadcasted_iota(jnp.int32, (1, total_keys), 1)
    allowed = column < tokens
    for slot, flag in enumerate(live):
        low = tokens + slot * BS
        inside = jnp.logical_and(column >= low, column < low + BS)
        allowed = jnp.logical_or(allowed, jnp.logical_and(inside, flag))
    for start in range(0, width, HD):
        head = slice(start, start + HD)
        keys, vals = k_all[:, head], v_all[:, head]
        for first in range(0, tokens, chunk):
            rows = slice(first, first + chunk)
            grads = d_ref[rows, head]
            scores = lax.dot_general(q_ref[rows, head], keys, contract_last, preferred_element_type=f32) * factor
            scores = jnp.where(allowed, scores, masked_score)
            weights = jnp.exp(scores - jnp.max(scores, axis=1, keepdims=True))
            probs = weights * (1.0 / jnp.sum(weights, axis=1, keepdims=True))
            probs_low = probs.astype(jnp.bfloat16)
            p_all[rows, :] = probs_low
            attended = jnp.dot(probs_low, vals, preferred_element_type=f32).astype(jnp.bfloat16)
            att_ref[rows, head] = attended
            inner = jnp.sum(grads.astype(f32) * attended.astype(f32), axis=1, keepdims=True)
            dprobs = lax.dot_general(grads, vals, contract_last, preferred_element_type=f32)
            dscores = (probs * (dprobs - inner)).astype(jnp.bfloat16)
            s_all[rows, :] = dscores
            grad_q = jnp.dot(dscores, keys, preferred_element_type=f32) * factor
            gq_ref[rows, head] = grad_q.astype(jnp.bfloat16)
        grad_k = lax.dot_general(s_all[...], q_ref[:, head], contract_first, preferred_element_type=f32) * factor
        grad_v = lax.dot_general(p_all[...], d_ref[:, head], contract_first, preferred_element_type=f32)
        gk_ref[:, head] = grad_k[:tokens]
        gv_ref[:, head] = grad_v[:tokens]
        for slot, back in enumerate(back_refs):
            rows = slice(tokens + slot * BS, tokens + (slot + 1) * BS)
            back[:, start : start + HD] = grad_k[rows].astype(jnp.bfloat16)
            back[:, width + start : width + start + HD] = grad_v[rows].astype(jnp.bfloat16)


def collect_kernel(frames, frame_ref, kept_ref, gk_ref, gv_ref, *refs):
    back_refs, (outk_ref, outv_ref, acc_k, acc_v) = refs[:6], refs[6:]
    frame = frame_ref[0]
    width = gk_ref.shape[1]
    acc_k[...] = gk_ref[...]
    acc_v[...] = gv_ref[...]
    for (distance, shifted), back in zip(EXCHANGES, back_refs):
        rows = pl.ds(block_start(kept_ref, frame, frames, distance, shifted), BS)

        @pl.when(is_live(frame, frames, distance, shifted))
        def _():
            acc_k[rows, :] += back[:, :width].astype(jnp.float32)
            acc_v[rows, :] += back[:, width:].astype(jnp.float32)

    outk_ref[...] = acc_k[...].astype(jnp.bfloat16)
    outv_ref[...] = acc_v[...].astype(jnp.bfloat16)


def swap(blocks, frames):
    return [
        lax.ppermute(block, "frame", route(distance, shifted, frames))
        for (distance, shifted), block in zip(EXCHANGES, blocks)
    ]


def on_device(queries, keys, values, cotangent, kept):
    frames = lax.axis_size("frame")
    heads = lax.axis_size("head")
    tokens, width = queries.shape
    frame = lax.axis_index("frame").reshape(1)
    flat = jax.ShapeDtypeStruct((tokens, width), jnp.bfloat16)
    wide = jax.ShapeDtypeStruct((tokens, width), jnp.float32)
    block = jax.ShapeDtypeStruct((BS, 2 * width), jnp.bfloat16)
    sums = pl.pallas_call(
        sums_kernel,
        out_shape=jax.ShapeDtypeStruct((heads, 2 * tokens // 128, 128), jnp.float32),
        in_specs=[VMEM] * 2,
        out_specs=VMEM,
        compiler_params=params(6),
        name="square_sums",
    )(queries, keys)
    sums = lax.all_to_all(sums, "head", 0, 0)
    q_norm, k_norm, *sent = pl.pallas_call(
        functools.partial(norm_kernel, frames, width * heads),
        out_shape=[flat, flat] + [block] * 6,
        in_specs=[SMEM] * 2 + [VMEM] * 4,
        out_specs=[VMEM] * 8,
        compiler_params=params(8),
        name="normalize",
    )(frame, kept, sums, queries, keys, values)
    far = swap(sent, frames)
    total_keys = tokens + 6 * BS
    attended, grad_q, own_k, own_v, *back = pl.pallas_call(
        functools.partial(attend_kernel, frames),
        out_shape=[flat, flat, wide, wide] + [block] * 6,
        in_specs=[SMEM] + [VMEM] * 10,
        out_specs=[VMEM] * 10,
        scratch_shapes=[
            pltpu.VMEM((total_keys, width), jnp.bfloat16),
            pltpu.VMEM((total_keys, width), jnp.bfloat16),
            pltpu.VMEM((tokens, total_keys), jnp.bfloat16),
            pltpu.VMEM((tokens, total_keys), jnp.bfloat16),
        ],
        compiler_params=params(32),
        name="attend",
    )(frame, q_norm, k_norm, values, cotangent, *far)
    back = swap(back, frames)
    grad_k, grad_v = pl.pallas_call(
        functools.partial(collect_kernel, frames),
        out_shape=[flat, flat],
        in_specs=[SMEM] * 2 + [VMEM] * 8,
        out_specs=[VMEM] * 2,
        scratch_shapes=[pltpu.VMEM((tokens, width), jnp.float32)] * 2,
        compiler_params=params(8),
        name="collect",
    )(frame, kept, own_k, own_v, *back)
    return attended, grad_q, grad_k, grad_v


def solution(mesh):
    spec = P("frame", "head")
    return jax.shard_map(
        on_device,
        mesh=mesh,
        in_specs=(spec, spec, spec, spec, P()),
        out_specs=(spec, spec, spec, spec),
        check_vma=False,
    )
```

time: 270 us -> 121 us (0.45)
  the two profiles are of different devices: /device:TPU:4 before, /device:TPU:6 now
where the time goes in v1:
time: 121 us; the launch traced here: 120 us
  starting transfers between devices  74.7 us (62%)
  waiting for transfers between devices  30 us (25%)
  Pallas kernels  11.2 us (9%)
  local copies, waits for them, and re-layouts  3.63 us (3%)
    ppermute x12, starting transfers between devices, swap(): lax.ppermute(block, 'frame', route(distance, shifted, frames))  50.6 us
    all_to_all x1, starting transfers between devices, on_device(): sums = lax.all_to_all(sums, 'head', 0, 0)  24.1 us
    all_to_all x1, waiting for transfers between devices, on_device(): sums = lax.all_to_all(sums, 'head', 0, 0)  16.4 us
    ppermute x12, waiting for transfers between devices, swap(): lax.ppermute(block, 'frame', route(distance, shifted, frames))  13.5 us
    pallas_call x1, Pallas kernels, on_device(): pl.pallas_call(functools.partial(attend_kernel, frames), out_shape=[flat,...  6.86 us
    unnamed x17, local copies, waits for them, and re-layouts  3.63 us
  transfers between devices with their start and end apart: 13, of which 5 were waited for; matrix products, arithmetic and copies ran while one was open for 0% of the time, Pallas kernels for 0%

profile of v1, /device:TPU:6, one launch (start us, length us, event | category | flops | bytes accessed | tf_op | source)
XLA Modules:
  0.0 120.3 jit_solution(15606519831421616831)
XLA Ops:
  0.6 0.9 copy-done
  1.6 0.9 copy-done.2
  2.5 0.8 square_sums.1
  3.4 24.1 %all-to-all-start = ((f32[16,8,128]{2,1,0:T(8,128)}), f32[16,8,128]{2,1,0:T(8,128)S(1)}, u32[]{:S(2)}, u32[]{:S(2)}) async-start(f32[16,8,128]{2,1,0:T(8,128)} %square_sums.1), calls=%async_computation | async-start | bytes 131072 | tf_op jit(solution)/shard_map/all_to_all | solution.py:186
  27.5 0.0 copy-start.7
  27.5 0.7 copy-done.7
  28.2 0.1 copy.9.kept_ref
  28.3 16.4 %all-to-all-done.sums_ref = f32[16,8,128]{2,1,0:T(8,128)S(1)} async-done(((f32[16,8,128]{2,1,0:T(8,128)}), f32[16,8,128]{2,1,0:T(8,128)S(1)}, u32[]{:S(2)}, u32[]{:S(2)}) %all-to-all-start) | async-done | bytes 65568 | tf_op jit(solution)/shard_map/all_to_all | solution.py:186
  44.7 0.9 copy-done.4
  45.7 1.3 %normalize.1 = (bf16[512,256]{1,0:T(8,128)(2,1)S(1)}, bf16[512,256]{1,0:T(8,128)(2,1)S(1)}, bf16[128,512]{1,0:T(8,128)(2,1)S(1)}, bf16[128,512]{1,0:T(8,128)(2,1...) custom-call(s32[1]{0:T(128)} %bitcast.frame_ref, ...), custom_call_target="tpu_custom_call" | custom-call | tf_op jit(solution)/shard_map/normalize/pallas_call | solution.py:187
  47.0 1.9 %collective-permute-start = (bf16[128,512]{1,0:T(8,128)(2,1)S(1)}, bf16[128,512]{1,0:T(8,128)(2,1)S(1)}, u32[]{:S(2)}, u32[]{:S(2)}) collective-permute-start(bf16[128,512]{1,0:T(8,128)(2,1)S(1)} %get-tuple-element.26), channel_id=1, source_target_pairs={{0,16},{16,0},{32,48},{48,32},{64,80},{80,64},{96,112},{112,96},{1... | collective-permute-start | bytes 393224 | tf_op jit(solution)/shard_map/ppermute | solution.py:165
  48.9 8.6 %collective-permute-start.1 = (bf16[128,512]{1,0:T(8,128)(2,1)S(1)}, bf16[128,512]{1,0:T(8,128)(2,1)S(1)}, u32[]{:S(2)}, u32[]{:S(2)}) collective-permute-start(bf16[128,512]{1,0:T(8,128)(2,1)S(1)} %get-tuple-element.27), channel_id=1, source_target_pairs={{64,128},{128,64},{80,144},{144,80},{96,160},{160,96},{112,176},{1... | collective-permute-start | bytes 393224 | tf_op jit(solution)/shard_map/ppermute | solution.py:165
  57.6 1.9 %collective-permute-start.2 = (bf16[128,512]{1,0:T(8,128)(2,1)S(1)}, bf16[128,512]{1,0:T(8,128)(2,1)S(1)}, u32[]{:S(2)}, u32[]{:S(2)}) collective-permute-start(bf16[128,512]{1,0:T(8,128)(2,1)S(1)} %get-tuple-element.28), channel_id=1, source_target_pairs={{0,64},{64,0},{16,80},{80,16},{32,96},{96,32},{48,112},{112,48},{1... | collective-permute-start | bytes 393224 | tf_op jit(solution)/shard_map/ppermute | solution.py:165
  59.5 4.8 %collective-permute-start.3 = (bf16[128,512]{1,0:T(8,128)(2,1)S(1)}, bf16[128,512]{1,0:T(8,128)(2,1)S(1)}, u32[]{:S(2)}, u32[]{:S(2)}) collective-permute-start(bf16[128,512]{1,0:T(8,128)(2,1)S(1)} %get-tuple-element.29), channel_id=1, source_target_pairs={{32,64},{64,32},{48,80},{80,48},{96,128},{128,96},{112,144},{144,1... | collective-permute-start | bytes 393224 | tf_op jit(solution)/shard_map/ppermute | solution.py:165
  64.3 2.5 %collective-permute-start.4 = (bf16[128,512]{1,0:T(8,128)(2,1)S(1)}, bf16[128,512]{1,0:T(8,128)(2,1)S(1)}, u32[]{:S(2)}, u32[]{:S(2)}) collective-permute-start(bf16[128,512]{1,0:T(8,128)(2,1)S(1)} %get-tuple-element.30), channel_id=1, source_target_pairs={{0,32},{32,0},{16,48},{48,16},{64,96},{96,64},{80,112},{112,80},{1... | collective-permute-start | bytes 393224 | tf_op jit(solution)/shard_map/ppermute | solution.py:165
  66.8 7.5 %collective-permute-start.5 = (bf16[128,512]{1,0:T(8,128)(2,1)S(1)}, bf16[128,512]{1,0:T(8,128)(2,1)S(1)}, u32[]{:S(2)}, u32[]{:S(2)}) collective-permute-start(bf16[128,512]{1,0:T(8,128)(2,1)S(1)} %get-tuple-element.31), channel_id=1, source_target_pairs={{16,32},{32,16},{48,64},{64,48},{80,96},{96,80},{112,128},{128,112... | collective-permute-start | bytes 393224 | tf_op jit(solution)/shard_map/ppermute | solution.py:165
  74.3 0.0 collective-permute-done.1.refs_1_
  74.3 0.0 collective-permute-done.2.refs_2_
  74.3 0.9 collective-permute-done.3.refs_3_
  75.3 0.0 collective-permute-done.4.refs_4_
  75.3 5.3 %collective-permute-done.5.refs_5_ = bf16[128,512]{1,0:T(8,128)(2,1)S(1)} collective-permute-done((bf16[128,512]{1,0:T(8,128)(2,1)S(1)}, bf16[128,512]{1,0:T(8,128)(2,1)S(1)}, u32[]{:S(2)}, u32[]{:S(2)}) %collective-permute-start.5) | collective-permute-done | bytes 131104 | tf_op jit(solution)/shard_map/ppermute | solution.py:165
  80.6 6.9 %attend.1 = (bf16[512,256]{1,0:T(8,128)(2,1)}, bf16[512,256]{1,0:T(8,128)(2,1)}, f32[512,256]{1,0:T(8,128)S(1)}, f32[512,256]{1,0:T(8,128)S(1)}, bf16[128,512]{1...) custom-call(s32[1]{0:T(128)} %bitcast.frame_ref, ...), custom_call_target="tpu_custom_call" | custom-call | tf_op jit(solution)/shard_map/attend/pallas_call | solution.py:197
  87.5 1.9 %collective-permute-start.6 = (bf16[128,512]{1,0:T(8,128)(2,1)S(1)}, bf16[128,512]{1,0:T(8,128)(2,1)S(1)}, u32[]{:S(2)}, u32[]{:S(2)}) collective-permute-start(bf16[128,512]{1,0:T(8,128)(2,1)S(1)} %get-tuple-element.36), channel_id=1, source_target_pairs={{0,16},{16,0},{32,48},{48,32},{64,80},{80,64},{96,112},{112,96},{1... | collective-permute-start | bytes 393224 | tf_op jit(solution)/shard_map/ppermute | solution.py:165
  89.4 4.7 %collective-permute-start.7 = (bf16[128,512]{1,0:T(8,128)(2,1)S(1)}, bf16[128,512]{1,0:T(8,128)(2,1)S(1)}, u32[]{:S(2)}, u32[]{:S(2)}) collective-permute-start(bf16[128,512]{1,0:T(8,128)(2,1)S(1)} %get-tuple-element.37), channel_id=1, source_target_pairs={{64,128},{128,64},{80,144},{144,80},{96,160},{160,96},{112,176},{1... | collective-permute-start | bytes 393224 | tf_op jit(solution)/shard_map/ppermute | solution.py:165
  94.1 1.9 %collective-permute-start.8 = (bf16[128,512]{1,0:T(8,128)(2,1)S(1)}, bf16[128,512]{1,0:T(8,128)(2,1)S(1)}, u32[]{:S(2)}, u32[]{:S(2)}) collective-permute-start(bf16[128,512]{1,0:T(8,128)(2,1)S(1)} %get-tuple-element.38), channel_id=1, source_target_pairs={{0,64},{64,0},{16,80},{80,16},{32,96},{96,32},{48,112},{112,48},{1... | collective-permute-start | bytes 393224 | tf_op jit(solution)/shard_map/ppermute | solution.py:165
  96.0 6.1 %collective-permute-start.9 = (bf16[128,512]{1,0:T(8,128)(2,1)S(1)}, bf16[128,512]{1,0:T(8,128)(2,1)S(1)}, u32[]{:S(2)}, u32[]{:S(2)}) collective-permute-start(bf16[128,512]{1,0:T(8,128)(2,1)S(1)} %get-tuple-element.39), channel_id=1, source_target_pairs={{32,64},{64,32},{48,80},{80,48},{96,128},{128,96},{112,144},{144,1... | collective-permute-start | bytes 393224 | tf_op jit(solution)/shard_map/ppermute | solution.py:165
  102.2 1.9 %collective-permute-start.10 = (bf16[128,512]{1,0:T(8,128)(2,1)S(1)}, bf16[128,512]{1,0:T(8,128)(2,1)S(1)}, u32[]{:S(2)}, u32[]{:S(2)}) collective-permute-start(bf16[128,512]{1,0:T(8,128)(2,1)S(1)} %get-tuple-element.40), channel_id=1, source_target_pairs={{0,32},{32,0},{16,48},{48,16},{64,96},{96,64},{80,112},{112,80},{1... | collective-permute-start | bytes 393224 | tf_op jit(solution)/shard_map/ppermute | solution.py:165
  104.1 6.8 %collective-permute-start.11 = (bf16[128,512]{1,0:T(8,128)(2,1)S(1)}, bf16[128,512]{1,0:T(8,128)(2,1)S(1)}, u32[]{:S(2)}, u32[]{:S(2)}) collective-permute-start(bf16[128,512]{1,0:T(8,128)(2,1)S(1)} %get-tuple-element.41), channel_id=1, source_target_pairs={{16,32},{32,16},{48,64},{64,48},{80,96},{96,80},{112,128},{128,112... | collective-permute-start | bytes 393224 | tf_op jit(solution)/shard_map/ppermute | solution.py:165
  110.9 0.0 collective-permute-done.7.refs_1_
  110.9 1.0 collective-permute-done.9.refs_3_
  111.9 6.2 %collective-permute-done.11.refs_5_ = bf16[128,512]{1,0:T(8,128)(2,1)S(1)} collective-permute-done((bf16[128,512]{1,0:T(8,128)(2,1)S(1)}, bf16[128,512]{1,0:T(8,128)(2,1)S(1)}, u32[]{:S(2)}, u32[]{:S(2)}) %collective-permute-start.11) | collective-permute-done | bytes 131104 | tf_op jit(solution)/shard_map/ppermute | solution.py:165
  118.2 2.2 %collect.1 = (bf16[512,256]{1,0:T(8,128)(2,1)}, bf16[512,256]{1,0:T(8,128)(2,1)}) custom-call(s32[1]{0:T(128)} %bitcast.frame_ref, s32[64,6]{1,0:T(8,128)S(1)} %copy.9.kept_ref, f32[512,256]{1,0:T(8,128)S(1)} %get-tuple-element.34.gk_ref, f32[512,256]{1,0:T(8,128)S(1)} %get-tuple-element.35.gv_ref, bf16[128,512]{1,0:T(8,128)(2,1)S(1)} %collective-permute-done.6.refs_0_, ...), custom_call_target="tpu_custom_call" | custom-call | tf_op jit(solution)/shard_map/collect/pallas_call | solution.py:212
  (15 shorter events, 0.0 us)
Async XLA Ops:
  0.6 1.0 copy-start
  1.6 0.9 copy-start.2
  2.5 42.2 %copy-start.1 = (bf16[512,256]{1,0:T(8,128)(2,1)S(1)}, bf16[512,256]{1,0:T(8,128)(2,1)}, u32[]{:S(2)}) copy-start(bf16[512,256]{1,0:T(8,128)(2,1)} %q_ref.3) | copy-start | bytes 786436
  2.5 42.2 %copy-start.3 = (bf16[512,256]{1,0:T(8,128)(2,1)S(1)}, bf16[512,256]{1,0:T(8,128)(2,1)}, u32[]{:S(2)}) copy-start(bf16[512,256]{1,0:T(8,128)(2,1)} %k_ref.3) | copy-start | bytes 786436
  3.4 41.3 %all-to-all-start = ((f32[16,8,128]{2,1,0:T(8,128)}), f32[16,8,128]{2,1,0:T(8,128)S(1)}, u32[]{:S(2)}, u32[]{:S(2)}) async-start(f32[16,8,128]{2,1,0:T(8,128)} %square_sums.1), calls=%async_computation | async-start | bytes 131072 | tf_op jit(solution)/shard_map/all_to_all | solution.py:186
  27.5 0.7 copy-start.7
  44.7 1.0 copy-start.4
  45.7 34.9 %copy-start.5 = (bf16[512,256]{1,0:T(8,128)(2,1)S(1)}, bf16[512,256]{1,0:T(8,128)(2,1)}, u32[]{:S(2)}) copy-start(bf16[512,256]{1,0:T(8,128)(2,1)} %v_ref.3) | copy-start | bytes 786436
  45.7 34.9 %copy-start.6 = (bf16[512,256]{1,0:T(8,128)(2,1)S(1)}, bf16[512,256]{1,0:T(8,128)(2,1)}, u32[]{:S(2)}) copy-start(bf16[512,256]{1,0:T(8,128)(2,1)} %d_ref.1) | copy-start | bytes 786436
  47.0 19.8 %collective-permute-start = (bf16[128,512]{1,0:T(8,128)(2,1)S(1)}, bf16[128,512]{1,0:T(8,128)(2,1)S(1)}, u32[]{:S(2)}, u32[]{:S(2)}) collective-permute-start(bf16[128,512]{1,0:T(8,128)(2,1)S(1)} %get-tuple-element.26), channel_id=1, source_target_pairs={{0,16},{16,0},{32,48},{48,32},{64,80},{80,64},{96,112},{112,96},{1... | collective-permute-start | bytes 393224 | tf_op jit(solution)/shard_map/ppermute | solution.py:165
  48.9 25.4 %collective-permute-start.1 = (bf16[128,512]{1,0:T(8,128)(2,1)S(1)}, bf16[128,512]{1,0:T(8,128)(2,1)S(1)}, u32[]{:S(2)}, u32[]{:S(2)}) collective-permute-start(bf16[128,512]{1,0:T(8,128)(2,1)S(1)} %get-tuple-element.27), channel_id=1, source_target_pairs={{64,128},{128,64},{80,144},{144,80},{96,160},{160,96},{112,176},{1... | collective-permute-start | bytes 393224 | tf_op jit(solution)/shard_map/ppermute | solution.py:165
  57.6 16.8 %collective-permute-start.2 = (bf16[128,512]{1,0:T(8,128)(2,1)S(1)}, bf16[128,512]{1,0:T(8,128)(2,1)S(1)}, u32[]{:S(2)}, u32[]{:S(2)}) collective-permute-start(bf16[128,512]{1,0:T(8,128)(2,1)S(1)} %get-tuple-element.28), channel_id=1, source_target_pairs={{0,64},{64,0},{16,80},{80,16},{32,96},{96,32},{48,112},{112,48},{1... | collective-permute-start | bytes 393224 | tf_op jit(solution)/shard_map/ppermute | solution.py:165
  59.5 15.8 %collective-permute-start.3 = (bf16[128,512]{1,0:T(8,128)(2,1)S(1)}, bf16[128,512]{1,0:T(8,128)(2,1)S(1)}, u32[]{:S(2)}, u32[]{:S(2)}) collective-permute-start(bf16[128,512]{1,0:T(8,128)(2,1)S(1)} %get-tuple-element.29), channel_id=1, source_target_pairs={{32,64},{64,32},{48,80},{80,48},{96,128},{128,96},{112,144},{144,1... | collective-permute-start | bytes 393224 | tf_op jit(solution)/shard_map/ppermute | solution.py:165
  64.3 11.0 %collective-permute-start.4 = (bf16[128,512]{1,0:T(8,128)(2,1)S(1)}, bf16[128,512]{1,0:T(8,128)(2,1)S(1)}, u32[]{:S(2)}, u32[]{:S(2)}) collective-permute-start(bf16[128,512]{1,0:T(8,128)(2,1)S(1)} %get-tuple-element.30), channel_id=1, source_target_pairs={{0,32},{32,0},{16,48},{48,16},{64,96},{96,64},{80,112},{112,80},{1... | collective-permute-start | bytes 393224 | tf_op jit(solution)/shard_map/ppermute | solution.py:165
  66.8 13.8 %collective-permute-start.5 = (bf16[128,512]{1,0:T(8,128)(2,1)S(1)}, bf16[128,512]{1,0:T(8,128)(2,1)S(1)}, u32[]{:S(2)}, u32[]{:S(2)}) collective-permute-start(bf16[128,512]{1,0:T(8,128)(2,1)S(1)} %get-tuple-element.31), channel_id=1, source_target_pairs={{16,32},{32,16},{48,64},{64,48},{80,96},{96,80},{112,128},{128,112... | collective-permute-start | bytes 393224 | tf_op jit(solution)/shard_map/ppermute | solution.py:165
  87.5 16.6 %collective-permute-start.6 = (bf16[128,512]{1,0:T(8,128)(2,1)S(1)}, bf16[128,512]{1,0:T(8,128)(2,1)S(1)}, u32[]{:S(2)}, u32[]{:S(2)}) collective-permute-start(bf16[128,512]{1,0:T(8,128)(2,1)S(1)} %get-tuple-element.36), channel_id=1, source_target_pairs={{0,16},{16,0},{32,48},{48,32},{64,80},{80,64},{96,112},{112,96},{1... | collective-permute-start | bytes 393224 | tf_op jit(solution)/shard_map/ppermute | solution.py:165
  89.4 21.5 %collective-permute-start.7 = (bf16[128,512]{1,0:T(8,128)(2,1)S(1)}, bf16[128,512]{1,0:T(8,128)(2,1)S(1)}, u32[]{:S(2)}, u32[]{:S(2)}) collective-permute-start(bf16[128,512]{1,0:T(8,128)(2,1)S(1)} %get-tuple-element.37), channel_id=1, source_target_pairs={{64,128},{128,64},{80,144},{144,80},{96,160},{160,96},{112,176},{1... | collective-permute-start | bytes 393224 | tf_op jit(solution)/shard_map/ppermute | solution.py:165
  94.1 16.8 %collective-permute-start.8 = (bf16[128,512]{1,0:T(8,128)(2,1)S(1)}, bf16[128,512]{1,0:T(8,128)(2,1)S(1)}, u32[]{:S(2)}, u32[]{:S(2)}) collective-permute-start(bf16[128,512]{1,0:T(8,128)(2,1)S(1)} %get-tuple-element.38), channel_id=1, source_target_pairs={{0,64},{64,0},{16,80},{80,16},{32,96},{96,32},{48,112},{112,48},{1... | collective-permute-start | bytes 393224 | tf_op jit(solution)/shard_map/ppermute | solution.py:165
  96.0 15.9 %collective-permute-start.9 = (bf16[128,512]{1,0:T(8,128)(2,1)S(1)}, bf16[128,512]{1,0:T(8,128)(2,1)S(1)}, u32[]{:S(2)}, u32[]{:S(2)}) collective-permute-start(bf16[128,512]{1,0:T(8,128)(2,1)S(1)} %get-tuple-element.39), channel_id=1, source_target_pairs={{32,64},{64,32},{48,80},{80,48},{96,128},{128,96},{112,144},{144,1... | collective-permute-start | bytes 393224 | tf_op jit(solution)/shard_map/ppermute | solution.py:165
  102.2 9.8 %collective-permute-start.10 = (bf16[128,512]{1,0:T(8,128)(2,1)S(1)}, bf16[128,512]{1,0:T(8,128)(2,1)S(1)}, u32[]{:S(2)}, u32[]{:S(2)}) collective-permute-start(bf16[128,512]{1,0:T(8,128)(2,1)S(1)} %get-tuple-element.40), channel_id=1, source_target_pairs={{0,32},{32,0},{16,48},{48,16},{64,96},{96,64},{80,112},{112,80},{1... | collective-permute-start | bytes 393224 | tf_op jit(solution)/shard_map/ppermute | solution.py:165
  104.1 14.0 %collective-permute-start.11 = (bf16[128,512]{1,0:T(8,128)(2,1)S(1)}, bf16[128,512]{1,0:T(8,128)(2,1)S(1)}, u32[]{:S(2)}, u32[]{:S(2)}) collective-permute-start(bf16[128,512]{1,0:T(8,128)(2,1)S(1)} %get-tuple-element.41), channel_id=1, source_target_pairs={{16,32},{32,16},{48,64},{64,48},{80,96},{96,80},{112,128},{128,112... | collective-permute-start | bytes 393224 | tf_op jit(solution)/shard_map/ppermute | solution.py:165

commit v2 on v1

v2 whole, which is shorter than its diff:
```python
import functools
import math

import jax
import jax.numpy as jnp
from jax import lax
from jax.experimental import pallas as pl
from jax.experimental.pallas import tpu as pltpu
from jax.sharding import PartitionSpec as P

HD = 128
BS = 128
EXCHANGES = ((1, False), (4, True), (4, False), (2, True), (2, False), (1, True))
RETURN_ORDER = (1, 3, 5, 2, 4, 0)

masked_score = -1e30
norm_eps = 1e-06

VMEM = pl.BlockSpec(memory_space=pltpu.VMEM)
SMEM = pl.BlockSpec(memory_space=pltpu.SMEM)


def params(mib):
    return pltpu.CompilerParams(vmem_limit_bytes=mib << 20)


def route(distance, shifted, frames):
    pairs = []
    for low in range(frames - distance):
        if ((low // distance) % 2 == 1) == shifted:
            pairs += [(low, low + distance), (low + distance, low)]
    return pairs


def partner(frame, distance, shifted):
    up = ((frame // distance) % 2 == 1) == shifted
    level = int(math.log2(distance))
    offset = jnp.where(up, distance, -distance)
    slot = jnp.where(up, 2 * level + 1, 2 * level)
    return offset, slot


def block_start(kept_ref, frame, frames, distance, shifted):
    offset, slot = partner(frame, distance, shifted)
    other = jnp.clip(frame + offset, 0, frames - 1)
    return pl.multiple_of(kept_ref[other, slot] * BS, BS)


def is_live(frame, frames, distance, shifted):
    offset, _ = partner(frame, distance, shifted)
    other = frame + offset
    return jnp.logical_and(other >= 0, other < frames)


def via_near(frame):
    return ((frame % 2) ^ ((frame // 2) % 2)) == 1


def prepare_kernel(frames, frame_ref, kept_ref, q_ref, k_ref, v_ref, sums_ref, *block_refs):
    frame = frame_ref[0]
    width = k_ref.shape[1]
    rows = []
    for ref in (q_ref, k_ref):
        for start in range(0, ref.shape[0], 128):
            total = jnp.zeros((128, 128), jnp.float32)
            for column in range(0, width, 128):
                part = ref[start : start + 128, column : column + 128].astype(jnp.float32)
                total += part * part
            rows.append(jnp.sum(total.T, axis=0, keepdims=True))
    packed = jnp.concatenate(rows, axis=0)
    for copy in range(sums_ref.shape[0]):
        sums_ref[copy] = packed
    first = block_refs[0]
    targets = [first.at[:BS], *block_refs[1:], first.at[BS:]]
    for (distance, shifted), block in zip(EXCHANGES, targets):
        rows = pl.ds(block_start(kept_ref, frame, frames, distance, shifted), BS)
        block[:, :width] = k_ref[rows, :]
        block[:, width:] = v_ref[rows, :]


def by_row(scale):
    return jnp.broadcast_to(scale, (128, 128)).T


def scaled(block, scale):
    return (block.astype(jnp.float32) * scale).astype(jnp.bfloat16)


def norm_kernel(frames, width_all, frame_ref, kept_ref, sums_ref, q_ref, k_ref, qn_ref, kn_ref, scale_ref, scale_rows):
    frame = frame_ref[0]
    width = q_ref.shape[1]
    total = sums_ref[0]
    for part in range(1, sums_ref.shape[0]):
        total += sums_ref[part]
    scale = lax.rsqrt(total / width_all + norm_eps)
    scale_rows[...] = scale
    scale_ref[...] = jnp.zeros_like(scale_ref)
    for distance, shifted in EXCHANGES:
        offset, _ = partner(frame, distance, shifted)
        block = block_start(kept_ref, frame, frames, distance, shifted) // BS
        row = q_ref.shape[0] // BS + block

        @pl.when(is_live(frame, frames, distance, shifted))
        def _():
            scale_ref[frame + offset] = scale_rows[pl.ds(row, 1), :]

    row = 0
    for ref, out in ((q_ref, qn_ref), (k_ref, kn_ref)):
        for start in range(0, ref.shape[0], 128):
            factor = by_row(scale[row : row + 1, :])
            row += 1
            for column in range(0, width, 128):
                part = ref[start : start + 128, column : column + 128]
                out[start : start + 128, column : column + 128] = scaled(part, factor)


CONTRACT_LAST = (((1,), (1,)), ((), ()))
CONTRACT_FIRST = (((0,), (0,)), ((), ()))
FACTOR = 1.0 / math.sqrt(HD)
CHUNK = 256


def dot(left, right, dims=(((1,), (0,)), ((), ()))):
    return lax.dot_general(left, right, dims, preferred_element_type=jnp.float32)


def attend_kernel(frames, frame_ref, scale_ref, q_ref, k_ref, v_ref, d_ref, *refs):
    far_refs = refs[:5]
    att_ref, p_own, s_own, s_far, k_far = refs[5:10]
    back_refs = refs[10:16]
    v_far, p_far = refs[16:]
    frame = frame_ref[0]
    tokens, width = q_ref.shape
    f32 = jnp.float32

    def place(slot, far):
        distance, shifted = EXCHANGES[slot]
        offset, _ = partner(frame, distance, shifted)
        scale = by_row(scale_ref[jnp.clip(frame + offset, 0, frames - 1)])
        start = slot * BS
        for column in range(0, width, 128):
            part = far[:BS, column : column + 128]
            k_far[start : start + BS, column : column + 128] = scaled(part, scale)
        v_far[start : start + BS] = far[:BS, width:]

    for slot, far in enumerate(far_refs):
        place(slot, far)

    @pl.when(via_near(frame))
    def _():
        place(5, far_refs[4].at[BS:])

    @pl.when(jnp.logical_not(via_near(frame)))
    def _():
        place(5, far_refs[3].at[BS:])

    column = lax.broadcasted_iota(jnp.int32, (1, 6 * BS), 1)
    allowed = column < 0
    for slot, (distance, shifted) in enumerate(EXCHANGES):
        inside = jnp.logical_and(column >= slot * BS, column < (slot + 1) * BS)
        live = is_live(frame, frames, distance, shifted)
        allowed = jnp.logical_or(allowed, jnp.logical_and(inside, live))
    for index in range(width // HD):
        head = slice(index * HD, (index + 1) * HD)
        keys, vals = k_far[:, head], v_far[:, head]
        for first in range(0, tokens, CHUNK):
            rows = slice(first, first + CHUNK)
            grads = d_ref[rows, head]
            own = dot(q_ref[rows, head], k_ref[:, head], CONTRACT_LAST) * FACTOR
            far = jnp.where(allowed, dot(q_ref[rows, head], keys, CONTRACT_LAST) * FACTOR, masked_score)
            top = jnp.maximum(jnp.max(own, axis=1, keepdims=True), jnp.max(far, axis=1, keepdims=True))
            own = jnp.exp(own - top)
            far = jnp.exp(far - top)
            share = 1.0 / (jnp.sum(own, axis=1, keepdims=True) + jnp.sum(far, axis=1, keepdims=True))
            own = own * share
            far = far * share
            own_low = own.astype(jnp.bfloat16)
            far_low = far.astype(jnp.bfloat16)
            p_own[index, rows, :] = own_low
            p_far[rows, :] = far_low
            attended = (dot(own_low, v_ref[:, head]) + dot(far_low, vals)).astype(jnp.bfloat16)
            att_ref[rows, head] = attended
            inner = jnp.sum(grads.astype(f32) * attended.astype(f32), axis=1, keepdims=True)
            s_own[index, rows, :] = (own * (dot(grads, v_ref[:, head], CONTRACT_LAST) - inner)).astype(jnp.bfloat16)
            s_far[index, rows, :] = (far * (dot(grads, vals, CONTRACT_LAST) - inner)).astype(jnp.bfloat16)
        grad_k = dot(s_far[index], q_ref[:, head], CONTRACT_FIRST) * FACTOR
        grad_v = dot(p_far[...], d_ref[:, head], CONTRACT_FIRST)
        for slot, back in zip(RETURN_ORDER, back_refs):
            rows = slice(slot * BS, (slot + 1) * BS)
            back[:, index * HD : (index + 1) * HD] = grad_k[rows].astype(jnp.bfloat16)
            back[:, width + index * HD : width + (index + 1) * HD] = grad_v[rows].astype(jnp.bfloat16)


def rest_kernel(p_own, s_own, s_far, k_far, q_ref, k_ref, d_ref, gq_ref, gk_ref, gv_ref):
    for index in range(q_ref.shape[1] // HD):
        head = slice(index * HD, (index + 1) * HD)
        grad_q = dot(s_own[index], k_ref[:, head]) + dot(s_far[index], k_far[:, head])
        gq_ref[:, head] = (grad_q * FACTOR).astype(jnp.bfloat16)
        gk_ref[:, head] = dot(s_own[index], q_ref[:, head], CONTRACT_FIRST) * FACTOR
        gv_ref[:, head] = dot(p_own[index], d_ref[:, head], CONTRACT_FIRST)


def collect_kernel(frames, frame_ref, kept_ref, gk_ref, gv_ref, *refs):
    back_refs, (outk_ref, outv_ref, acc_k, acc_v) = refs[:6], refs[6:]
    frame = frame_ref[0]
    width = gk_ref.shape[1]
    acc_k[...] = gk_ref[...]
    acc_v[...] = gv_ref[...]
    for which, back in zip(RETURN_ORDER, back_refs):
        distance, shifted = EXCHANGES[which]
        rows = pl.ds(block_start(kept_ref, frame, frames, distance, shifted), BS)

        @pl.when(is_live(frame, frames, distance, shifted))
        def _():
            acc_k[rows, :] += back[:, :width].astype(jnp.float32)
            acc_v[rows, :] += back[:, width:].astype(jnp.float32)

    outk_ref[...] = acc_k[...].astype(jnp.bfloat16)
    outv_ref[...] = acc_v[...].astype(jnp.bfloat16)


def exchange(block, frames, which):
    return lax.ppermute(block, "frame", route(*EXCHANGES[which], frames))


def swap_relayed(blocks, frames):
    first, wide_far, near_far, wide_two, near_two = blocks
    got_first = exchange(first, frames, 0)
    got_wide_far = exchange(wide_far, frames, 1)
    got_near_far = exchange(near_far, frames, 2)
    relay = got_first[BS:]
    got_wide_two = exchange(jnp.concatenate([wide_two, relay]), frames, 3)
    got_near_two = exchange(jnp.concatenate([near_two, relay]), frames, 4)
    return got_first, got_wide_far, got_near_far, got_wide_two, got_near_two


def swap(blocks, frames):
    return [exchange(block, frames, which) for which, block in zip(RETURN_ORDER, blocks)]


def on_device(queries, keys, values, cotangent, kept):
    frames = lax.axis_size("frame")
    heads = lax.axis_size("head")
    tokens, width = queries.shape
    frame = lax.axis_index("frame").reshape(1)
    stat_rows = 2 * tokens // 128
    flat = jax.ShapeDtypeStruct((tokens, width), jnp.bfloat16)
    wide = jax.ShapeDtypeStruct((tokens, width), jnp.float32)
    block = jax.ShapeDtypeStruct((BS, 2 * width), jnp.bfloat16)
    pair = jax.ShapeDtypeStruct((2 * BS, 2 * width), jnp.bfloat16)
    sums, *sent = pl.pallas_call(
        functools.partial(prepare_kernel, frames),
        out_shape=[jax.ShapeDtypeStruct((heads, stat_rows, 128), jnp.float32), pair] + [block] * 4,
        in_specs=[SMEM] * 2 + [VMEM] * 3,
        out_specs=[VMEM] * 6,
        compiler_params=params(8),
        name="prepare",
    )(frame, kept, queries, keys, values)
    sums = lax.all_to_all(sums, "head", 0, 0)
    far = swap_relayed(sent, frames)
    q_norm, k_norm, scales = pl.pallas_call(
        functools.partial(norm_kernel, frames, width * heads),
        out_shape=[flat, flat, jax.ShapeDtypeStruct((frames, 1, BS), jnp.float32)],
        in_specs=[SMEM] * 2 + [VMEM] * 3,
        out_specs=[VMEM] * 3,
        scratch_shapes=[pltpu.VMEM((stat_rows, 128), jnp.float32)],
        compiler_params=params(8),
        name="normalize",
    )(frame, kept, sums, queries, keys)
    scales = lax.all_to_all(scales, "frame", 0, 0)
    heads_dev = width // HD
    own_shape = (heads_dev, tokens, tokens)
    own_flops = 2 * tokens * tokens * width
    attended, own_p, own_s, far_s, far_k, *back = pl.pallas_call(
        functools.partial(attend_kernel, frames),
        out_shape=[
            flat,
            jax.ShapeDtypeStruct(own_shape, jnp.bfloat16),
            jax.ShapeDtypeStruct(own_shape, jnp.bfloat16),
            jax.ShapeDtypeStruct((heads_dev, tokens, 6 * BS), jnp.bfloat16),
            jax.ShapeDtypeStruct((6 * BS, width), jnp.bfloat16),
        ]
        + [block] * 6,
        in_specs=[SMEM] + [VMEM] * 10,
        out_specs=[VMEM] * 11,
        scratch_shapes=[
            pltpu.VMEM((6 * BS, width), jnp.bfloat16),
            pltpu.VMEM((tokens, 6 * BS), jnp.bfloat16),
        ],
        compiler_params=params(20),
        name="attend",
    )(frame, scales, q_norm, k_norm, values, cotangent, *far)
    grad_q, own_k, own_v = pl.pallas_call(
        rest_kernel,
        out_shape=[flat, wide, wide],
        in_specs=[VMEM] * 7,
        out_specs=[VMEM] * 3,
        compiler_params=params(8),
        cost_estimate=pl.CostEstimate(flops=4 * own_flops, bytes_accessed=8 << 20, transcendentals=0),
        name="rest",
    )(own_p, own_s, far_s, far_k, q_norm, k_norm, cotangent)
    back = swap(back, frames)
    grad_k, grad_v = pl.pallas_call(
        functools.partial(collect_kernel, frames),
        out_shape=[flat, flat],
        in_specs=[SMEM] * 2 + [VMEM] * 8,
        out_specs=[VMEM] * 2,
        scratch_shapes=[pltpu.VMEM((tokens, width), jnp.float32)] * 2,
        compiler_params=params(8),
        name="collect",
    )(frame, kept, own_k, own_v, *back)
    return attended, grad_q, grad_k, grad_v


def solution(mesh):
    spec = P("frame", "head")
    return jax.shard_map(
        on_device,
        mesh=mesh,
        in_specs=(spec, spec, spec, spec, P()),
        out_specs=(spec, spec, spec, spec),
        check_vma=False,
    )
```

time: 121 us -> 111 us (0.917)
  the two profiles are of different devices: /device:TPU:6 before, /device:TPU:10 now
where the time goes in v2:
time: 111 us
  starting transfers between devices  75.9 us (68%)
  waiting for transfers between devices  16.3 us (15%)
  Pallas kernels  14 us (13%)
  local copies, waits for them, and re-layouts  3.69 us (3%)
    ppermute x11, starting transfers between devices, exchange(): return lax.ppermute(block, 'frame', route(*EXCHANGES[which], frames))  38.3 us
    all_to_all x1, starting transfers between devices, on_device(): sums = lax.all_to_all(sums, 'head', 0, 0)  24.5 us
    all_to_all x1, starting transfers between devices, on_device(): scales = lax.all_to_all(scales, 'frame', 0, 0)  13.2 us
    all_to_all x1, waiting for transfers between devices, on_device(): scales = lax.all_to_all(scales, 'frame', 0, 0)  8.28 us
    ppermute x11, waiting for transfers between devices, exchange(): return lax.ppermute(block, 'frame', route(*EXCHANGES[which], frames))  7.15 us
    pallas_call x1, Pallas kernels, on_device(): pl.pallas_call(functools.partial(attend_kernel, frames), out_shape=[flat,...  6.01 us
    unnamed x15, local copies, waits for them, and re-layouts  3.68 us
  transfers between devices with their start and end apart: 13, of which 5 were waited for; matrix products, arithmetic and copies ran while one was open for 0% of the time, Pallas kernels for 4%

profile of v2, /device:TPU:10, one launch (start us, length us, event | category | flops | bytes accessed | tf_op | source)
XLA Modules:
  0.0 110.7 jit_solution(9956190784711049111)
XLA Ops:
  0.6 0.8 copy.10.kept_ref
  1.5 0.9 copy-done.1
  2.4 0.9 copy-done.3
  3.4 0.9 copy-done.5
  4.3 1.9 %prepare.1 = (f32[16,8,128]{2,1,0:T(8,128)}, bf16[256,512]{1,0:T(8,128)(2,1)S(1)}, bf16[128,512]{1,0:T(8,128)(2,1)S(1)}, bf16[128,512]{1,0:T(8,128)(2,1)S(1)}, b...) custom-call(s32[1]{0:T(128)} %bitcast.frame_ref, s32[64,6]{1,0:T(8,128)S(1)} %copy.10.kept_ref, ...), custom_call_target="tpu_custom_call" | custom-call | tf_op jit(solution)/shard_map/prepare/pallas_call | solution.py:251
  6.2 1.9 %collective-permute-start = (bf16[256,512]{1,0:T(8,128)(2,1)S(1)}, bf16[256,512]{1,0:T(8,128)(2,1)S(1)}, u32[]{:S(2)}, u32[]{:S(2)}) collective-permute-start(bf16[256,512]{1,0:T(8,128)(2,1)S(1)} %get-tuple-element.33), channel_id=1, source_target_pairs={{0,16},{16,0},{32,48},{48,32},{64,80},{80,64},{96,112},{112,96},{1... | collective-permute-start | bytes 786440 | tf_op jit(solution)/shard_map/ppermute | solution.py:223
  8.2 24.5 %all-to-all-start = ((f32[16,8,128]{2,1,0:T(8,128)}), f32[16,8,128]{2,1,0:T(8,128)S(1)}, u32[]{:S(2)}, u32[]{:S(2)}) async-start(f32[16,8,128]{2,1,0:T(8,128)} %get-tuple-element.29), calls=%async_computation | async-start | bytes 131072 | tf_op jit(solution)/shard_map/all_to_all | solution.py:259
  32.6 0.0 collective-permute-done.refs_0_
  32.7 3.4 %collective-permute-start.4 = (bf16[256,512]{1,0:T(8,128)(2,1)S(1)}, bf16[256,512]{1,0:T(8,128)(2,1)S(1)}, u32[]{:S(2)}, u32[]{:S(2)}) collective-permute-start(bf16[256,512]{1,0:T(8,128)(2,1)S(1)} %get-tuple-element.54), channel_id=1, source_target_pairs={{0,32},{32,0},{16,48},{48,16},{64,96},{96,64},{80,112},{112,80},{1... | collective-permute-start | bytes 786440 | tf_op jit(solution)/shard_map/ppermute | solution.py:223
  36.1 7.9 %collective-permute-start.3 = (bf16[256,512]{1,0:T(8,128)(2,1)S(1)}, bf16[256,512]{1,0:T(8,128)(2,1)S(1)}, u32[]{:S(2)}, u32[]{:S(2)}) collective-permute-start(bf16[256,512]{1,0:T(8,128)(2,1)S(1)} %get-tuple-element.55), channel_id=1, source_target_pairs={{32,64},{64,32},{48,80},{80,48},{96,128},{128,96},{112,144},{144,1... | collective-permute-start | bytes 786440 | tf_op jit(solution)/shard_map/ppermute | solution.py:223
  44.0 1.9 %collective-permute-start.1 = (bf16[128,512]{1,0:T(8,128)(2,1)S(1)}, bf16[128,512]{1,0:T(8,128)(2,1)S(1)}, u32[]{:S(2)}, u32[]{:S(2)}) collective-permute-start(bf16[128,512]{1,0:T(8,128)(2,1)S(1)} %get-tuple-element.34), channel_id=1, source_target_pairs={{64,128},{128,64},{80,144},{144,80},{96,160},{160,96},{112,176},{1... | collective-permute-start | bytes 393224 | tf_op jit(solution)/shard_map/ppermute | solution.py:223
  45.9 1.9 %collective-permute-start.2 = (bf16[128,512]{1,0:T(8,128)(2,1)S(1)}, bf16[128,512]{1,0:T(8,128)(2,1)S(1)}, u32[]{:S(2)}, u32[]{:S(2)}) collective-permute-start(bf16[128,512]{1,0:T(8,128)(2,1)S(1)} %get-tuple-element.35), channel_id=1, source_target_pairs={{0,64},{64,0},{16,80},{80,16},{32,96},{96,32},{48,112},{112,48},{1... | collective-permute-start | bytes 393224 | tf_op jit(solution)/shard_map/ppermute | solution.py:223
  47.8 0.9 all-to-all-done.sums_ref
  48.7 1.8 %normalize.1 = (bf16[512,256]{1,0:T(8,128)(2,1)S(1)}, bf16[512,256]{1,0:T(8,128)(2,1)S(1)}, f32[64,1,128]{2,1,0:T(1,128)}) custom-call(s32[1]{0:T(128)} %bitcast.frame_ref, s32[64,6]{1,0:T(8,128)S(1)} %copy.10.kept_ref, f32[16,8,128]{2,1,0:T(8,128)S(1)} %all-to-all-done.sums_ref, bf16[512,256]{1,0:T(8,128)(2,1)S(1)} %copy-done.4, bf16[512,256]{1,0:T(8,128)(2,1)S(1)} %copy-done.6), custom_call_target="tpu_custom_call" | custom-call | tf_op jit(solution)/shard_map/normalize/pallas_call | solution.py:261
  50.5 13.2 %all-to-all-start.1 = ((f32[64,1,128]{2,1,0:T(1,128)}), f32[64,1,128]{2,1,0:T(1,128)S(1)}, u32[]{:S(2)}, u32[]{:S(2)}) async-start(f32[64,1,128]{2,1,0:T(1,128)} %get-tuple-element.30), calls=%async_computation.1 | async-start | bytes 65536 | tf_op jit(solution)/shard_map/all_to_all | solution.py:270
  63.7 3.2 %collective-permute-done.1.refs_1_ = bf16[128,512]{1,0:T(8,128)(2,1)S(1)} collective-permute-done((bf16[128,512]{1,0:T(8,128)(2,1)S(1)}, bf16[128,512]{1,0:T(8,128)(2,1)S(1)}, u32[]{:S(2)}, u32[]{:S(2)}) %collective-permute-start.1) | collective-permute-done | bytes 131104 | tf_op jit(solution)/shard_map/ppermute | solution.py:223
  66.9 0.0 collective-permute-done.2.refs_2_
  66.9 8.3 %all-to-all-done.1.scale_ref = f32[64,1,128]{2,1,0:T(1,128)S(1)} async-done(((f32[64,1,128]{2,1,0:T(1,128)}), f32[64,1,128]{2,1,0:T(1,128)S(1)}, u32[]{:S(2)}, u32[]{:S(2)}) %all-to-all-start.1) | async-done | bytes 32800 | tf_op jit(solution)/shard_map/all_to_all | solution.py:270
  75.2 0.0 collective-permute-done.4.refs_4_
  75.2 6.0 %attend.1 = (bf16[512,256]{1,0:T(8,128)(2,1)}, bf16[2,512,512]{2,1,0:T(8,128)(2,1)S(1)}, bf16[2,512,512]{2,1,0:T(8,128)(2,1)S(1)}, bf16[2,512,768]{2,1,0:T(8,128...) custom-call(s32[1]{0:T(128)} %bitcast.frame_ref, ...), custom_call_target="tpu_custom_call" | custom-call | tf_op jit(solution)/shard_map/attend/pallas_call | solution.py:274
  81.2 3.2 %collective-permute-start.5 = (bf16[128,512]{1,0:T(8,128)(2,1)S(1)}, bf16[128,512]{1,0:T(8,128)(2,1)S(1)}, u32[]{:S(2)}, u32[]{:S(2)}) collective-permute-start(bf16[128,512]{1,0:T(8,128)(2,1)S(1)} %get-tuple-element.46), channel_id=1, source_target_pairs={{64,128},{128,64},{80,144},{144,80},{96,160},{160,96},{112,176},{1... | collective-permute-start | bytes 393224 | tf_op jit(solution)/shard_map/ppermute | solution.py:223
  84.4 8.9 %collective-permute-start.6 = (bf16[128,512]{1,0:T(8,128)(2,1)S(1)}, bf16[128,512]{1,0:T(8,128)(2,1)S(1)}, u32[]{:S(2)}, u32[]{:S(2)}) collective-permute-start(bf16[128,512]{1,0:T(8,128)(2,1)S(1)} %get-tuple-element.47), channel_id=1, source_target_pairs={{32,64},{64,32},{48,80},{80,48},{96,128},{128,96},{112,144},{144,1... | collective-permute-start | bytes 393224 | tf_op jit(solution)/shard_map/ppermute | solution.py:223
  93.4 3.3 %collective-permute-start.7 = (bf16[128,512]{1,0:T(8,128)(2,1)S(1)}, bf16[128,512]{1,0:T(8,128)(2,1)S(1)}, u32[]{:S(2)}, u32[]{:S(2)}) collective-permute-start(bf16[128,512]{1,0:T(8,128)(2,1)S(1)} %get-tuple-element.48), channel_id=1, source_target_pairs={{16,32},{32,16},{48,64},{64,48},{80,96},{96,80},{112,128},{128,112... | collective-permute-start | bytes 393224 | tf_op jit(solution)/shard_map/ppermute | solution.py:223
  96.7 1.9 %collective-permute-start.8 = (bf16[128,512]{1,0:T(8,128)(2,1)S(1)}, bf16[128,512]{1,0:T(8,128)(2,1)S(1)}, u32[]{:S(2)}, u32[]{:S(2)}) collective-permute-start(bf16[128,512]{1,0:T(8,128)(2,1)S(1)} %get-tuple-element.49), channel_id=1, source_target_pairs={{0,64},{64,0},{16,80},{80,16},{32,96},{96,32},{48,112},{112,48},{1... | collective-permute-start | bytes 393224 | tf_op jit(solution)/shard_map/ppermute | solution.py:223
  98.6 1.9 %collective-permute-start.9 = (bf16[128,512]{1,0:T(8,128)(2,1)S(1)}, bf16[128,512]{1,0:T(8,128)(2,1)S(1)}, u32[]{:S(2)}, u32[]{:S(2)}) collective-permute-start(bf16[128,512]{1,0:T(8,128)(2,1)S(1)} %get-tuple-element.50), channel_id=1, source_target_pairs={{0,32},{32,0},{16,48},{48,16},{64,96},{96,64},{80,112},{112,80},{1... | collective-permute-start | bytes 393224 | tf_op jit(solution)/shard_map/ppermute | solution.py:223
  100.6 0.0 collective-permute-done.5.refs_0_
  100.6 1.9 %collective-permute-start.10 = (bf16[128,512]{1,0:T(8,128)(2,1)S(1)}, bf16[128,512]{1,0:T(8,128)(2,1)S(1)}, u32[]{:S(2)}, u32[]{:S(2)}) collective-permute-start(bf16[128,512]{1,0:T(8,128)(2,1)S(1)} %get-tuple-element.51), channel_id=1, source_target_pairs={{0,16},{16,0},{32,48},{48,32},{64,80},{80,64},{96,112},{112,96},{1... | collective-permute-start | bytes 393224 | tf_op jit(solution)/shard_map/ppermute | solution.py:223
  102.5 2.1 %rest.1 = (bf16[512,256]{1,0:T(8,128)(2,1)}, f32[512,256]{1,0:T(8,128)S(1)}, f32[512,256]{1,0:T(8,128)S(1)}) custom-call(bf16[2,512,512]{2,1,0:T(8,128)(2,1)S(1)} %get-tuple-element.39.p_own, bf16[2,512,512]{2,1,0:T(8,128)(2,1)S(1)} %get-tuple-element.40.s_own, bf16[2,512,768]{2,1,0:T(8,128)(2,1)S(1)} %get-tuple-element.41.s_far, ...), custom_call_target="tpu_custom_call" | custom-call | flops 536870912 | bytes 8388608 | tf_op jit(solution)/shard_map/rest/pallas_call | solution.py:293
  104.6 2.8 %collective-permute-done.7.refs_2_ = bf16[128,512]{1,0:T(8,128)(2,1)S(1)} collective-permute-done((bf16[128,512]{1,0:T(8,128)(2,1)S(1)}, bf16[128,512]{1,0:T(8,128)(2,1)S(1)}, u32[]{:S(2)}, u32[]{:S(2)}) %collective-permute-start.7) | collective-permute-done | bytes 131104 | tf_op jit(solution)/shard_map/ppermute | solution.py:223
  107.5 1.1 %collective-permute-done.8.refs_3_ = bf16[128,512]{1,0:T(8,128)(2,1)S(1)} collective-permute-done((bf16[128,512]{1,0:T(8,128)(2,1)S(1)}, bf16[128,512]{1,0:T(8,128)(2,1)S(1)}, u32[]{:S(2)}, u32[]{:S(2)}) %collective-permute-start.8) | collective-permute-done | bytes 131104 | tf_op jit(solution)/shard_map/ppermute | solution.py:223
  108.6 0.0 collective-permute-done.10.refs_5_
  108.6 2.2 %collect.1 = (bf16[512,256]{1,0:T(8,128)(2,1)}, bf16[512,256]{1,0:T(8,128)(2,1)}) custom-call(s32[1]{0:T(128)} %bitcast.frame_ref, s32[64,6]{1,0:T(8,128)S(1)} %copy.10.kept_ref, f32[512,256]{1,0:T(8,128)S(1)} %get-tuple-element.44.gk_ref, f32[512,256]{1,0:T(8,128)S(1)} %get-tuple-element.45.gv_ref, bf16[128,512]{1,0:T(8,128)(2,1)S(1)} %collective-permute-done.5.refs_0_, ...), custom_call_target="tpu_custom_call" | custom-call | tf_op jit(solution)/shard_map/collect/pallas_call | solution.py:303
  (16 shorter events, 0.1 us)
Async XLA Ops:
  0.6 74.6 %copy-start = (bf16[512,256]{1,0:T(8,128)(2,1)S(1)}, bf16[512,256]{1,0:T(8,128)(2,1)}, u32[]{:S(2)}) copy-start(bf16[512,256]{1,0:T(8,128)(2,1)} %d_ref.3) | copy-start | bytes 786436
  1.5 0.9 copy-start.1
  2.4 0.9 copy-start.3
  3.4 0.9 copy-start.5
  4.3 44.4 %copy-start.4 = (bf16[512,256]{1,0:T(8,128)(2,1)S(1)}, bf16[512,256]{1,0:T(8,128)(2,1)}, u32[]{:S(2)}) copy-start(bf16[512,256]{1,0:T(8,128)(2,1)} %q_ref.3) | copy-start | bytes 786436
  4.3 44.4 %copy-start.6 = (bf16[512,256]{1,0:T(8,128)(2,1)S(1)}, bf16[512,256]{1,0:T(8,128)(2,1)}, u32[]{:S(2)}) copy-start(bf16[512,256]{1,0:T(8,128)(2,1)} %k_ref.3) | copy-start | bytes 786436
  4.3 70.9 %copy-start.2 = (bf16[512,256]{1,0:T(8,128)(2,1)S(1)}, bf16[512,256]{1,0:T(8,128)(2,1)}, u32[]{:S(2)}) copy-start(bf16[512,256]{1,0:T(8,128)(2,1)} %v_ref.3) | copy-start | bytes 786436
  6.2 26.4 %collective-permute-start = (bf16[256,512]{1,0:T(8,128)(2,1)S(1)}, bf16[256,512]{1,0:T(8,128)(2,1)S(1)}, u32[]{:S(2)}, u32[]{:S(2)}) collective-permute-start(bf16[256,512]{1,0:T(8,128)(2,1)S(1)} %get-tuple-element.33), channel_id=1, source_target_pairs={{0,16},{16,0},{32,48},{48,32},{64,80},{80,64},{96,112},{112,96},{1... | collective-permute-start | bytes 786440 | tf_op jit(solution)/shard_map/ppermute | solution.py:223
  8.2 40.6 %all-to-all-start = ((f32[16,8,128]{2,1,0:T(8,128)}), f32[16,8,128]{2,1,0:T(8,128)S(1)}, u32[]{:S(2)}, u32[]{:S(2)}) async-start(f32[16,8,128]{2,1,0:T(8,128)} %get-tuple-element.29), calls=%async_computation | async-start | bytes 131072 | tf_op jit(solution)/shard_map/all_to_all | solution.py:259
  32.7 42.5 %collective-permute-start.4 = (bf16[256,512]{1,0:T(8,128)(2,1)S(1)}, bf16[256,512]{1,0:T(8,128)(2,1)S(1)}, u32[]{:S(2)}, u32[]{:S(2)}) collective-permute-start(bf16[256,512]{1,0:T(8,128)(2,1)S(1)} %get-tuple-element.54), channel_id=1, source_target_pairs={{0,32},{32,0},{16,48},{48,16},{64,96},{96,64},{80,112},{112,80},{1... | collective-permute-start | bytes 786440 | tf_op jit(solution)/shard_map/ppermute | solution.py:223
  36.1 39.1 %collective-permute-start.3 = (bf16[256,512]{1,0:T(8,128)(2,1)S(1)}, bf16[256,512]{1,0:T(8,128)(2,1)S(1)}, u32[]{:S(2)}, u32[]{:S(2)}) collective-permute-start(bf16[256,512]{1,0:T(8,128)(2,1)S(1)} %get-tuple-element.55), channel_id=1, source_target_pairs={{32,64},{64,32},{48,80},{80,48},{96,128},{128,96},{112,144},{144,1... | collective-permute-start | bytes 786440 | tf_op jit(solution)/shard_map/ppermute | solution.py:223
  44.0 22.9 %collective-permute-start.1 = (bf16[128,512]{1,0:T(8,128)(2,1)S(1)}, bf16[128,512]{1,0:T(8,128)(2,1)S(1)}, u32[]{:S(2)}, u32[]{:S(2)}) collective-permute-start(bf16[128,512]{1,0:T(8,128)(2,1)S(1)} %get-tuple-element.34), channel_id=1, source_target_pairs={{64,128},{128,64},{80,144},{144,80},{96,160},{160,96},{112,176},{1... | collective-permute-start | bytes 393224 | tf_op jit(solution)/shard_map/ppermute | solution.py:223
  45.9 21.0 %collective-permute-start.2 = (bf16[128,512]{1,0:T(8,128)(2,1)S(1)}, bf16[128,512]{1,0:T(8,128)(2,1)S(1)}, u32[]{:S(2)}, u32[]{:S(2)}) collective-permute-start(bf16[128,512]{1,0:T(8,128)(2,1)S(1)} %get-tuple-element.35), channel_id=1, source_target_pairs={{0,64},{64,0},{16,80},{80,16},{32,96},{96,32},{48,112},{112,48},{1... | collective-permute-start | bytes 393224 | tf_op jit(solution)/shard_map/ppermute | solution.py:223
  50.5 24.6 %all-to-all-start.1 = ((f32[64,1,128]{2,1,0:T(1,128)}), f32[64,1,128]{2,1,0:T(1,128)S(1)}, u32[]{:S(2)}, u32[]{:S(2)}) async-start(f32[64,1,128]{2,1,0:T(1,128)} %get-tuple-element.30), calls=%async_computation.1 | async-start | bytes 65536 | tf_op jit(solution)/shard_map/all_to_all | solution.py:270
  81.2 19.4 %collective-permute-start.5 = (bf16[128,512]{1,0:T(8,128)(2,1)S(1)}, bf16[128,512]{1,0:T(8,128)(2,1)S(1)}, u32[]{:S(2)}, u32[]{:S(2)}) collective-permute-start(bf16[128,512]{1,0:T(8,128)(2,1)S(1)} %get-tuple-element.46), channel_id=1, source_target_pairs={{64,128},{128,64},{80,144},{144,80},{96,160},{160,96},{112,176},{1... | collective-permute-start | bytes 393224 | tf_op jit(solution)/shard_map/ppermute | solution.py:223
  84.4 20.2 %collective-permute-start.6 = (bf16[128,512]{1,0:T(8,128)(2,1)S(1)}, bf16[128,512]{1,0:T(8,128)(2,1)S(1)}, u32[]{:S(2)}, u32[]{:S(2)}) collective-permute-start(bf16[128,512]{1,0:T(8,128)(2,1)S(1)} %get-tuple-element.47), channel_id=1, source_target_pairs={{32,64},{64,32},{48,80},{80,48},{96,128},{128,96},{112,144},{144,1... | collective-permute-start | bytes 393224 | tf_op jit(solution)/shard_map/ppermute | solution.py:223
  93.4 14.1 %collective-permute-start.7 = (bf16[128,512]{1,0:T(8,128)(2,1)S(1)}, bf16[128,512]{1,0:T(8,128)(2,1)S(1)}, u32[]{:S(2)}, u32[]{:S(2)}) collective-permute-start(bf16[128,512]{1,0:T(8,128)(2,1)S(1)} %get-tuple-element.48), channel_id=1, source_target_pairs={{16,32},{32,16},{48,64},{64,48},{80,96},{96,80},{112,128},{128,112... | collective-permute-start | bytes 393224 | tf_op jit(solution)/shard_map/ppermute | solution.py:223
  96.7 11.9 %collective-permute-start.8 = (bf16[128,512]{1,0:T(8,128)(2,1)S(1)}, bf16[128,512]{1,0:T(8,128)(2,1)S(1)}, u32[]{:S(2)}, u32[]{:S(2)}) collective-permute-start(bf16[128,512]{1,0:T(8,128)(2,1)S(1)} %get-tuple-element.49), channel_id=1, source_target_pairs={{0,64},{64,0},{16,80},{80,16},{32,96},{96,32},{48,112},{112,48},{1... | collective-permute-start | bytes 393224 | tf_op jit(solution)/shard_map/ppermute | solution.py:223
  98.6 9.9 %collective-permute-start.9 = (bf16[128,512]{1,0:T(8,128)(2,1)S(1)}, bf16[128,512]{1,0:T(8,128)(2,1)S(1)}, u32[]{:S(2)}, u32[]{:S(2)}) collective-permute-start(bf16[128,512]{1,0:T(8,128)(2,1)S(1)} %get-tuple-element.50), channel_id=1, source_target_pairs={{0,32},{32,0},{16,48},{48,16},{64,96},{96,64},{80,112},{112,80},{1... | collective-permute-start | bytes 393224 | tf_op jit(solution)/shard_map/ppermute | solution.py:223
  100.6 8.0 %collective-permute-start.10 = (bf16[128,512]{1,0:T(8,128)(2,1)S(1)}, bf16[128,512]{1,0:T(8,128)(2,1)S(1)}, u32[]{:S(2)}, u32[]{:S(2)}) collective-permute-start(bf16[128,512]{1,0:T(8,128)(2,1)S(1)} %get-tuple-element.51), channel_id=1, source_target_pairs={{0,16},{16,0},{32,48},{48,32},{64,80},{80,64},{96,112},{112,96},{1... | collective-permute-start | bytes 393224 | tf_op jit(solution)/shard_map/ppermute | solution.py:223

commit v3 on v2

--- a/solution.py
+++ b/solution.py
@@ -11,7 +11,10 @@
 HD = 128
 BS = 128
 EXCHANGES = ((1, False), (4, True), (4, False), (2, True), (2, False), (1, True))
+FAR_ORDER = (0, 4, 3, 1, 2)
 RETURN_ORDER = (1, 3, 5, 2, 4, 0)
+QUAD = 4
+PREPARE_MIB = 60
 
 masked_score = -1e30
 norm_eps = 1e-06
@@ -56,20 +59,29 @@
     return ((frame % 2) ^ ((frame // 2) % 2)) == 1
 
 
-def prepare_kernel(frames, frame_ref, kept_ref, q_ref, k_ref, v_ref, sums_ref, *block_refs):
-    frame = frame_ref[0]
-    width = k_ref.shape[1]
+def prepare_kernel(frames, frame_ref, kept_ref, q_hbm, k_hbm, v_hbm, sums_ref, *refs):
+    block_refs, (q_ref, k_ref, v_ref, sems) = refs[:5], refs[5:]
+    copies = [
+        pltpu.make_async_copy(source, target, sems.at[index])
+        for index, (source, target) in enumerate(((q_hbm, q_ref), (k_hbm, k_ref), (v_hbm, v_ref)))
+    ]
+    for copy in copies:
+        copy.start()
     rows = []
-    for ref in (q_ref, k_ref):
+    for copy, ref in zip(copies, (q_ref, k_ref)):
+        copy.wait()
         for start in range(0, ref.shape[0], 128):
             total = jnp.zeros((128, 128), jnp.float32)
-            for column in range(0, width, 128):
+            for column in range(0, ref.shape[1], 128):
                 part = ref[start : start + 128, column : column + 128].astype(jnp.float32)
                 total += part * part
             rows.append(jnp.sum(total.T, axis=0, keepdims=True))
     packed = jnp.concatenate(rows, axis=0)
     for copy in range(sums_ref.shape[0]):
         sums_ref[copy] = packed
+    copies[2].wait()
+    frame = frame_ref[0]
+    width = k_ref.shape[1]
     first = block_refs[0]
     targets = [first.at[:BS], *block_refs[1:], first.at[BS:]]
     for (distance, shifted), block in zip(EXCHANGES, targets):
@@ -86,24 +98,14 @@
     return (block.astype(jnp.float32) * scale).astype(jnp.bfloat16)
 
 
-def norm_kernel(frames, width_all, frame_ref, kept_ref, sums_ref, q_ref, k_ref, qn_ref, kn_ref, scale_ref, scale_rows):
-    frame = frame_ref[0]
+def norm_kernel(width_all, sums_ref, q_ref, k_ref, qn_ref, kn_ref, scale_ref):
     width = q_ref.shape[1]
     total = sums_ref[0]
     for part in range(1, sums_ref.shape[0]):
         total += sums_ref[part]
     scale = lax.rsqrt(total / width_all + norm_eps)
-    scale_rows[...] = scale
-    scale_ref[...] = jnp.zeros_like(scale_ref)
-    for distance, shifted in EXCHANGES:
-        offset, _ = partner(frame, distance, shifted)
-        block = block_start(kept_ref, frame, frames, distance, shifted) // BS
-        row = q_ref.shape[0] // BS + block
-
-        @pl.when(is_live(frame, frames, distance, shifted))
-        def _():
-            scale_ref[frame + offset] = scale_rows[pl.ds(row, 1), :]
-
+    for copy in range(scale_ref.shape[0]):
+        scale_ref[copy] = scale[q_ref.shape[0] // 128 :]
     row = 0
     for ref, out in ((q_ref, qn_ref), (k_ref, kn_ref)):
         for start in range(0, ref.shape[0], 128):
@@ -124,7 +126,14 @@
     return lax.dot_general(left, right, dims, preferred_element_type=jnp.float32)
 
 
-def attend_kernel(frames, frame_ref, scale_ref, q_ref, k_ref, v_ref, d_ref, *refs):
+def own_kernel(q_ref, k_ref, v_ref, d_ref, scores_ref, dprobs_ref):
+    for index in range(q_ref.shape[1] // HD):
+        head = slice(index * HD, (index + 1) * HD)
+        scores_ref[index] = dot(q_ref[:, head], k_ref[:, head], CONTRACT_LAST) * FACTOR
+        dprobs_ref[index] = dot(d_ref[:, head], v_ref[:, head], CONTRACT_LAST)
+
+
+def attend_kernel(frames, frame_ref, kept_ref, here_ref, near_ref, wide_ref, scores_ref, dprobs_ref, q_ref, v_ref, d_ref, *refs):
     far_refs = refs[:5]
     att_ref, p_own, s_own, s_far, k_far = refs[5:10]
     back_refs = refs[10:16]
@@ -135,24 +144,29 @@
 
     def place(slot, far):
         distance, shifted = EXCHANGES[slot]
-        offset, _ = partner(frame, distance, shifted)
-        scale = by_row(scale_ref[jnp.clip(frame + offset, 0, frames - 1)])
+        offset, slot_there = partner(frame, distance, shifted)
+        other = jnp.clip(frame + offset, 0, frames - 1)
+        member, block = other % QUAD, pl.ds(kept_ref[frame, slot_there ^ 1], 1)
+        scale = jnp.where(
+            other // QUAD == (frame ^ QUAD) // QUAD, near_ref[member, block, :], wide_ref[member, block, :]
+        )
+        scale = by_row(jnp.where(other // QUAD == frame // QUAD, here_ref[member, block, :], scale))
         start = slot * BS
         for column in range(0, width, 128):
             part = far[:BS, column : column + 128]
             k_far[start : start + BS, column : column + 128] = scaled(part, scale)
         v_far[start : start + BS] = far[:BS, width:]
 
-    for slot, far in enumerate(far_refs):
+    for slot, far in zip(FAR_ORDER, far_refs):
         place(slot, far)
 
     @pl.when(via_near(frame))
     def _():
-        place(5, far_refs[4].at[BS:])
+        place(5, far_refs[1].at[BS:])
 
     @pl.when(jnp.logical_not(via_near(frame)))
     def _():
-        place(5, far_refs[3].at[BS:])
+        place(5, far_refs[2].at[BS:])
 
     column = lax.broadcasted_iota(jnp.int32, (1, 6 * BS), 1)
     allowed = column < 0
@@ -166,7 +180,7 @@
         for first in range(0, tokens, CHUNK):
             rows = slice(first, first + CHUNK)
             grads = d_ref[rows, head]
-            own = dot(q_ref[rows, head], k_ref[:, head], CONTRACT_LAST) * FACTOR
+            own = scores_ref[index, rows, :]
             far = jnp.where(allowed, dot(q_ref[rows, head], keys, CONTRACT_LAST) * FACTOR, masked_score)
             top = jnp.maximum(jnp.max(own, axis=1, keepdims=True), jnp.max(far, axis=1, keepdims=True))
             own = jnp.exp(own - top)
@@ -181,7 +195,7 @@
             attended = (dot(own_low, v_ref[:, head]) + dot(far_low, vals)).astype(jnp.bfloat16)
             att_ref[rows, head] = attended
             inner = jnp.sum(grads.astype(f32) * attended.astype(f32), axis=1, keepdims=True)
-            s_own[index, rows, :] = (own * (dot(grads, v_ref[:, head], CONTRACT_LAST) - inner)).astype(jnp.bfloat16)
+            s_own[index, rows, :] = (own * (dprobs_ref[index, rows, :] - inner)).astype(jnp.bfloat16)
             s_far[index, rows, :] = (far * (dot(grads, vals, CONTRACT_LAST) - inner)).astype(jnp.bfloat16)
         grad_k = dot(s_far[index], q_ref[:, head], CONTRACT_FIRST) * FACTOR
         grad_v = dot(p_far[...], d_ref[:, head], CONTRACT_FIRST)
@@ -231,7 +245,7 @@
     relay = got_first[BS:]
     got_wide_two = exchange(jnp.concatenate([wide_two, relay]), frames, 3)
     got_near_two = exchange(jnp.concatenate([near_two, relay]), frames, 4)
-    return got_first, got_wide_far, got_near_far, got_wide_two, got_near_two
+    return got_first, got_near_two, got_wide_two, got_wide_far, got_near_far
 
 
 def swap(blocks, frames):
@@ -251,26 +265,38 @@
     sums, *sent = pl.pallas_call(
         functools.partial(prepare_kernel, frames),
         out_shape=[jax.ShapeDtypeStruct((heads, stat_rows, 128), jnp.float32), pair] + [block] * 4,
-        in_specs=[SMEM] * 2 + [VMEM] * 3,
+        in_specs=[SMEM] * 2 + [pl.BlockSpec(memory_space=pl.ANY)] * 3,
         out_specs=[VMEM] * 6,
-        compiler_params=params(8),
+        scratch_shapes=[pltpu.VMEM((tokens, width), jnp.bfloat16)] * 3 + [pltpu.SemaphoreType.DMA((3,))],
+        compiler_params=params(PREPARE_MIB),
         name="prepare",
     )(frame, kept, queries, keys, values)
     sums = lax.all_to_all(sums, "head", 0, 0)
     far = swap_relayed(sent, frames)
     q_norm, k_norm, scales = pl.pallas_call(
-        functools.partial(norm_kernel, frames, width * heads),
-        out_shape=[flat, flat, jax.ShapeDtypeStruct((frames, 1, BS), jnp.float32)],
-        in_specs=[SMEM] * 2 + [VMEM] * 3,
+        functools.partial(norm_kernel, width * heads),
+        out_shape=[flat, flat, jax.ShapeDtypeStruct((QUAD, tokens // BS, BS), jnp.float32)],
+        in_specs=[VMEM] * 3,
         out_specs=[VMEM] * 3,
-        scratch_shapes=[pltpu.VMEM((stat_rows, 128), jnp.float32)],
         compiler_params=params(8),
         name="normalize",
-    )(frame, kept, sums, queries, keys)
-    scales = lax.all_to_all(scales, "frame", 0, 0)
+    )(sums, queries, keys)
+    quads = [list(range(low, low + QUAD)) for low in range(0, frames, QUAD)]
+    here_scales = lax.all_to_all(scales, "frame", 0, 0, axis_index_groups=quads)
+    wide_scales = exchange(here_scales, frames, 1)
+    near_scales = exchange(here_scales, frames, 2)
     heads_dev = width // HD
     own_shape = (heads_dev, tokens, tokens)
     own_flops = 2 * tokens * tokens * width
+    own_scores, own_dprobs = pl.pallas_call(
+        own_kernel,
+        out_shape=[jax.ShapeDtypeStruct(own_shape, jnp.float32)] * 2,
+        in_specs=[VMEM] * 4,
+        out_specs=[VMEM] * 2,
+        compiler_params=params(8),
+        cost_estimate=pl.CostEstimate(flops=2 * own_flops, bytes_accessed=5 << 20, transcendentals=0),
+        name="own_scores",
+    )(q_norm, k_norm, values, cotangent)
     attended, own_p, own_s, far_s, far_k, *back = pl.pallas_call(
         functools.partial(attend_kernel, frames),
         out_shape=[
@@ -281,7 +307,7 @@
             jax.ShapeDtypeStruct((6 * BS, width), jnp.bfloat16),
         ]
         + [block] * 6,
-        in_specs=[SMEM] + [VMEM] * 10,
+        in_specs=[SMEM] * 2 + [VMEM] * 13,
         out_specs=[VMEM] * 11,
         scratch_shapes=[
             pltpu.VMEM((6 * BS, width), jnp.bfloat16),
@@ -289,7 +315,9 @@
         ],
         compiler_params=params(20),
         name="attend",
-    )(frame, scales, q_norm, k_norm, values, cotangent, *far)
+    )(
+        frame, kept, here_scales, near_scales, wide_scales, own_scores, own_dprobs, q_norm, values, cotangent, *far
+    )
     grad_q, own_k, own_v = pl.pallas_call(
         rest_kernel,
         out_shape=[flat, wide, wide],

time: 111 us -> 113 us (1.018)
  waiting for transfers between devices: 16.3 us -> 5.07 us
  blocking collectives: 0 us -> 10.2 us
  starting transfers between devices: 75.9 us -> 78.2 us
  local copies, waits for them, and re-layouts: 3.69 us -> 1.51 us
  Pallas kernels: 14 us -> 15.3 us
    ppermute x11 -> x13, starting transfers between devices: 38.3 us -> 53.7 us  [exchange(): return lax.ppermute(block, 'frame', route(*EXCHANGES[which], frames))]
    all_to_all x1 -> x0, starting transfers between devices: 13.2 us -> none  [on_device(): scales = lax.all_to_all(scales, 'frame', 0, 0)]
    all_to_all x0 -> x1, blocking collectives: none -> 10.2 us  [on_device(): here_scales = lax.all_to_all(scales, 'frame', 0, 0, axis_index_groups=quads)]
    all_to_all x1 -> x0, waiting for transfers between devices: 8.28 us -> none  [on_device(): scales = lax.all_to_all(scales, 'frame', 0, 0)]
    unnamed x15 -> x11, local copies, waits for them, and re-layouts: 3.68 us -> 1.49 us
    ppermute x11 -> x13, waiting for transfers between devices: 7.15 us -> 5.06 us  [exchange(): return lax.ppermute(block, 'frame', route(*EXCHANGES[which], frames))]
    pallas_call x1, Pallas kernels: 1.92 us -> 3.53 us  [on_device(): pl.pallas_call(functools.partial(prepare_kernel, frames), out_shape=[jax....]
  transfers between devices with their start and end apart: 13 -> 14, of which waited for: 5 -> 3; matrix products, arithmetic and copies ran while one was open for 0% -> 1% of each run, Pallas kernels for 4% -> 3%
where the time goes in v3:
time: 113 us; the launch traced here: 112 us
  starting transfers between devices  78.2 us (69%)
  Pallas kernels  15.3 us (14%)
  blocking collectives  10.2 us (9%)
  waiting for transfers between devices  5.07 us (4%)
  local copies, waits for them, and re-layouts  1.51 us (1%)
    ppermute x13, starting transfers between devices, exchange(): return lax.ppermute(block, 'frame', route(*EXCHANGES[which], frames))  53.7 us
    all_to_all x1, starting transfers between devices, on_device(): sums = lax.all_to_all(sums, 'head', 0, 0)  24.5 us
    all_to_all x1, blocking collectives, on_device(): here_scales = lax.all_to_all(scales, 'frame', 0, 0, axis_index_groups=quads)  10.2 us
    pallas_call x1, Pallas kernels, on_device(): pl.pallas_call(functools.partial(attend_kernel, frames), out_shape=[flat,...  6.53 us
    ppermute x13, waiting for transfers between devices, exchange(): return lax.ppermute(block, 'frame', route(*EXCHANGES[which], frames))  5.06 us
    pallas_call x1, Pallas kernels, on_device(): pl.pallas_call(functools.partial(prepare_kernel, frames), out_shape=[jax....  3.53 us
  transfers between devices with their start and end apart: 14, of which 3 were waited for; matrix products, arithmetic and copies ran while one was open for 1% of the time, Pallas kernels for 3%

profile of v3, /device:TPU:10, one launch (start us, length us, event | category | flops | bytes accessed | tf_op | source)
XLA Modules:
  0.0 112.1 jit_solution(7998100980049739319)
XLA Ops:
  0.6 0.0 copy-start.1
  0.6 0.0 copy-start.3
  0.7 0.0 copy-start.2
  0.7 1.5 %copy.10.kept_ref = s32[64,6]{1,0:T(8,128)} copy(s32[64,6]{0,1:T(8,128)} %param.9) | data formatting | bytes 3072 | tf_op args[4]
  2.2 3.5 %prepare.1 = (f32[16,8,128]{2,1,0:T(8,128)}, bf16[256,512]{1,0:T(8,128)(2,1)}, bf16[128,512]{1,0:T(8,128)(2,1)}, bf16[128,512]{1,0:T(8,128)(2,1)}, bf16[128,512]{1,0:T(8,128)(2,1)}, /*index=5*/bf16[128,512]{1,0:T(8,128)(2,1)}) custom-call(s32[1]{0:T(128)} %bitcast.frame_ref, s32[64,6]{1,0:T(8,128)} %copy.10.kept_ref, bf16[512,256]{1,0:T(8,128)(2,1)} %q_ref.1, ...), custom_call_target="tpu_custom_call" | custom-call | tf_op jit(solution)/shard_map/prepare/pallas_call | solution.py:265
  5.7 1.9 %collective-permute-start.2 = (bf16[256,512]{1,0:T(8,128)(2,1)}, bf16[256,512]{1,0:T(8,128)(2,1)S(1)}, u32[]{:S(2)}, u32[]{:S(2)}) collective-permute-start(bf16[256,512]{1,0:T(8,128)(2,1)} %get-tuple-element.37), channel_id=1, source_target_pairs={{0,16},{16,0},{32,48},{48,32},{64,80},{80,64},{96,112},{112,96},{1... | collective-permute-start | bytes 786440 | tf_op jit(solution)/shard_map/ppermute | solution.py:237
  7.6 24.5 %all-to-all-start = ((f32[16,8,128]{2,1,0:T(8,128)}), f32[16,8,128]{2,1,0:T(8,128)S(1)}, u32[]{:S(2)}, u32[]{:S(2)}) async-start(f32[16,8,128]{2,1,0:T(8,128)} %get-tuple-element.31), calls=%async_computation | async-start | bytes 131072 | tf_op jit(solution)/shard_map/all_to_all | solution.py:274
  32.1 0.0 collective-permute-done.2.refs_0_
  32.1 1.0 pad_maximum_fusion
  33.1 8.8 %collective-permute-start.4 = (bf16[256,512]{1,0:T(8,128)(2,1)S(1)}, bf16[256,512]{1,0:T(8,128)(2,1)S(1)}, u32[]{:S(2)}, u32[]{:S(2)}) collective-permute-start(bf16[256,512]{1,0:T(8,128)(2,1)S(1)} %get-tuple-element.58), channel_id=1, source_target_pairs={{32,64},{64,32},{48,80},{80,48},{96,128},{128,96},{112,144},{144,1... | collective-permute-start | bytes 786440 | tf_op jit(solution)/shard_map/ppermute | solution.py:237
  41.9 1.9 %collective-permute-start.3 = (bf16[256,512]{1,0:T(8,128)(2,1)S(1)}, bf16[256,512]{1,0:T(8,128)(2,1)S(1)}, u32[]{:S(2)}, u32[]{:S(2)}) collective-permute-start(bf16[256,512]{1,0:T(8,128)(2,1)S(1)} %get-tuple-element.59), channel_id=1, source_target_pairs={{0,32},{32,0},{16,48},{48,16},{64,96},{96,64},{80,112},{112,80},{1... | collective-permute-start | bytes 786440 | tf_op jit(solution)/shard_map/ppermute | solution.py:237
  43.9 5.1 %collective-permute-start.5 = (bf16[128,512]{1,0:T(8,128)(2,1)}, bf16[128,512]{1,0:T(8,128)(2,1)S(1)}, u32[]{:S(2)}, u32[]{:S(2)}) collective-permute-start(bf16[128,512]{1,0:T(8,128)(2,1)} %get-tuple-element.40), channel_id=1, source_target_pairs={{64,128},{128,64},{80,144},{144,80},{96,160},{160,96},{112,176},{1... | collective-permute-start | bytes 393224 | tf_op jit(solution)/shard_map/ppermute | solution.py:237
  49.0 1.9 %collective-permute-start.6 = (bf16[128,512]{1,0:T(8,128)(2,1)}, bf16[128,512]{1,0:T(8,128)(2,1)S(1)}, u32[]{:S(2)}, u32[]{:S(2)}) collective-permute-start(bf16[128,512]{1,0:T(8,128)(2,1)} %get-tuple-element.41), channel_id=1, source_target_pairs={{0,64},{64,0},{16,80},{80,16},{32,96},{96,32},{48,112},{112,48},{1... | collective-permute-start | bytes 393224 | tf_op jit(solution)/shard_map/ppermute | solution.py:237
  50.9 0.0 all-to-all-done.sums_ref
  50.9 0.2 normalize.1
  51.1 10.2 %all_to_all.10.here_ref = f32[4,4,128]{2,1,0:T(4,128)S(1)} all-to-all(f32[4,4,128]{2,1,0:T(4,128)S(1)} %get-tuple-element.32), channel_id=1, replica_groups={{0,16,32,48},{64,80,96,112},{128,144,160,176},{192,208,224,240},{256,27..., dimensions={0} | all-to-all | bytes 16384 | tf_op jit(solution)/shard_map/all_to_all | solution.py:285
  61.4 4.7 %collective-permute-start.1 = (f32[4,4,128]{2,1,0:T(4,128)S(1)}, f32[4,4,128]{2,1,0:T(4,128)S(1)}, u32[]{:S(2)}, u32[]{:S(2)}) collective-permute-start(f32[4,4,128]{2,1,0:T(4,128)S(1)} %all_to_all.10.here_ref), channel_id=1, source_target_pairs={{64,128},{128,64},{80,144},{144,80},{96,160},{160,96},{112,176},{1... | collective-permute-start | bytes 24584 | tf_op jit(solution)/shard_map/ppermute | solution.py:237
  66.1 7.1 %collective-permute-start = (f32[4,4,128]{2,1,0:T(4,128)S(1)}, f32[4,4,128]{2,1,0:T(4,128)S(1)}, u32[]{:S(2)}, u32[]{:S(2)}) collective-permute-start(f32[4,4,128]{2,1,0:T(4,128)S(1)} %all_to_all.10.here_ref), channel_id=1, source_target_pairs={{0,64},{64,0},{16,80},{80,16},{32,96},{96,32},{48,112},{112,48},{1... | collective-permute-start | bytes 24584 | tf_op jit(solution)/shard_map/ppermute | solution.py:237
  73.2 0.7 own_scores.1
  73.9 0.0 collective-permute-done.1.wide_ref
  73.9 0.9 collective-permute-done.near_ref
  74.8 6.5 %attend.1 = (bf16[512,256]{1,0:T(8,128)(2,1)}, bf16[2,512,512]{2,1,0:T(8,128)(2,1)S(1)}, bf16[2,512,512]{2,1,0:T(8,128)(2,1)S(1)}, bf16[2,512,768]{2,1,0:T(8,128...) custom-call(s32[1]{0:T(128)} %bitcast.frame_ref, ...), custom_call_target="tpu_custom_call" | custom-call | tf_op jit(solution)/shard_map/attend/pallas_call | solution.py:300
  81.3 5.5 %collective-permute-start.7 = (bf16[128,512]{1,0:T(8,128)(2,1)S(1)}, bf16[128,512]{1,0:T(8,128)(2,1)S(1)}, u32[]{:S(2)}, u32[]{:S(2)}) collective-permute-start(bf16[128,512]{1,0:T(8,128)(2,1)S(1)} %get-tuple-element.50), channel_id=1, source_target_pairs={{64,128},{128,64},{80,144},{144,80},{96,160},{160,96},{112,176},{1... | collective-permute-start | bytes 393224 | tf_op jit(solution)/shard_map/ppermute | solution.py:237
  86.8 7.2 %collective-permute-start.8 = (bf16[128,512]{1,0:T(8,128)(2,1)S(1)}, bf16[128,512]{1,0:T(8,128)(2,1)S(1)}, u32[]{:S(2)}, u32[]{:S(2)}) collective-permute-start(bf16[128,512]{1,0:T(8,128)(2,1)S(1)} %get-tuple-element.51), channel_id=1, source_target_pairs={{32,64},{64,32},{48,80},{80,48},{96,128},{128,96},{112,144},{144,1... | collective-permute-start | bytes 393224 | tf_op jit(solution)/shard_map/ppermute | solution.py:237
  94.0 3.8 %collective-permute-start.9 = (bf16[128,512]{1,0:T(8,128)(2,1)S(1)}, bf16[128,512]{1,0:T(8,128)(2,1)S(1)}, u32[]{:S(2)}, u32[]{:S(2)}) collective-permute-start(bf16[128,512]{1,0:T(8,128)(2,1)S(1)} %get-tuple-element.52), channel_id=1, source_target_pairs={{16,32},{32,16},{48,64},{64,48},{80,96},{96,80},{112,128},{128,112... | collective-permute-start | bytes 393224 | tf_op jit(solution)/shard_map/ppermute | solution.py:237
  97.9 1.9 %collective-permute-start.10 = (bf16[128,512]{1,0:T(8,128)(2,1)S(1)}, bf16[128,512]{1,0:T(8,128)(2,1)S(1)}, u32[]{:S(2)}, u32[]{:S(2)}) collective-permute-start(bf16[128,512]{1,0:T(8,128)(2,1)S(1)} %get-tuple-element.53), channel_id=1, source_target_pairs={{0,64},{64,0},{16,80},{80,16},{32,96},{96,32},{48,112},{112,48},{1... | collective-permute-start | bytes 393224 | tf_op jit(solution)/shard_map/ppermute | solution.py:237
  99.8 1.9 %collective-permute-start.11 = (bf16[128,512]{1,0:T(8,128)(2,1)S(1)}, bf16[128,512]{1,0:T(8,128)(2,1)S(1)}, u32[]{:S(2)}, u32[]{:S(2)}) collective-permute-start(bf16[128,512]{1,0:T(8,128)(2,1)S(1)} %get-tuple-element.54), channel_id=1, source_target_pairs={{0,32},{32,0},{16,48},{48,16},{64,96},{96,64},{80,112},{112,80},{1... | collective-permute-start | bytes 393224 | tf_op jit(solution)/shard_map/ppermute | solution.py:237
  101.7 1.9 %collective-permute-start.12 = (bf16[128,512]{1,0:T(8,128)(2,1)S(1)}, bf16[128,512]{1,0:T(8,128)(2,1)S(1)}, u32[]{:S(2)}, u32[]{:S(2)}) collective-permute-start(bf16[128,512]{1,0:T(8,128)(2,1)S(1)} %get-tuple-element.55), channel_id=1, source_target_pairs={{0,16},{16,0},{32,48},{48,32},{64,80},{80,64},{96,112},{112,96},{1... | collective-permute-start | bytes 393224 | tf_op jit(solution)/shard_map/ppermute | solution.py:237
  103.7 2.1 %rest.1 = (bf16[512,256]{1,0:T(8,128)(2,1)}, f32[512,256]{1,0:T(8,128)S(1)}, f32[512,256]{1,0:T(8,128)S(1)}) custom-call(bf16[2,512,512]{2,1,0:T(8,128)(2,1)S(1)} %get-tuple-element.43.p_own, bf16[2,512,512]{2,1,0:T(8,128)(2,1)S(1)} %get-tuple-element.44.s_own, bf16[2,512,768]{2,1,0:T(8,128)(2,1)S(1)} %get-tuple-element.45.s_far, ...), custom_call_target="tpu_custom_call" | custom-call | flops 536870912 | bytes 8388608 | tf_op jit(solution)/shard_map/rest/pallas_call | solution.py:321
  105.8 2.8 %collective-permute-done.9.refs_2_ = bf16[128,512]{1,0:T(8,128)(2,1)S(1)} collective-permute-done((bf16[128,512]{1,0:T(8,128)(2,1)S(1)}, bf16[128,512]{1,0:T(8,128)(2,1)S(1)}, u32[]{:S(2)}, u32[]{:S(2)}) %collective-permute-start.9) | collective-permute-done | bytes 131104 | tf_op jit(solution)/shard_map/ppermute | solution.py:237
  108.5 1.4 %collective-permute-done.10.refs_3_ = bf16[128,512]{1,0:T(8,128)(2,1)S(1)} collective-permute-done((bf16[128,512]{1,0:T(8,128)(2,1)S(1)}, bf16[128,512]{1,0:T(8,128)(2,1)S(1)}, u32[]{:S(2)}, u32[]{:S(2)}) %collective-permute-start.10) | collective-permute-done | bytes 131104 | tf_op jit(solution)/shard_map/ppermute | solution.py:237
  110.0 2.2 %collect.1 = (bf16[512,256]{1,0:T(8,128)(2,1)}, bf16[512,256]{1,0:T(8,128)(2,1)}) custom-call(s32[1]{0:T(128)} %bitcast.frame_ref, s32[64,6]{1,0:T(8,128)S(1)} %copy-done.4, f32[512,256]{1,0:T(8,128)S(1)} %get-tuple-element.48.gk_ref, f32[512,256]{1,0:T(8,128)S(1)} %get-tuple-element.49.gv_ref, bf16[128,512]{1,0:T(8,128)(2,1)S(1)} %collective-permute-done.7.refs_0_, ...), custom_call_target="tpu_custom_call" | custom-call | tf_op jit(solution)/shard_map/collect/pallas_call | solution.py:331
  (16 shorter events, 0.0 us)
Async XLA Ops:
  0.6 72.6 %copy-start.1 = (bf16[512,256]{1,0:T(8,128)(2,1)S(1)}, bf16[512,256]{1,0:T(8,128)(2,1)}, u32[]{:S(2)}) copy-start(bf16[512,256]{1,0:T(8,128)(2,1)} %v_ref.3) | copy-start | bytes 786436
  0.6 50.3 %copy-start.3 = (bf16[512,256]{1,0:T(8,128)(2,1)S(1)}, bf16[512,256]{1,0:T(8,128)(2,1)}, u32[]{:S(2)}) copy-start(bf16[512,256]{1,0:T(8,128)(2,1)} %k_ref.1) | copy-start | bytes 786436
  0.7 50.3 %copy-start.2 = (bf16[512,256]{1,0:T(8,128)(2,1)S(1)}, bf16[512,256]{1,0:T(8,128)(2,1)}, u32[]{:S(2)}) copy-start(bf16[512,256]{1,0:T(8,128)(2,1)} %q_ref.1) | copy-start | bytes 786436
  0.7 72.5 %copy-start = (bf16[512,256]{1,0:T(8,128)(2,1)S(1)}, bf16[512,256]{1,0:T(8,128)(2,1)}, u32[]{:S(2)}) copy-start(bf16[512,256]{1,0:T(8,128)(2,1)} %d_ref.5) | copy-start | bytes 786436
  2.1 72.7 %copy-start.4 = (s32[64,6]{1,0:T(8,128)S(1)}, s32[64,6]{1,0:T(8,128)}, u32[]{:S(2)}) copy-start(s32[64,6]{1,0:T(8,128)} %copy.10.kept_ref) | copy-start | bytes 4612
  5.7 26.4 %collective-permute-start.2 = (bf16[256,512]{1,0:T(8,128)(2,1)}, bf16[256,512]{1,0:T(8,128)(2,1)S(1)}, u32[]{:S(2)}, u32[]{:S(2)}) collective-permute-start(bf16[256,512]{1,0:T(8,128)(2,1)} %get-tuple-element.37), channel_id=1, source_target_pairs={{0,16},{16,0},{32,48},{48,32},{64,80},{80,64},{96,112},{112,96},{1... | collective-permute-start | bytes 786440 | tf_op jit(solution)/shard_map/ppermute | solution.py:237
  7.6 43.3 %all-to-all-start = ((f32[16,8,128]{2,1,0:T(8,128)}), f32[16,8,128]{2,1,0:T(8,128)S(1)}, u32[]{:S(2)}, u32[]{:S(2)}) async-start(f32[16,8,128]{2,1,0:T(8,128)} %get-tuple-element.31), calls=%async_computation | async-start | bytes 131072 | tf_op jit(solution)/shard_map/all_to_all | solution.py:274
  33.1 41.7 %collective-permute-start.4 = (bf16[256,512]{1,0:T(8,128)(2,1)S(1)}, bf16[256,512]{1,0:T(8,128)(2,1)S(1)}, u32[]{:S(2)}, u32[]{:S(2)}) collective-permute-start(bf16[256,512]{1,0:T(8,128)(2,1)S(1)} %get-tuple-element.58), channel_id=1, source_target_pairs={{32,64},{64,32},{48,80},{80,48},{96,128},{128,96},{112,144},{144,1... | collective-permute-start | bytes 786440 | tf_op jit(solution)/shard_map/ppermute | solution.py:237
  41.9 32.9 %collective-permute-start.3 = (bf16[256,512]{1,0:T(8,128)(2,1)S(1)}, bf16[256,512]{1,0:T(8,128)(2,1)S(1)}, u32[]{:S(2)}, u32[]{:S(2)}) collective-permute-start(bf16[256,512]{1,0:T(8,128)(2,1)S(1)} %get-tuple-element.59), channel_id=1, source_target_pairs={{0,32},{32,0},{16,48},{48,16},{64,96},{96,64},{80,112},{112,80},{1... | collective-permute-start | bytes 786440 | tf_op jit(solution)/shard_map/ppermute | solution.py:237
  43.9 22.2 %collective-permute-start.5 = (bf16[128,512]{1,0:T(8,128)(2,1)}, bf16[128,512]{1,0:T(8,128)(2,1)S(1)}, u32[]{:S(2)}, u32[]{:S(2)}) collective-permute-start(bf16[128,512]{1,0:T(8,128)(2,1)} %get-tuple-element.40), channel_id=1, source_target_pairs={{64,128},{128,64},{80,144},{144,80},{96,160},{160,96},{112,176},{1... | collective-permute-start | bytes 393224 | tf_op jit(solution)/shard_map/ppermute | solution.py:237
  49.0 25.0 %collective-permute-start.6 = (bf16[128,512]{1,0:T(8,128)(2,1)}, bf16[128,512]{1,0:T(8,128)(2,1)S(1)}, u32[]{:S(2)}, u32[]{:S(2)}) collective-permute-start(bf16[128,512]{1,0:T(8,128)(2,1)} %get-tuple-element.41), channel_id=1, source_target_pairs={{0,64},{64,0},{16,80},{80,16},{32,96},{96,32},{48,112},{112,48},{1... | collective-permute-start | bytes 393224 | tf_op jit(solution)/shard_map/ppermute | solution.py:237
  61.4 12.5 %collective-permute-start.1 = (f32[4,4,128]{2,1,0:T(4,128)S(1)}, f32[4,4,128]{2,1,0:T(4,128)S(1)}, u32[]{:S(2)}, u32[]{:S(2)}) collective-permute-start(f32[4,4,128]{2,1,0:T(4,128)S(1)} %all_to_all.10.here_ref), channel_id=1, source_target_pairs={{64,128},{128,64},{80,144},{144,80},{96,160},{160,96},{112,176},{1... | collective-permute-start | bytes 24584 | tf_op jit(solution)/shard_map/ppermute | solution.py:237
  66.1 8.7 %collective-permute-start = (f32[4,4,128]{2,1,0:T(4,128)S(1)}, f32[4,4,128]{2,1,0:T(4,128)S(1)}, u32[]{:S(2)}, u32[]{:S(2)}) collective-permute-start(f32[4,4,128]{2,1,0:T(4,128)S(1)} %all_to_all.10.here_ref), channel_id=1, source_target_pairs={{0,64},{64,0},{16,80},{80,16},{32,96},{96,32},{48,112},{112,48},{1... | collective-permute-start | bytes 24584 | tf_op jit(solution)/shard_map/ppermute | solution.py:237
  81.3 20.4 %collective-permute-start.7 = (bf16[128,512]{1,0:T(8,128)(2,1)S(1)}, bf16[128,512]{1,0:T(8,128)(2,1)S(1)}, u32[]{:S(2)}, u32[]{:S(2)}) collective-permute-start(bf16[128,512]{1,0:T(8,128)(2,1)S(1)} %get-tuple-element.50), channel_id=1, source_target_pairs={{64,128},{128,64},{80,144},{144,80},{96,160},{160,96},{112,176},{1... | collective-permute-start | bytes 393224 | tf_op jit(solution)/shard_map/ppermute | solution.py:237
  86.8 19.0 %collective-permute-start.8 = (bf16[128,512]{1,0:T(8,128)(2,1)S(1)}, bf16[128,512]{1,0:T(8,128)(2,1)S(1)}, u32[]{:S(2)}, u32[]{:S(2)}) collective-permute-start(bf16[128,512]{1,0:T(8,128)(2,1)S(1)} %get-tuple-element.51), channel_id=1, source_target_pairs={{32,64},{64,32},{48,80},{80,48},{96,128},{128,96},{112,144},{144,1... | collective-permute-start | bytes 393224 | tf_op jit(solution)/shard_map/ppermute | solution.py:237
  94.0 14.5 %collective-permute-start.9 = (bf16[128,512]{1,0:T(8,128)(2,1)S(1)}, bf16[128,512]{1,0:T(8,128)(2,1)S(1)}, u32[]{:S(2)}, u32[]{:S(2)}) collective-permute-start(bf16[128,512]{1,0:T(8,128)(2,1)S(1)} %get-tuple-element.52), channel_id=1, source_target_pairs={{16,32},{32,16},{48,64},{64,48},{80,96},{96,80},{112,128},{128,112... | collective-permute-start | bytes 393224 | tf_op jit(solution)/shard_map/ppermute | solution.py:237
  97.9 12.1 %collective-permute-start.10 = (bf16[128,512]{1,0:T(8,128)(2,1)S(1)}, bf16[128,512]{1,0:T(8,128)(2,1)S(1)}, u32[]{:S(2)}, u32[]{:S(2)}) collective-permute-start(bf16[128,512]{1,0:T(8,128)(2,1)S(1)} %get-tuple-element.53), channel_id=1, source_target_pairs={{0,64},{64,0},{16,80},{80,16},{32,96},{96,32},{48,112},{112,48},{1... | collective-permute-start | bytes 393224 | tf_op jit(solution)/shard_map/ppermute | solution.py:237
  99.8 10.2 %collective-permute-start.11 = (bf16[128,512]{1,0:T(8,128)(2,1)S(1)}, bf16[128,512]{1,0:T(8,128)(2,1)S(1)}, u32[]{:S(2)}, u32[]{:S(2)}) collective-permute-start(bf16[128,512]{1,0:T(8,128)(2,1)S(1)} %get-tuple-element.54), channel_id=1, source_target_pairs={{0,32},{32,0},{16,48},{48,16},{64,96},{96,64},{80,112},{112,80},{1... | collective-permute-start | bytes 393224 | tf_op jit(solution)/shard_map/ppermute | solution.py:237
  101.7 8.2 %collective-permute-start.12 = (bf16[128,512]{1,0:T(8,128)(2,1)S(1)}, bf16[128,512]{1,0:T(8,128)(2,1)S(1)}, u32[]{:S(2)}, u32[]{:S(2)}) collective-permute-start(bf16[128,512]{1,0:T(8,128)(2,1)S(1)} %get-tuple-element.55), channel_id=1, source_target_pairs={{0,16},{16,0},{32,48},{48,32},{64,80},{80,64},{96,112},{112,96},{1... | collective-permute-start | bytes 393224 | tf_op jit(solution)/shard_map/ppermute | solution.py:237

commit v4 on v3

v4 whole, which is shorter than its diff:
```python
import functools
import math

import jax
import jax.numpy as jnp
from jax import lax
from jax.experimental import pallas as pl
from jax.experimental.pallas import tpu as pltpu
from jax.sharding import PartitionSpec as P

HD = 128
BS = 128
EXCHANGES = ((4, True), (2, True), (1, True), (4, False), (2, False), (1, False))
EARLY = (0, 3)

masked_score = -1e30
norm_eps = 1e-06

VMEM = pl.BlockSpec(memory_space=pltpu.VMEM)
SMEM = pl.BlockSpec(memory_space=pltpu.SMEM)


def params(mib):
    return pltpu.CompilerParams(vmem_limit_bytes=mib << 20)


def route(distance, shifted, frames):
    pairs = []
    for low in range(frames - distance):
        if ((low // distance) % 2 == 1) == shifted:
            pairs += [(low, low + distance), (low + distance, low)]
    return pairs


def partner(frame, distance, shifted):
    up = ((frame // distance) % 2 == 1) == shifted
    level = int(math.log2(distance))
    offset = jnp.where(up, distance, -distance)
    slot = jnp.where(up, 2 * level + 1, 2 * level)
    return offset, slot


def block_start(kept_ref, frame, frames, distance, shifted):
    offset, slot = partner(frame, distance, shifted)
    other = jnp.clip(frame + offset, 0, frames - 1)
    return pl.multiple_of(kept_ref[other, slot] * BS, BS)


def is_live(frame, frames, distance, shifted):
    offset, _ = partner(frame, distance, shifted)
    other = frame + offset
    return jnp.logical_and(other >= 0, other < frames)


def sums_kernel(q_ref, k_ref, sums_ref, q_held, k_held):
    rows = []
    for ref, held in ((q_ref, q_held), (k_ref, k_held)):
        for start in range(0, ref.shape[0], 128):
            total = jnp.zeros((128, 128), jnp.float32)
            for column in range(0, ref.shape[1], 128):
                part = ref[start : start + 128, column : column + 128]
                held[start : start + 128, column : column + 128] = part
                part = part.astype(jnp.float32)
                total += part * part
            rows.append(jnp.sum(total.T, axis=0, keepdims=True))
    packed = jnp.concatenate(rows, axis=0)
    for copy in range(sums_ref.shape[0]):
        sums_ref[copy] = packed


def early_kernel(frames, frame_ref, kept_ref, v_ref, v_held, *block_refs):
    v_held[...] = v_ref[...]
    for which, block in zip(EARLY, block_refs):
        block[...] = v_ref[pl.ds(block_start(kept_ref, frame_ref[0], frames, *EXCHANGES[which]), BS), :]


def by_row(scale):
    return jnp.broadcast_to(scale, (128, 128)).T


def scaled(block, scale):
    return (block.astype(jnp.float32) * scale).astype(jnp.bfloat16)


def norm_kernel(frames, width_all, frame_ref, kept_ref, sums_ref, q_ref, k_ref, v_ref, qn_ref, kn_ref, *block_refs):
    width = q_ref.shape[1]
    total = sums_ref[0]
    for part in range(1, sums_ref.shape[0]):
        total += sums_ref[part]
    scale = lax.rsqrt(total / width_all + norm_eps)
    row = 0
    for ref, out in ((q_ref, qn_ref), (k_ref, kn_ref)):
        for start in range(0, ref.shape[0], 128):
            factor = by_row(scale[row : row + 1, :])
            row += 1
            for column in range(0, width, 128):
                part = ref[start : start + 128, column : column + 128]
                out[start : start + 128, column : column + 128] = scaled(part, factor)
    for which, block in enumerate(block_refs):
        rows = pl.ds(block_start(kept_ref, frame_ref[0], frames, *EXCHANGES[which]), BS)
        block[:, :width] = kn_ref[rows, :]
        if which not in EARLY:
            block[:, width:] = v_ref[rows, :]


CONTRACT_LAST = (((1,), (1,)), ((), ()))
CONTRACT_FIRST = (((0,), (0,)), ((), ()))
FACTOR = 1.0 / math.sqrt(HD)
EXPONENT = FACTOR * math.log2(math.e)
CHUNK = 256


def dot(left, right, dims=(((1,), (0,)), ((), ()))):
    return lax.dot_general(left, right, dims, preferred_element_type=jnp.float32)


def own_kernel(q_ref, k_ref, v_ref, d_ref, scores_ref, dprobs_ref):
    for index in range(q_ref.shape[1] // HD):
        head = slice(index * HD, (index + 1) * HD)
        scores_ref[index] = dot(q_ref[:, head], k_ref[:, head], CONTRACT_LAST)
        dprobs_ref[index] = dot(d_ref[:, head], v_ref[:, head], CONTRACT_LAST)


def attend_kernel(frames, frame_ref, scores_ref, dprobs_ref, q_ref, v_ref, d_ref, *refs):
    far_refs, early_refs = refs[:6], refs[6:8]
    att_ref, p_own, s_own, s_far, k_far = refs[8:13]
    back_refs = refs[13:19]
    v_far, p_far = refs[19:]
    frame = frame_ref[0]
    tokens, width = q_ref.shape
    f32 = jnp.float32
    column = lax.broadcasted_iota(jnp.int32, (1, 6 * BS), 1)
    allowed = column < 0
    for slot, (distance, shifted) in enumerate(EXCHANGES):
        rows = slice(slot * BS, (slot + 1) * BS)
        k_far[rows] = far_refs[slot][:, :width]
        v_far[rows] = early_refs[EARLY.index(slot)][...] if slot in EARLY else far_refs[slot][:, width:]
        inside = jnp.logical_and(column >= slot * BS, column < (slot + 1) * BS)
        live = is_live(frame, frames, distance, shifted)
        allowed = jnp.logical_or(allowed, jnp.logical_and(inside, live))
    for index in range(width // HD):
        head = slice(index * HD, (index + 1) * HD)
        keys, vals = k_far[:, head], v_far[:, head]
        for first in range(0, tokens, CHUNK):
            rows = slice(first, first + CHUNK)
            grads = d_ref[rows, head]
            own = scores_ref[index, rows, :]
            far = jnp.where(allowed, dot(q_ref[rows, head], keys, CONTRACT_LAST), masked_score)
            top = jnp.maximum(jnp.max(own, axis=1, keepdims=True), jnp.max(far, axis=1, keepdims=True))
            own = jnp.exp2((own - top) * EXPONENT)
            far = jnp.exp2((far - top) * EXPONENT)
            share = 1.0 / (jnp.sum(own, axis=1, keepdims=True) + jnp.sum(far, axis=1, keepdims=True))
            own_low = (own * share).astype(jnp.bfloat16)
            far_low = (far * share).astype(jnp.bfloat16)
            p_own[index, rows, :] = own_low
            p_far[rows, :] = far_low
            attended = (dot(own_low, v_ref[:, head]) + dot(far_low, vals)).astype(jnp.bfloat16)
            att_ref[rows, head] = attended
            inner = jnp.sum(grads.astype(f32) * attended.astype(f32), axis=1, keepdims=True)
            s_own[index, rows, :] = (own * ((dprobs_ref[index, rows, :] - inner) * share)).astype(jnp.bfloat16)
            s_far[index, rows, :] = (far * ((dot(grads, vals, CONTRACT_LAST) - inner) * share)).astype(jnp.bfloat16)
        grad_k = dot(s_far[index], q_ref[:, head], CONTRACT_FIRST) * FACTOR
        grad_v = dot(p_far[...], d_ref[:, head], CONTRACT_FIRST)
        for slot, back in enumerate(back_refs):
            rows = slice(slot * BS, (slot + 1) * BS)
            back[:, index * HD : (index + 1) * HD] = grad_k[rows].astype(jnp.bfloat16)
            back[:, width + index * HD : width + (index + 1) * HD] = grad_v[rows].astype(jnp.bfloat16)


def rest_kernel(p_own, s_own, s_far, k_far, q_ref, k_ref, d_ref, gq_ref, gk_ref, gv_ref):
    for index in range(q_ref.shape[1] // HD):
        head = slice(index * HD, (index + 1) * HD)
        grad_q = dot(s_own[index], k_ref[:, head]) + dot(s_far[index], k_far[:, head])
        gq_ref[:, head] = (grad_q * FACTOR).astype(jnp.bfloat16)
        gk_ref[:, head] = dot(s_own[index], q_ref[:, head], CONTRACT_FIRST) * FACTOR
        gv_ref[:, head] = dot(p_own[index], d_ref[:, head], CONTRACT_FIRST)


def collect_kernel(frames, frame_ref, kept_ref, gk_ref, gv_ref, *refs):
    back_refs, (outk_ref, outv_ref, acc_k, acc_v) = refs[:6], refs[6:]
    frame = frame_ref[0]
    width = gk_ref.shape[1]
    acc_k[...] = gk_ref[...]
    acc_v[...] = gv_ref[...]
    for (distance, shifted), back in zip(EXCHANGES, back_refs):
        rows = pl.ds(block_start(kept_ref, frame, frames, distance, shifted), BS)

        @pl.when(is_live(frame, frames, distance, shifted))
        def _():
            acc_k[rows, :] += back[:, :width].astype(jnp.float32)
            acc_v[rows, :] += back[:, width:].astype(jnp.float32)

    outk_ref[...] = acc_k[...].astype(jnp.bfloat16)
    outv_ref[...] = acc_v[...].astype(jnp.bfloat16)


def exchange(block, frames, which):
    return lax.ppermute(block, "frame", route(*EXCHANGES[which], frames))


def on_device(queries, keys, values, cotangent, kept):
    frames = lax.axis_size("frame")
    heads = lax.axis_size("head")
    tokens, width = queries.shape
    heads_dev = width // HD
    frame = lax.axis_index("frame").reshape(1)
    flat = jax.ShapeDtypeStruct((tokens, width), jnp.bfloat16)
    wide = jax.ShapeDtypeStruct((tokens, width), jnp.float32)
    half = jax.ShapeDtypeStruct((BS, width), jnp.bfloat16)
    block = jax.ShapeDtypeStruct((BS, 2 * width), jnp.bfloat16)
    sent_shapes = [half if which in EARLY else block for which in range(len(EXCHANGES))]
    sums, queries, keys = pl.pallas_call(
        sums_kernel,
        out_shape=[jax.ShapeDtypeStruct((heads, 2 * tokens // 128, 128), jnp.float32)] + [flat] * 2,
        in_specs=[VMEM] * 2,
        out_specs=[VMEM] * 3,
        compiler_params=params(6),
        name="square_sums",
    )(queries, keys)
    sums = lax.all_to_all(sums, "head", 0, 0)
    values, *early = pl.pallas_call(
        functools.partial(early_kernel, frames),
        out_shape=[flat] + [half] * len(EARLY),
        in_specs=[SMEM] * 2 + [VMEM],
        out_specs=[VMEM] * (1 + len(EARLY)),
        compiler_params=params(6),
        name="early",
    )(frame, kept, values)
    early = [exchange(part, frames, which) for which, part in zip(EARLY, early)]
    q_norm, k_norm, *sent = pl.pallas_call(
        functools.partial(norm_kernel, frames, width * heads),
        out_shape=[flat, flat] + sent_shapes,
        in_specs=[SMEM] * 2 + [VMEM] * 4,
        out_specs=[VMEM] * 8,
        compiler_params=params(8),
        name="normalize",
    )(frame, kept, sums, queries, keys, values)
    far = [exchange(part, frames, which) for which, part in enumerate(sent)]
    own_shape = (heads_dev, tokens, tokens)
    own_flops = 2 * tokens * tokens * width
    own_scores, own_dprobs = pl.pallas_call(
        own_kernel,
        out_shape=[jax.ShapeDtypeStruct(own_shape, jnp.float32)] * 2,
        in_specs=[VMEM] * 4,
        out_specs=[VMEM] * 2,
        compiler_params=params(8),
        cost_estimate=pl.CostEstimate(flops=2 * own_flops, bytes_accessed=5 << 20, transcendentals=0),
        name="own_scores",
    )(q_norm, k_norm, values, cotangent)
    attended, own_p, own_s, far_s, far_k, *back = pl.pallas_call(
        functools.partial(attend_kernel, frames),
        out_shape=[
            flat,
            jax.ShapeDtypeStruct(own_shape, jnp.bfloat16),
            jax.ShapeDtypeStruct(own_shape, jnp.bfloat16),
            jax.ShapeDtypeStruct((heads_dev, tokens, 6 * BS), jnp.bfloat16),
            jax.ShapeDtypeStruct((6 * BS, width), jnp.bfloat16),
        ]
        + [block] * 6,
        in_specs=[SMEM] + [VMEM] * 13,
        out_specs=[VMEM] * 11,
        scratch_shapes=[
            pltpu.VMEM((6 * BS, width), jnp.bfloat16),
            pltpu.VMEM((tokens, 6 * BS), jnp.bfloat16),
        ],
        compiler_params=params(20),
        name="attend",
    )(frame, own_scores, own_dprobs, q_norm, values, cotangent, *far, *early)
    grad_q, own_k, own_v = pl.pallas_call(
        rest_kernel,
        out_shape=[flat, wide, wide],
        in_specs=[VMEM] * 7,
        out_specs=[VMEM] * 3,
        compiler_params=params(8),
        cost_estimate=pl.CostEstimate(flops=4 * own_flops, bytes_accessed=8 << 20, transcendentals=0),
        name="rest",
    )(own_p, own_s, far_s, far_k, q_norm, k_norm, cotangent)
    back = [exchange(part, frames, which) for which, part in enumerate(back)]
    grad_k, grad_v = pl.pallas_call(
        functools.partial(collect_kernel, frames),
        out_shape=[flat, flat],
        in_specs=[SMEM] * 2 + [VMEM] * 8,
        out_specs=[VMEM] * 2,
        scratch_shapes=[pltpu.VMEM((tokens, width), jnp.float32)] * 2,
        compiler_params=params(8),
        name="collect",
    )(frame, kept, own_k, own_v, *back)
    return attended, grad_q, grad_k, grad_v


def solution(mesh):
    spec = P("frame", "head")
    return jax.shard_map(
        on_device,
        mesh=mesh,
        in_specs=(spec, spec, spec, spec, P()),
        out_specs=(spec, spec, spec, spec),
        check_vma=False,
    )
```

time: 113 us -> 115 us (1.018)
  the two profiles are of different devices: /device:TPU:10 before, /device:TPU:2 now
where the time goes in v4:
time: 115 us
  starting transfers between devices  83.6 us (73%)
  Pallas kernels  13.2 us (11%)
  waiting for transfers between devices  12.4 us (11%)
  local copies, waits for them, and re-layouts  4.57 us (4%)
    ppermute x14, starting transfers between devices, exchange(): return lax.ppermute(block, 'frame', route(*EXCHANGES[which], frames))  59.5 us
    all_to_all x1, starting transfers between devices, on_device(): sums = lax.all_to_all(sums, 'head', 0, 0)  24.1 us
    ppermute x14, waiting for transfers between devices, exchange(): return lax.ppermute(block, 'frame', route(*EXCHANGES[which], frames))  7.86 us
    pallas_call x1, Pallas kernels, on_device(): pl.pallas_call(functools.partial(attend_kernel, frames), out_shape=[flat,...  4.9 us
    unnamed x11, local copies, waits for them, and re-layouts  4.57 us
    all_to_all x1, waiting for transfers between devices, on_device(): sums = lax.all_to_all(sums, 'head', 0, 0)  4.56 us
  transfers between devices with their start and end apart: 15, of which 5 were waited for; matrix products, arithmetic and copies ran while one was open for 1% of the time, Pallas kernels for 5%

profile of v4, /device:TPU:2, one launch (start us, length us, event | category | flops | bytes accessed | tf_op | source)
XLA Modules:
  0.0 114.7 jit_solution(3180925280180171558)
XLA Ops:
  0.6 0.9 copy-done.3
  1.6 0.9 copy-done.4
  2.5 0.9 square_sums.1
  3.4 24.1 %all-to-all-start = ((f32[16,8,128]{2,1,0:T(8,128)}), f32[16,8,128]{2,1,0:T(8,128)S(1)}, u32[]{:S(2)}, u32[]{:S(2)}) async-start(f32[16,8,128]{2,1,0:T(8,128)} %get-tuple-element.36), calls=%async_computation | async-start | bytes 131072 | tf_op jit(solution)/shard_map/all_to_all | solution.py:220
  27.5 0.8 copy.10.kept_ref
  28.3 0.9 copy-done.2
  29.3 1.1 early.1
  30.4 7.9 %collective-permute-start.6 = (bf16[128,256]{1,0:T(8,128)(2,1)S(1)}, bf16[128,256]{1,0:T(8,128)(2,1)S(1)}, u32[]{:S(2)}, u32[]{:S(2)}) collective-permute-start(bf16[128,256]{1,0:T(8,128)(2,1)S(1)} %get-tuple-element.50), channel_id=1, source_target_pairs={{64,128},{128,64},{80,144},{144,80},{96,160},{160,96},{112,176},{1... | collective-permute-start | bytes 196616 | tf_op jit(solution)/shard_map/ppermute | solution.py:198
  38.3 1.9 %collective-permute-start.7 = (bf16[128,256]{1,0:T(8,128)(2,1)S(1)}, bf16[128,256]{1,0:T(8,128)(2,1)S(1)}, u32[]{:S(2)}, u32[]{:S(2)}) collective-permute-start(bf16[128,256]{1,0:T(8,128)(2,1)S(1)} %get-tuple-element.51), channel_id=1, source_target_pairs={{0,64},{64,0},{16,80},{80,16},{32,96},{96,32},{48,112},{112,48},{1... | collective-permute-start | bytes 196616 | tf_op jit(solution)/shard_map/ppermute | solution.py:198
  40.2 4.6 %all-to-all-done.sums_ref = f32[16,8,128]{2,1,0:T(8,128)S(1)} async-done(((f32[16,8,128]{2,1,0:T(8,128)}), f32[16,8,128]{2,1,0:T(8,128)S(1)}, u32[]{:S(2)}, u32[]{:S(2)}) %all-to-all-start) | async-done | bytes 65568 | tf_op jit(solution)/shard_map/all_to_all | solution.py:220
  44.8 1.3 %normalize.1 = (bf16[512,256]{1,0:T(8,128)(2,1)S(1)}, bf16[512,256]{1,0:T(8,128)(2,1)S(1)}, bf16[128,256]{1,0:T(8,128)(2,1)S(1)}, bf16[128,512]{1,0:T(8,128)(2,1...) custom-call(s32[1]{0:T(128)} %bitcast.frame_ref, ...), custom_call_target="tpu_custom_call" | custom-call | tf_op jit(solution)/shard_map/normalize/pallas_call | solution.py:230
  46.1 8.4 %collective-permute-start = (bf16[128,256]{1,0:T(8,128)(2,1)S(1)}, bf16[128,256]{1,0:T(8,128)(2,1)S(1)}, u32[]{:S(2)}, u32[]{:S(2)}) collective-permute-start(bf16[128,256]{1,0:T(8,128)(2,1)S(1)} %get-tuple-element.44), channel_id=1, source_target_pairs={{64,128},{128,64},{80,144},{144,80},{96,160},{160,96},{112,176},{1... | collective-permute-start | bytes 196616 | tf_op jit(solution)/shard_map/ppermute | solution.py:198
  54.5 5.0 %collective-permute-start.1 = (bf16[128,512]{1,0:T(8,128)(2,1)S(1)}, bf16[128,512]{1,0:T(8,128)(2,1)S(1)}, u32[]{:S(2)}, u32[]{:S(2)}) collective-permute-start(bf16[128,512]{1,0:T(8,128)(2,1)S(1)} %get-tuple-element.45), channel_id=1, source_target_pairs={{32,64},{64,32},{48,80},{80,48},{96,128},{128,96},{112,144},{144,1... | collective-permute-start | bytes 393224 | tf_op jit(solution)/shard_map/ppermute | solution.py:198
  59.5 5.8 %collective-permute-start.2 = (bf16[128,512]{1,0:T(8,128)(2,1)S(1)}, bf16[128,512]{1,0:T(8,128)(2,1)S(1)}, u32[]{:S(2)}, u32[]{:S(2)}) collective-permute-start(bf16[128,512]{1,0:T(8,128)(2,1)S(1)} %get-tuple-element.46), channel_id=1, source_target_pairs={{16,32},{32,16},{48,64},{64,48},{80,96},{96,80},{112,128},{128,112... | collective-permute-start | bytes 393224 | tf_op jit(solution)/shard_map/ppermute | solution.py:198
  65.3 1.9 %collective-permute-start.4 = (bf16[128,512]{1,0:T(8,128)(2,1)S(1)}, bf16[128,512]{1,0:T(8,128)(2,1)S(1)}, u32[]{:S(2)}, u32[]{:S(2)}) collective-permute-start(bf16[128,512]{1,0:T(8,128)(2,1)S(1)} %get-tuple-element.48), channel_id=1, source_target_pairs={{0,32},{32,0},{16,48},{48,16},{64,96},{96,64},{80,112},{112,80},{1... | collective-permute-start | bytes 393224 | tf_op jit(solution)/shard_map/ppermute | solution.py:198
  67.2 1.9 %collective-permute-start.5 = (bf16[128,512]{1,0:T(8,128)(2,1)S(1)}, bf16[128,512]{1,0:T(8,128)(2,1)S(1)}, u32[]{:S(2)}, u32[]{:S(2)}) collective-permute-start(bf16[128,512]{1,0:T(8,128)(2,1)S(1)} %get-tuple-element.49), channel_id=1, source_target_pairs={{0,16},{16,0},{32,48},{48,32},{64,80},{80,64},{96,112},{112,96},{1... | collective-permute-start | bytes 393224 | tf_op jit(solution)/shard_map/ppermute | solution.py:198
  69.1 1.9 %collective-permute-start.3 = (bf16[128,256]{1,0:T(8,128)(2,1)S(1)}, bf16[128,256]{1,0:T(8,128)(2,1)S(1)}, u32[]{:S(2)}, u32[]{:S(2)}) collective-permute-start(bf16[128,256]{1,0:T(8,128)(2,1)S(1)} %get-tuple-element.47), channel_id=1, source_target_pairs={{0,64},{64,0},{16,80},{80,16},{32,96},{96,32},{48,112},{112,48},{1... | collective-permute-start | bytes 196616 | tf_op jit(solution)/shard_map/ppermute | solution.py:198
  71.1 0.9 copy-done
  72.0 0.7 own_scores.1
  72.7 3.7 %collective-permute-done.3.refs_3_ = bf16[128,256]{1,0:T(8,128)(2,1)S(1)} collective-permute-done((bf16[128,256]{1,0:T(8,128)(2,1)S(1)}, bf16[128,256]{1,0:T(8,128)(2,1)S(1)}, u32[]{:S(2)}, u32[]{:S(2)}) %collective-permute-start.3) | collective-permute-done | bytes 65568 | tf_op jit(solution)/shard_map/ppermute | solution.py:198
  76.5 4.9 %attend.1 = (bf16[512,256]{1,0:T(8,128)(2,1)}, bf16[2,512,512]{2,1,0:T(8,128)(2,1)S(1)}, bf16[2,512,512]{2,1,0:T(8,128)(2,1)S(1)}, bf16[2,512,768]{2,1,0:T(8,128...) custom-call(s32[1]{0:T(128)} %bitcast.frame_ref, ...), custom_call_target="tpu_custom_call" | custom-call | tf_op jit(solution)/shard_map/attend/pallas_call | solution.py:250
  81.4 7.7 %collective-permute-start.8 = (bf16[128,512]{1,0:T(8,128)(2,1)S(1)}, bf16[128,512]{1,0:T(8,128)(2,1)S(1)}, u32[]{:S(2)}, u32[]{:S(2)}) collective-permute-start(bf16[128,512]{1,0:T(8,128)(2,1)S(1)} %get-tuple-element.60), channel_id=1, source_target_pairs={{64,128},{128,64},{80,144},{144,80},{96,160},{160,96},{112,176},{1... | collective-permute-start | bytes 393224 | tf_op jit(solution)/shard_map/ppermute | solution.py:198
  89.1 6.2 %collective-permute-start.9 = (bf16[128,512]{1,0:T(8,128)(2,1)S(1)}, bf16[128,512]{1,0:T(8,128)(2,1)S(1)}, u32[]{:S(2)}, u32[]{:S(2)}) collective-permute-start(bf16[128,512]{1,0:T(8,128)(2,1)S(1)} %get-tuple-element.61), channel_id=1, source_target_pairs={{32,64},{64,32},{48,80},{80,48},{96,128},{128,96},{112,144},{144,1... | collective-permute-start | bytes 393224 | tf_op jit(solution)/shard_map/ppermute | solution.py:198
  95.2 5.2 %collective-permute-start.10 = (bf16[128,512]{1,0:T(8,128)(2,1)S(1)}, bf16[128,512]{1,0:T(8,128)(2,1)S(1)}, u32[]{:S(2)}, u32[]{:S(2)}) collective-permute-start(bf16[128,512]{1,0:T(8,128)(2,1)S(1)} %get-tuple-element.62), channel_id=1, source_target_pairs={{16,32},{32,16},{48,64},{64,48},{80,96},{96,80},{112,128},{128,112... | collective-permute-start | bytes 393224 | tf_op jit(solution)/shard_map/ppermute | solution.py:198
  100.4 1.9 %collective-permute-start.11 = (bf16[128,512]{1,0:T(8,128)(2,1)S(1)}, bf16[128,512]{1,0:T(8,128)(2,1)S(1)}, u32[]{:S(2)}, u32[]{:S(2)}) collective-permute-start(bf16[128,512]{1,0:T(8,128)(2,1)S(1)} %get-tuple-element.63), channel_id=1, source_target_pairs={{0,64},{64,0},{16,80},{80,16},{32,96},{96,32},{48,112},{112,48},{1... | collective-permute-start | bytes 393224 | tf_op jit(solution)/shard_map/ppermute | solution.py:198
  102.4 1.9 %collective-permute-start.12 = (bf16[128,512]{1,0:T(8,128)(2,1)S(1)}, bf16[128,512]{1,0:T(8,128)(2,1)S(1)}, u32[]{:S(2)}, u32[]{:S(2)}) collective-permute-start(bf16[128,512]{1,0:T(8,128)(2,1)S(1)} %get-tuple-element.64), channel_id=1, source_target_pairs={{0,32},{32,0},{16,48},{48,16},{64,96},{96,64},{80,112},{112,80},{1... | collective-permute-start | bytes 393224 | tf_op jit(solution)/shard_map/ppermute | solution.py:198
  104.3 1.9 %collective-permute-start.13 = (bf16[128,512]{1,0:T(8,128)(2,1)S(1)}, bf16[128,512]{1,0:T(8,128)(2,1)S(1)}, u32[]{:S(2)}, u32[]{:S(2)}) collective-permute-start(bf16[128,512]{1,0:T(8,128)(2,1)S(1)} %get-tuple-element.65), channel_id=1, source_target_pairs={{0,16},{16,0},{32,48},{48,32},{64,80},{80,64},{96,112},{112,96},{1... | collective-permute-start | bytes 393224 | tf_op jit(solution)/shard_map/ppermute | solution.py:198
  106.2 2.1 %rest.1 = (bf16[512,256]{1,0:T(8,128)(2,1)}, f32[512,256]{1,0:T(8,128)S(1)}, f32[512,256]{1,0:T(8,128)S(1)}) custom-call(bf16[2,512,512]{2,1,0:T(8,128)(2,1)S(1)} %get-tuple-element.53.p_own, bf16[2,512,512]{2,1,0:T(8,128)(2,1)S(1)} %get-tuple-element.54.s_own, bf16[2,512,768]{2,1,0:T(8,128)(2,1)S(1)} %get-tuple-element.55.s_far, ...), custom_call_target="tpu_custom_call" | custom-call | flops 536870912 | bytes 8388608 | tf_op jit(solution)/shard_map/rest/pallas_call | solution.py:269
  108.4 2.0 %collective-permute-done.10.refs_2_ = bf16[128,512]{1,0:T(8,128)(2,1)S(1)} collective-permute-done((bf16[128,512]{1,0:T(8,128)(2,1)S(1)}, bf16[128,512]{1,0:T(8,128)(2,1)S(1)}, u32[]{:S(2)}, u32[]{:S(2)}) %collective-permute-start.10) | collective-permute-done | bytes 131104 | tf_op jit(solution)/shard_map/ppermute | solution.py:198
  110.3 1.3 %collective-permute-done.11.refs_3_ = bf16[128,512]{1,0:T(8,128)(2,1)S(1)} collective-permute-done((bf16[128,512]{1,0:T(8,128)(2,1)S(1)}, bf16[128,512]{1,0:T(8,128)(2,1)S(1)}, u32[]{:S(2)}, u32[]{:S(2)}) %collective-permute-start.11) | collective-permute-done | bytes 131104 | tf_op jit(solution)/shard_map/ppermute | solution.py:198
  111.6 0.9 collective-permute-done.12.refs_4_
  112.5 2.2 %collect.1 = (bf16[512,256]{1,0:T(8,128)(2,1)}, bf16[512,256]{1,0:T(8,128)(2,1)}) custom-call(s32[1]{0:T(128)} %bitcast.frame_ref, s32[64,6]{1,0:T(8,128)S(1)} %copy.10.kept_ref, f32[512,256]{1,0:T(8,128)S(1)} %get-tuple-element.58.gk_ref, f32[512,256]{1,0:T(8,128)S(1)} %get-tuple-element.59.gv_ref, bf16[128,512]{1,0:T(8,128)(2,1)S(1)} %collective-permute-done.8.refs_0_, ...), custom_call_target="tpu_custom_call" | custom-call | tf_op jit(solution)/shard_map/collect/pallas_call | solution.py:279
  (16 shorter events, 0.0 us)
Async XLA Ops:
  0.6 1.0 copy-start.3
  1.6 0.9 copy-start.4
  2.5 73.9 %copy-start.1 = (bf16[512,256]{1,0:T(8,128)(2,1)S(1)}, bf16[512,256]{1,0:T(8,128)(2,1)}, u32[]{:S(2)}) copy-start(bf16[512,256]{1,0:T(8,128)(2,1)} %d_ref.5) | copy-start | bytes 786436
  3.4 41.3 %all-to-all-start = ((f32[16,8,128]{2,1,0:T(8,128)}), f32[16,8,128]{2,1,0:T(8,128)S(1)}, u32[]{:S(2)}, u32[]{:S(2)}) async-start(f32[16,8,128]{2,1,0:T(8,128)} %get-tuple-element.36), calls=%async_computation | async-start | bytes 131072 | tf_op jit(solution)/shard_map/all_to_all | solution.py:220
  28.3 0.9 copy-start.2
  30.4 34.9 %collective-permute-start.6 = (bf16[128,256]{1,0:T(8,128)(2,1)S(1)}, bf16[128,256]{1,0:T(8,128)(2,1)S(1)}, u32[]{:S(2)}, u32[]{:S(2)}) collective-permute-start(bf16[128,256]{1,0:T(8,128)(2,1)S(1)} %get-tuple-element.50), channel_id=1, source_target_pairs={{64,128},{128,64},{80,144},{144,80},{96,160},{160,96},{112,176},{1... | collective-permute-start | bytes 196616 | tf_op jit(solution)/shard_map/ppermute | solution.py:198
  38.3 28.9 %collective-permute-start.7 = (bf16[128,256]{1,0:T(8,128)(2,1)S(1)}, bf16[128,256]{1,0:T(8,128)(2,1)S(1)}, u32[]{:S(2)}, u32[]{:S(2)}) collective-permute-start(bf16[128,256]{1,0:T(8,128)(2,1)S(1)} %get-tuple-element.51), channel_id=1, source_target_pairs={{0,64},{64,0},{16,80},{80,16},{32,96},{96,32},{48,112},{112,48},{1... | collective-permute-start | bytes 196616 | tf_op jit(solution)/shard_map/ppermute | solution.py:198
  46.1 23.0 %collective-permute-start = (bf16[128,256]{1,0:T(8,128)(2,1)S(1)}, bf16[128,256]{1,0:T(8,128)(2,1)S(1)}, u32[]{:S(2)}, u32[]{:S(2)}) collective-permute-start(bf16[128,256]{1,0:T(8,128)(2,1)S(1)} %get-tuple-element.44), channel_id=1, source_target_pairs={{64,128},{128,64},{80,144},{144,80},{96,160},{160,96},{112,176},{1... | collective-permute-start | bytes 196616 | tf_op jit(solution)/shard_map/ppermute | solution.py:198
  54.5 22.0 %collective-permute-start.1 = (bf16[128,512]{1,0:T(8,128)(2,1)S(1)}, bf16[128,512]{1,0:T(8,128)(2,1)S(1)}, u32[]{:S(2)}, u32[]{:S(2)}) collective-permute-start(bf16[128,512]{1,0:T(8,128)(2,1)S(1)} %get-tuple-element.45), channel_id=1, source_target_pairs={{32,64},{64,32},{48,80},{80,48},{96,128},{128,96},{112,144},{144,1... | collective-permute-start | bytes 393224 | tf_op jit(solution)/shard_map/ppermute | solution.py:198
  59.5 17.0 %collective-permute-start.2 = (bf16[128,512]{1,0:T(8,128)(2,1)S(1)}, bf16[128,512]{1,0:T(8,128)(2,1)S(1)}, u32[]{:S(2)}, u32[]{:S(2)}) collective-permute-start(bf16[128,512]{1,0:T(8,128)(2,1)S(1)} %get-tuple-element.46), channel_id=1, source_target_pairs={{16,32},{32,16},{48,64},{64,48},{80,96},{96,80},{112,128},{128,112... | collective-permute-start | bytes 393224 | tf_op jit(solution)/shard_map/ppermute | solution.py:198
  65.3 11.2 %collective-permute-start.4 = (bf16[128,512]{1,0:T(8,128)(2,1)S(1)}, bf16[128,512]{1,0:T(8,128)(2,1)S(1)}, u32[]{:S(2)}, u32[]{:S(2)}) collective-permute-start(bf16[128,512]{1,0:T(8,128)(2,1)S(1)} %get-tuple-element.48), channel_id=1, source_target_pairs={{0,32},{32,0},{16,48},{48,16},{64,96},{96,64},{80,112},{112,80},{1... | collective-permute-start | bytes 393224 | tf_op jit(solution)/shard_map/ppermute | solution.py:198
  67.2 9.2 %collective-permute-start.5 = (bf16[128,512]{1,0:T(8,128)(2,1)S(1)}, bf16[128,512]{1,0:T(8,128)(2,1)S(1)}, u32[]{:S(2)}, u32[]{:S(2)}) collective-permute-start(bf16[128,512]{1,0:T(8,128)(2,1)S(1)} %get-tuple-element.49), channel_id=1, source_target_pairs={{0,16},{16,0},{32,48},{48,32},{64,80},{80,64},{96,112},{112,96},{1... | collective-permute-start | bytes 393224 | tf_op jit(solution)/shard_map/ppermute | solution.py:198
  69.1 7.3 %collective-permute-start.3 = (bf16[128,256]{1,0:T(8,128)(2,1)S(1)}, bf16[128,256]{1,0:T(8,128)(2,1)S(1)}, u32[]{:S(2)}, u32[]{:S(2)}) collective-permute-start(bf16[128,256]{1,0:T(8,128)(2,1)S(1)} %get-tuple-element.47), channel_id=1, source_target_pairs={{0,64},{64,0},{16,80},{80,16},{32,96},{96,32},{48,112},{112,48},{1... | collective-permute-start | bytes 196616 | tf_op jit(solution)/shard_map/ppermute | solution.py:198
  71.1 1.0 copy-start
  81.4 22.9 %collective-permute-start.8 = (bf16[128,512]{1,0:T(8,128)(2,1)S(1)}, bf16[128,512]{1,0:T(8,128)(2,1)S(1)}, u32[]{:S(2)}, u32[]{:S(2)}) collective-permute-start(bf16[128,512]{1,0:T(8,128)(2,1)S(1)} %get-tuple-element.60), channel_id=1, source_target_pairs={{64,128},{128,64},{80,144},{144,80},{96,160},{160,96},{112,176},{1... | collective-permute-start | bytes 393224 | tf_op jit(solution)/shard_map/ppermute | solution.py:198
  89.1 19.3 %collective-permute-start.9 = (bf16[128,512]{1,0:T(8,128)(2,1)S(1)}, bf16[128,512]{1,0:T(8,128)(2,1)S(1)}, u32[]{:S(2)}, u32[]{:S(2)}) collective-permute-start(bf16[128,512]{1,0:T(8,128)(2,1)S(1)} %get-tuple-element.61), channel_id=1, source_target_pairs={{32,64},{64,32},{48,80},{80,48},{96,128},{128,96},{112,144},{144,1... | collective-permute-start | bytes 393224 | tf_op jit(solution)/shard_map/ppermute | solution.py:198
  95.2 15.1 %collective-permute-start.10 = (bf16[128,512]{1,0:T(8,128)(2,1)S(1)}, bf16[128,512]{1,0:T(8,128)(2,1)S(1)}, u32[]{:S(2)}, u32[]{:S(2)}) collective-permute-start(bf16[128,512]{1,0:T(8,128)(2,1)S(1)} %get-tuple-element.62), channel_id=1, source_target_pairs={{16,32},{32,16},{48,64},{64,48},{80,96},{96,80},{112,128},{128,112... | collective-permute-start | bytes 393224 | tf_op jit(solution)/shard_map/ppermute | solution.py:198
  100.4 11.1 %collective-permute-start.11 = (bf16[128,512]{1,0:T(8,128)(2,1)S(1)}, bf16[128,512]{1,0:T(8,128)(2,1)S(1)}, u32[]{:S(2)}, u32[]{:S(2)}) collective-permute-start(bf16[128,512]{1,0:T(8,128)(2,1)S(1)} %get-tuple-element.63), channel_id=1, source_target_pairs={{0,64},{64,0},{16,80},{80,16},{32,96},{96,32},{48,112},{112,48},{1... | collective-permute-start | bytes 393224 | tf_op jit(solution)/shard_map/ppermute | solution.py:198
  102.4 10.1 %collective-permute-start.12 = (bf16[128,512]{1,0:T(8,128)(2,1)S(1)}, bf16[128,512]{1,0:T(8,128)(2,1)S(1)}, u32[]{:S(2)}, u32[]{:S(2)}) collective-permute-start(bf16[128,512]{1,0:T(8,128)(2,1)S(1)} %get-tuple-element.64), channel_id=1, source_target_pairs={{0,32},{32,0},{16,48},{48,16},{64,96},{96,64},{80,112},{112,80},{1... | collective-permute-start | bytes 393224 | tf_op jit(solution)/shard_map/ppermute | solution.py:198
  104.3 8.2 %collective-permute-start.13 = (bf16[128,512]{1,0:T(8,128)(2,1)S(1)}, bf16[128,512]{1,0:T(8,128)(2,1)S(1)}, u32[]{:S(2)}, u32[]{:S(2)}) collective-permute-start(bf16[128,512]{1,0:T(8,128)(2,1)S(1)} %get-tuple-element.65), channel_id=1, source_target_pairs={{0,16},{16,0},{32,48},{48,32},{64,80},{80,64},{96,112},{112,96},{1... | collective-permute-start | bytes 393224 | tf_op jit(solution)/shard_map/ppermute | solution.py:198

commit v5 on v4

v5 whole, which is shorter than its diff:
```python
import functools
import math

import jax
import jax.numpy as jnp
from jax import lax
from jax.experimental import pallas as pl
from jax.experimental.pallas import tpu as pltpu
from jax.sharding import PartitionSpec as P

HD = 128
BS = 128
EXCHANGES = ((4, True), (2, True), (1, True), (4, False), (2, False), (1, False))

masked_score = -1e30
norm_eps = 1e-06

VMEM = pl.BlockSpec(memory_space=pltpu.VMEM)
ANY = pl.BlockSpec(memory_space=pl.ANY)
SMEM = pl.BlockSpec(memory_space=pltpu.SMEM)


def params(mib):
    return pltpu.CompilerParams(vmem_limit_bytes=mib << 20)


def route(distance, shifted, frames):
    pairs = []
    for low in range(frames - distance):
        if ((low // distance) % 2 == 1) == shifted:
            pairs += [(low, low + distance), (low + distance, low)]
    return pairs


def partner(frame, distance, shifted):
    up = ((frame // distance) % 2 == 1) == shifted
    level = int(math.log2(distance))
    offset = jnp.where(up, distance, -distance)
    slot = jnp.where(up, 2 * level + 1, 2 * level)
    return offset, slot


def block_start(kept_ref, frame, frames, distance, shifted):
    offset, slot = partner(frame, distance, shifted)
    other = jnp.clip(frame + offset, 0, frames - 1)
    return pl.multiple_of(kept_ref[slot, other] * BS, BS)


def is_live(frame, frames, distance, shifted):
    offset, _ = partner(frame, distance, shifted)
    other = frame + offset
    return jnp.logical_and(other >= 0, other < frames)


def pack_kernel(frames, frame_ref, kept_ref, k_hbm, v_hbm, *refs):
    block_refs, sems = refs[:-1], refs[-1]
    width = k_hbm.shape[1]
    copies = []
    for index, (exchange, block) in enumerate(zip(EXCHANGES, block_refs)):
        rows = pl.ds(block_start(kept_ref, frame_ref[0], frames, *exchange), BS)
        copies.append(pltpu.make_async_copy(k_hbm.at[rows, :], block.at[:, pl.ds(0, width)], sems.at[0, index]))
        copies.append(pltpu.make_async_copy(v_hbm.at[rows, :], block.at[:, pl.ds(width, width)], sems.at[1, index]))
    for copy in copies:
        copy.start()
    for copy in copies:
        copy.wait()


def square_sums(ref, start, width):
    total = jnp.zeros((128, 128), jnp.float32)
    for column in range(0, width, 128):
        part = ref[start : start + 128, column : column + 128].astype(jnp.float32)
        total += part * part
    return jnp.sum(total.T, axis=0, keepdims=True)


def own_sums_kernel(q_ref, k_ref, sums_ref):
    rows = [square_sums(ref, start, ref.shape[1]) for ref in (q_ref, k_ref) for start in range(0, ref.shape[0], 128)]
    sums_ref[...] = jnp.concatenate(rows, axis=0)


def all_sums_kernel(own_ref, *refs):
    far_refs, sums_ref = refs[:-1], refs[-1]
    rows = [own_ref[...]] + [square_sums(far, 0, far.shape[1] // 2) for far in far_refs]
    packed = jnp.concatenate(rows, axis=0)
    pad = sums_ref.shape[1] - packed.shape[0]
    packed = jnp.concatenate([packed, jnp.zeros((pad, 128), jnp.float32)], axis=0)
    for copy in range(sums_ref.shape[0]):
        sums_ref[copy] = packed


def by_row(scale):
    return jnp.broadcast_to(scale, (128, 128)).T


def scaled(block, scale):
    return (block.astype(jnp.float32) * scale).astype(jnp.bfloat16)


def norm_kernel(width_all, sums_ref, q_ref, k_ref, *refs):
    far_refs, (qn_ref, kn_ref, far_ref) = refs[:6], refs[6:]
    width = q_ref.shape[1]
    total = sums_ref[0]
    for part in range(1, sums_ref.shape[0]):
        total += sums_ref[part]
    scale = lax.rsqrt(total / width_all + norm_eps)
    pieces = [(ref, start, out, start) for ref, out in ((q_ref, qn_ref), (k_ref, kn_ref)) for start in range(0, ref.shape[0], 128)]
    pieces += [(far, 0, far_ref, slot * BS) for slot, far in enumerate(far_refs)]
    for row, (ref, start, out, place) in enumerate(pieces):
        factor = by_row(scale[row : row + 1, :])
        for column in range(0, width, 128):
            part = ref[start : start + 128, column : column + 128]
            out[place : place + 128, column : column + 128] = scaled(part, factor)


CONTRACT_LAST = (((1,), (1,)), ((), ()))
CONTRACT_FIRST = (((0,), (0,)), ((), ()))
FACTOR = 1.0 / math.sqrt(HD)
EXPONENT = FACTOR * math.log2(math.e)
CHUNK = 256


def dot(left, right, dims=(((1,), (0,)), ((), ()))):
    return lax.dot_general(left, right, dims, preferred_element_type=jnp.float32)


def attend_kernel(frames, frame_ref, q_ref, k_ref, v_ref, d_ref, k_far, *refs):
    far_refs = refs[:6]
    att_ref, p_own, s_own, s_far = refs[6:10]
    back_refs = refs[10:16]
    v_far, p_far = refs[16:]
    frame = frame_ref[0]
    tokens, width = q_ref.shape
    f32 = jnp.float32
    column = lax.broadcasted_iota(jnp.int32, (1, 6 * BS), 1)
    allowed = column < 0
    for slot, (distance, shifted) in enumerate(EXCHANGES):
        v_far[slot * BS : (slot + 1) * BS] = far_refs[slot][:, width:]
        inside = jnp.logical_and(column >= slot * BS, column < (slot + 1) * BS)
        live = is_live(frame, frames, distance, shifted)
        allowed = jnp.logical_or(allowed, jnp.logical_and(inside, live))
    for index in range(width // HD):
        head = slice(index * HD, (index + 1) * HD)
        keys, vals = k_far[:, head], v_far[:, head]
        for first in range(0, tokens, CHUNK):
            rows = slice(first, first + CHUNK)
            grads = d_ref[rows, head]
            own = dot(q_ref[rows, head], k_ref[:, head], CONTRACT_LAST)
            far = jnp.where(allowed, dot(q_ref[rows, head], keys, CONTRACT_LAST), masked_score)
            top = jnp.maximum(jnp.max(own, axis=1, keepdims=True), jnp.max(far, axis=1, keepdims=True))
            own = jnp.exp2((own - top) * EXPONENT)
            far = jnp.exp2((far - top) * EXPONENT)
            share = 1.0 / (jnp.sum(own, axis=1, keepdims=True) + jnp.sum(far, axis=1, keepdims=True))
            own_low = (own * share).astype(jnp.bfloat16)
            far_low = (far * share).astype(jnp.bfloat16)
            p_own[index, rows, :] = own_low
            p_far[rows, :] = far_low
            attended = (dot(own_low, v_ref[:, head]) + dot(far_low, vals)).astype(jnp.bfloat16)
            att_ref[rows, head] = attended
            inner = jnp.sum(grads.astype(f32) * attended.astype(f32), axis=1, keepdims=True)
            s_own[index, rows, :] = (own * ((dot(grads, v_ref[:, head], CONTRACT_LAST) - inner) * share)).astype(jnp.bfloat16)
            s_far[index, rows, :] = (far * ((dot(grads, vals, CONTRACT_LAST) - inner) * share)).astype(jnp.bfloat16)
        grad_k = dot(s_far[index], q_ref[:, head], CONTRACT_FIRST) * FACTOR
        grad_v = dot(p_far[...], d_ref[:, head], CONTRACT_FIRST)
        for slot, back in enumerate(back_refs):
            rows = slice(slot * BS, (slot + 1) * BS)
            back[:, index * HD : (index + 1) * HD] = grad_k[rows].astype(jnp.bfloat16)
            back[:, width + index * HD : width + (index + 1) * HD] = grad_v[rows].astype(jnp.bfloat16)


def rest_kernel(p_own, s_own, s_far, k_far, q_ref, k_ref, d_ref, gq_ref, gk_ref, gv_ref):
    for index in range(q_ref.shape[1] // HD):
        head = slice(index * HD, (index + 1) * HD)
        grad_q = dot(s_own[index], k_ref[:, head]) + dot(s_far[index], k_far[:, head])
        gq_ref[:, head] = (grad_q * FACTOR).astype(jnp.bfloat16)
        gk_ref[:, head] = dot(s_own[index], q_ref[:, head], CONTRACT_FIRST) * FACTOR
        gv_ref[:, head] = dot(p_own[index], d_ref[:, head], CONTRACT_FIRST)


def collect_kernel(frames, frame_ref, kept_ref, gk_ref, gv_ref, *refs):
    back_refs, (outk_ref, outv_ref, acc_k, acc_v) = refs[:6], refs[6:]
    frame = frame_ref[0]
    width = gk_ref.shape[1]
    acc_k[...] = gk_ref[...]
    acc_v[...] = gv_ref[...]
    for (distance, shifted), back in zip(EXCHANGES, back_refs):
        rows = pl.ds(block_start(kept_ref, frame, frames, distance, shifted), BS)

        @pl.when(is_live(frame, frames, distance, shifted))
        def _():
            acc_k[rows, :] += back[:, :width].astype(jnp.float32)
            acc_v[rows, :] += back[:, width:].astype(jnp.float32)

    outk_ref[...] = acc_k[...].astype(jnp.bfloat16)
    outv_ref[...] = acc_v[...].astype(jnp.bfloat16)


def exchange(block, frames, which):
    return lax.ppermute(block, "frame", route(*EXCHANGES[which], frames))


def on_device(queries, keys, values, cotangent, kept):
    frames = lax.axis_size("frame")
    heads = lax.axis_size("head")
    tokens, width = queries.shape
    heads_dev = width // HD
    frame = lax.axis_index("frame").reshape(1)
    kept = kept.T
    flat = jax.ShapeDtypeStruct((tokens, width), jnp.bfloat16)
    wide = jax.ShapeDtypeStruct((tokens, width), jnp.float32)
    block = jax.ShapeDtypeStruct((BS, 2 * width), jnp.bfloat16)
    sent = pl.pallas_call(
        functools.partial(pack_kernel, frames),
        out_shape=[block] * 6,
        in_specs=[SMEM] * 2 + [ANY] * 2,
        out_specs=[ANY] * 6,
        scratch_shapes=[pltpu.SemaphoreType.DMA((2, 6))],
        compiler_params=params(60),
        name="pack",
    )(frame, kept, keys, values)
    far = [exchange(part, frames, which) for which, part in enumerate(sent)]
    own_rows = 2 * tokens // 128
    own_sums = pl.pallas_call(
        own_sums_kernel,
        out_shape=jax.ShapeDtypeStruct((own_rows, 128), jnp.float32),
        in_specs=[VMEM] * 2,
        out_specs=VMEM,
        compiler_params=params(6),
        cost_estimate=pl.CostEstimate(flops=4 * tokens * width, bytes_accessed=4 * tokens * width, transcendentals=0),
        name="own_sums",
    )(queries, keys)
    sums = pl.pallas_call(
        all_sums_kernel,
        out_shape=jax.ShapeDtypeStruct((heads, own_rows + 8, 128), jnp.float32),
        in_specs=[VMEM] * 7,
        out_specs=VMEM,
        compiler_params=params(6),
        name="all_sums",
    )(own_sums, *far)
    sums = lax.all_to_all(sums, "head", 0, 0)
    far_shape = jax.ShapeDtypeStruct((6 * BS, width), jnp.bfloat16)
    q_norm, k_norm, far_k = pl.pallas_call(
        functools.partial(norm_kernel, width * heads),
        out_shape=[flat, flat, far_shape],
        in_specs=[VMEM] * 9,
        out_specs=[VMEM] * 3,
        compiler_params=params(8),
        name="normalize",
    )(sums, queries, keys, *far)
    own_shape = (heads_dev, tokens, tokens)
    own_flops = 2 * tokens * tokens * width
    attended, own_p, own_s, far_s, *back = pl.pallas_call(
        functools.partial(attend_kernel, frames),
        out_shape=[
            flat,
            jax.ShapeDtypeStruct(own_shape, jnp.bfloat16),
            jax.ShapeDtypeStruct(own_shape, jnp.bfloat16),
            jax.ShapeDtypeStruct((heads_dev, tokens, 6 * BS), jnp.bfloat16),
        ]
        + [block] * 6,
        in_specs=[SMEM] + [VMEM] * 11,
        out_specs=[VMEM] * 10,
        scratch_shapes=[
            pltpu.VMEM((6 * BS, width), jnp.bfloat16),
            pltpu.VMEM((tokens, 6 * BS), jnp.bfloat16),
        ],
        compiler_params=params(20),
        name="attend",
    )(frame, q_norm, k_norm, values, cotangent, far_k, *far)
    grad_q, own_k, own_v = pl.pallas_call(
        rest_kernel,
        out_shape=[flat, wide, wide],
        in_specs=[VMEM] * 7,
        out_specs=[VMEM] * 3,
        compiler_params=params(8),
        cost_estimate=pl.CostEstimate(flops=4 * own_flops, bytes_accessed=8 << 20, transcendentals=0),
        name="rest",
    )(own_p, own_s, far_s, far_k, q_norm, k_norm, cotangent)
    back = [exchange(part, frames, which) for which, part in enumerate(back)]
    grad_k, grad_v = pl.pallas_call(
        functools.partial(collect_kernel, frames),
        out_shape=[flat, flat],
        in_specs=[SMEM] * 2 + [VMEM] * 8,
        out_specs=[VMEM] * 2,
        scratch_shapes=[pltpu.VMEM((tokens, width), jnp.float32)] * 2,
        compiler_params=params(8),
        name="collect",
    )(frame, kept, own_k, own_v, *back)
    return attended, grad_q, grad_k, grad_v


def solution(mesh):
    spec = P("frame", "head")
    return jax.shard_map(
        on_device,
        mesh=mesh,
        in_specs=(spec, spec, spec, spec, P()),
        out_specs=(spec, spec, spec, spec),
        check_vma=False,
    )
```

time: 115 us -> 135 us (1.17)
  the two profiles are of different devices: /device:TPU:2 before, /device:TPU:4 now
where the time goes in v5:
time: 135 us
  starting transfers between devices  53.9 us (40%)
  Pallas kernels  36.2 us (27%)
  blocking collectives  35.3 us (26%)
  waiting for transfers between devices  6.88 us (5%)
  local copies, waits for them, and re-layouts  1.92 us (1%)
    ppermute x12, starting transfers between devices, exchange(): return lax.ppermute(block, 'frame', route(*EXCHANGES[which], frames))  53.9 us
    all_to_all x1, blocking collectives, on_device(): sums = lax.all_to_all(sums, 'head', 0, 0)  35.3 us
    pallas_call x1, Pallas kernels, on_device(): pl.pallas_call(functools.partial(pack_kernel, frames), out_shape=[block]...  25.9 us
    ppermute x12, waiting for transfers between devices, exchange(): return lax.ppermute(block, 'frame', route(*EXCHANGES[which], frames))  6.88 us
    pallas_call x1, Pallas kernels, on_device(): pl.pallas_call(functools.partial(attend_kernel, frames), out_shape=[flat,...  5.7 us
  transfers between devices with their start and end apart: 12, of which 4 were waited for; matrix products, arithmetic and copies ran while one was open for 0% of the time, Pallas kernels for 2%

profile of v5, /device:TPU:4, one launch (start us, length us, event | category | flops | bytes accessed | tf_op | source)
XLA Modules:
  0.0 135.0 jit_solution(5162657632304447021)
XLA Ops:
  0.6 0.0 copy-start.1
  0.6 0.0 copy-start.5
  0.7 25.9 %pack.1 = (bf16[128,512]{1,0:T(8,128)(2,1)}, bf16[128,512]{1,0:T(8,128)(2,1)}, bf16[128,512]{1,0:T(8,128)(2,1)}, bf16[128,512]{1,0:T(8,128)(2,1)}, bf16[128,512]{1,0:T(8,128)(2,1)}, /*index=5*/bf16[128,512]{1,0:T(8,128)(2,1)}) custom-call(s32[1]{0:T(128)} %bitcast.frame_ref, s32[6,64]{1,0:T(8,128)} %bitcast.2, bf16[512,256]{1,0:T(8,128)(2,1)} %k_ref.3, ...), custom_call_target="tpu_custom_call" | custom-call | tf_op jit(solution)/shard_map/pack/pallas_call | solution.py:212
  26.6 14.5 %collective-permute-start = (bf16[128,512]{1,0:T(8,128)(2,1)}, bf16[128,512]{1,0:T(8,128)(2,1)S(1)}, u32[]{:S(2)}, u32[]{:S(2)}) collective-permute-start(bf16[128,512]{1,0:T(8,128)(2,1)} %get-tuple-element.28), channel_id=1, source_target_pairs={{64,128},{128,64},{80,144},{144,80},{96,160},{160,96},{112,176},{1... | collective-permute-start | bytes 393224 | tf_op jit(solution)/shard_map/ppermute | solution.py:199
  41.1 3.7 %collective-permute-start.1 = (bf16[128,512]{1,0:T(8,128)(2,1)}, bf16[128,512]{1,0:T(8,128)(2,1)S(1)}, u32[]{:S(2)}, u32[]{:S(2)}) collective-permute-start(bf16[128,512]{1,0:T(8,128)(2,1)} %get-tuple-element.29), channel_id=1, source_target_pairs={{32,64},{64,32},{48,80},{80,48},{96,128},{128,96},{112,144},{144,1... | collective-permute-start | bytes 393224 | tf_op jit(solution)/shard_map/ppermute | solution.py:199
  44.8 8.5 %collective-permute-start.2 = (bf16[128,512]{1,0:T(8,128)(2,1)}, bf16[128,512]{1,0:T(8,128)(2,1)S(1)}, u32[]{:S(2)}, u32[]{:S(2)}) collective-permute-start(bf16[128,512]{1,0:T(8,128)(2,1)} %get-tuple-element.30), channel_id=1, source_target_pairs={{16,32},{32,16},{48,64},{64,48},{80,96},{96,80},{112,128},{128,112... | collective-permute-start | bytes 393224 | tf_op jit(solution)/shard_map/ppermute | solution.py:199
  53.3 1.9 %collective-permute-start.3 = (bf16[128,512]{1,0:T(8,128)(2,1)}, bf16[128,512]{1,0:T(8,128)(2,1)S(1)}, u32[]{:S(2)}, u32[]{:S(2)}) collective-permute-start(bf16[128,512]{1,0:T(8,128)(2,1)} %get-tuple-element.31), channel_id=1, source_target_pairs={{0,64},{64,0},{16,80},{80,16},{32,96},{96,32},{48,112},{112,48},{1... | collective-permute-start | bytes 393224 | tf_op jit(solution)/shard_map/ppermute | solution.py:199
  55.3 1.9 %collective-permute-start.4 = (bf16[128,512]{1,0:T(8,128)(2,1)}, bf16[128,512]{1,0:T(8,128)(2,1)S(1)}, u32[]{:S(2)}, u32[]{:S(2)}) collective-permute-start(bf16[128,512]{1,0:T(8,128)(2,1)} %get-tuple-element.32), channel_id=1, source_target_pairs={{0,32},{32,0},{16,48},{48,16},{64,96},{96,64},{80,112},{112,80},{1... | collective-permute-start | bytes 393224 | tf_op jit(solution)/shard_map/ppermute | solution.py:199
  57.2 0.0 collective-permute-done.refs_0_
  57.2 1.9 %collective-permute-start.5 = (bf16[128,512]{1,0:T(8,128)(2,1)}, bf16[128,512]{1,0:T(8,128)(2,1)S(1)}, u32[]{:S(2)}, u32[]{:S(2)}) collective-permute-start(bf16[128,512]{1,0:T(8,128)(2,1)} %get-tuple-element.33), channel_id=1, source_target_pairs={{0,16},{16,0},{32,48},{48,32},{64,80},{80,64},{96,112},{112,96},{1... | collective-permute-start | bytes 393224 | tf_op jit(solution)/shard_map/ppermute | solution.py:199
  59.1 0.0 copy-start
  59.2 0.9 copy-done
  60.1 0.9 copy-done.4
  61.0 0.2 own_sums.1.own_ref
  61.3 0.0 collective-permute-done.1.refs_1_
  61.3 1.6 %collective-permute-done.3.refs_3_ = bf16[128,512]{1,0:T(8,128)(2,1)S(1)} collective-permute-done((bf16[128,512]{1,0:T(8,128)(2,1)}, bf16[128,512]{1,0:T(8,128)(2,1)S(1)}, u32[]{:S(2)}, u32[]{:S(2)}) %collective-permute-start.3) | collective-permute-done | bytes 131104 | tf_op jit(solution)/shard_map/ppermute | solution.py:199
  62.9 1.3 collective-permute-done.4.refs_4_
  64.2 0.2 all_sums.1
  64.4 35.3 %all_to_all.5.sums_ref = f32[16,16,128]{2,1,0:T(8,128)S(1)} all-to-all(f32[16,16,128]{2,1,0:T(8,128)S(1)} %all_sums.1), channel_id=1, replica_groups=mesh['frame'=64,'head'=16] {'head'}, dimensions={0} | all-to-all | bytes 262144 | tf_op jit(solution)/shard_map/all_to_all | solution.py:240
  99.7 0.3 normalize.1
  100.1 5.7 %attend.1 = (bf16[512,256]{1,0:T(8,128)(2,1)}, bf16[2,512,512]{2,1,0:T(8,128)(2,1)S(1)}, bf16[2,512,512]{2,1,0:T(8,128)(2,1)S(1)}, bf16[2,512,768]{2,1,0:T(8,128...) custom-call(s32[1]{0:T(128)} %bitcast.frame_ref, ...), custom_call_target="tpu_custom_call" | custom-call | tf_op jit(solution)/shard_map/attend/pallas_call | solution.py:252
  105.8 6.1 %collective-permute-start.6 = (bf16[128,512]{1,0:T(8,128)(2,1)S(1)}, bf16[128,512]{1,0:T(8,128)(2,1)S(1)}, u32[]{:S(2)}, u32[]{:S(2)}) collective-permute-start(bf16[128,512]{1,0:T(8,128)(2,1)S(1)} %get-tuple-element.44), channel_id=1, source_target_pairs={{64,128},{128,64},{80,144},{144,80},{96,160},{160,96},{112,176},{1... | collective-permute-start | bytes 393224 | tf_op jit(solution)/shard_map/ppermute | solution.py:199
  111.9 5.4 %collective-permute-start.7 = (bf16[128,512]{1,0:T(8,128)(2,1)S(1)}, bf16[128,512]{1,0:T(8,128)(2,1)S(1)}, u32[]{:S(2)}, u32[]{:S(2)}) collective-permute-start(bf16[128,512]{1,0:T(8,128)(2,1)S(1)} %get-tuple-element.45), channel_id=1, source_target_pairs={{32,64},{64,32},{48,80},{80,48},{96,128},{128,96},{112,144},{144,1... | collective-permute-start | bytes 393224 | tf_op jit(solution)/shard_map/ppermute | solution.py:199
  117.3 4.1 %collective-permute-start.8 = (bf16[128,512]{1,0:T(8,128)(2,1)S(1)}, bf16[128,512]{1,0:T(8,128)(2,1)S(1)}, u32[]{:S(2)}, u32[]{:S(2)}) collective-permute-start(bf16[128,512]{1,0:T(8,128)(2,1)S(1)} %get-tuple-element.46), channel_id=1, source_target_pairs={{16,32},{32,16},{48,64},{64,48},{80,96},{96,80},{112,128},{128,112... | collective-permute-start | bytes 393224 | tf_op jit(solution)/shard_map/ppermute | solution.py:199
  121.4 1.9 %collective-permute-start.9 = (bf16[128,512]{1,0:T(8,128)(2,1)S(1)}, bf16[128,512]{1,0:T(8,128)(2,1)S(1)}, u32[]{:S(2)}, u32[]{:S(2)}) collective-permute-start(bf16[128,512]{1,0:T(8,128)(2,1)S(1)} %get-tuple-element.47), channel_id=1, source_target_pairs={{0,64},{64,0},{16,80},{80,16},{32,96},{96,32},{48,112},{112,48},{1... | collective-permute-start | bytes 393224 | tf_op jit(solution)/shard_map/ppermute | solution.py:199
  123.4 1.9 %collective-permute-start.10 = (bf16[128,512]{1,0:T(8,128)(2,1)S(1)}, bf16[128,512]{1,0:T(8,128)(2,1)S(1)}, u32[]{:S(2)}, u32[]{:S(2)}) collective-permute-start(bf16[128,512]{1,0:T(8,128)(2,1)S(1)} %get-tuple-element.48), channel_id=1, source_target_pairs={{0,32},{32,0},{16,48},{48,16},{64,96},{96,64},{80,112},{112,80},{1... | collective-permute-start | bytes 393224 | tf_op jit(solution)/shard_map/ppermute | solution.py:199
  125.3 1.9 %collective-permute-start.11 = (bf16[128,512]{1,0:T(8,128)(2,1)S(1)}, bf16[128,512]{1,0:T(8,128)(2,1)S(1)}, u32[]{:S(2)}, u32[]{:S(2)}) collective-permute-start(bf16[128,512]{1,0:T(8,128)(2,1)S(1)} %get-tuple-element.49), channel_id=1, source_target_pairs={{0,16},{16,0},{32,48},{48,32},{64,80},{80,64},{96,112},{112,96},{1... | collective-permute-start | bytes 393224 | tf_op jit(solution)/shard_map/ppermute | solution.py:199
  127.2 0.0 copy-start.6
  127.2 2.1 %rest.1 = (bf16[512,256]{1,0:T(8,128)(2,1)}, f32[512,256]{1,0:T(8,128)S(1)}, f32[512,256]{1,0:T(8,128)S(1)}) custom-call(bf16[2,512,512]{2,1,0:T(8,128)(2,1)S(1)} %get-tuple-element.38.p_own, bf16[2,512,512]{2,1,0:T(8,128)(2,1)S(1)} %get-tuple-element.39.s_own, bf16[2,512,768]{2,1,0:T(8,128)(2,1)S(1)} %get-tuple-element.40.s_far, ...), custom_call_target="tpu_custom_call" | custom-call | flops 536870912 | bytes 8388608 | tf_op jit(solution)/shard_map/rest/pallas_call | solution.py:270
  129.4 3.3 %collective-permute-done.8.refs_2_ = bf16[128,512]{1,0:T(8,128)(2,1)S(1)} collective-permute-done((bf16[128,512]{1,0:T(8,128)(2,1)S(1)}, bf16[128,512]{1,0:T(8,128)(2,1)S(1)}, u32[]{:S(2)}, u32[]{:S(2)}) %collective-permute-start.8) | collective-permute-done | bytes 131104 | tf_op jit(solution)/shard_map/ppermute | solution.py:199
  132.6 0.6 collective-permute-done.10.refs_4_
  133.3 1.7 %collect.1 = (bf16[512,256]{1,0:T(8,128)(2,1)}, bf16[512,256]{1,0:T(8,128)(2,1)}) custom-call(s32[1]{0:T(128)} %bitcast.frame_ref, s32[6,64]{1,0:T(8,128)S(1)} %bitcast.3, f32[512,256]{1,0:T(8,128)S(1)} %get-tuple-element.42.gk_ref, f32[512,256]{1,0:T(8,128)S(1)} %get-tuple-element.43.gv_ref, bf16[128,512]{1,0:T(8,128)(2,1)S(1)} %collective-permute-done.6.refs_0_, ...), custom_call_target="tpu_custom_call" | custom-call | tf_op jit(solution)/shard_map/collect/pallas_call | solution.py:280
  (14 shorter events, 0.0 us)
Async XLA Ops:
  0.6 99.1 %copy-start.1 = (bf16[512,256]{1,0:T(8,128)(2,1)S(1)}, bf16[512,256]{1,0:T(8,128)(2,1)}, u32[]{:S(2)}) copy-start(bf16[512,256]{1,0:T(8,128)(2,1)} %k_ref.3) | copy-start | bytes 786436
  0.6 99.1 %copy-start.5 = (bf16[512,256]{1,0:T(8,128)(2,1)S(1)}, bf16[512,256]{1,0:T(8,128)(2,1)}, u32[]{:S(2)}) copy-start(bf16[512,256]{1,0:T(8,128)(2,1)} %q_ref.3) | copy-start | bytes 786436
  26.6 30.6 %collective-permute-start = (bf16[128,512]{1,0:T(8,128)(2,1)}, bf16[128,512]{1,0:T(8,128)(2,1)S(1)}, u32[]{:S(2)}, u32[]{:S(2)}) collective-permute-start(bf16[128,512]{1,0:T(8,128)(2,1)} %get-tuple-element.28), channel_id=1, source_target_pairs={{64,128},{128,64},{80,144},{144,80},{96,160},{160,96},{112,176},{1... | collective-permute-start | bytes 393224 | tf_op jit(solution)/shard_map/ppermute | solution.py:199
  41.1 20.2 %collective-permute-start.1 = (bf16[128,512]{1,0:T(8,128)(2,1)}, bf16[128,512]{1,0:T(8,128)(2,1)S(1)}, u32[]{:S(2)}, u32[]{:S(2)}) collective-permute-start(bf16[128,512]{1,0:T(8,128)(2,1)} %get-tuple-element.29), channel_id=1, source_target_pairs={{32,64},{64,32},{48,80},{80,48},{96,128},{128,96},{112,144},{144,1... | collective-permute-start | bytes 393224 | tf_op jit(solution)/shard_map/ppermute | solution.py:199
  44.8 16.4 %collective-permute-start.2 = (bf16[128,512]{1,0:T(8,128)(2,1)}, bf16[128,512]{1,0:T(8,128)(2,1)S(1)}, u32[]{:S(2)}, u32[]{:S(2)}) collective-permute-start(bf16[128,512]{1,0:T(8,128)(2,1)} %get-tuple-element.30), channel_id=1, source_target_pairs={{16,32},{32,16},{48,64},{64,48},{80,96},{96,80},{112,128},{128,112... | collective-permute-start | bytes 393224 | tf_op jit(solution)/shard_map/ppermute | solution.py:199
  53.3 9.6 %collective-permute-start.3 = (bf16[128,512]{1,0:T(8,128)(2,1)}, bf16[128,512]{1,0:T(8,128)(2,1)S(1)}, u32[]{:S(2)}, u32[]{:S(2)}) collective-permute-start(bf16[128,512]{1,0:T(8,128)(2,1)} %get-tuple-element.31), channel_id=1, source_target_pairs={{0,64},{64,0},{16,80},{80,16},{32,96},{96,32},{48,112},{112,48},{1... | collective-permute-start | bytes 393224 | tf_op jit(solution)/shard_map/ppermute | solution.py:199
  55.3 9.0 %collective-permute-start.4 = (bf16[128,512]{1,0:T(8,128)(2,1)}, bf16[128,512]{1,0:T(8,128)(2,1)S(1)}, u32[]{:S(2)}, u32[]{:S(2)}) collective-permute-start(bf16[128,512]{1,0:T(8,128)(2,1)} %get-tuple-element.32), channel_id=1, source_target_pairs={{0,32},{32,0},{16,48},{48,16},{64,96},{96,64},{80,112},{112,80},{1... | collective-permute-start | bytes 393224 | tf_op jit(solution)/shard_map/ppermute | solution.py:199
  57.2 7.0 %collective-permute-start.5 = (bf16[128,512]{1,0:T(8,128)(2,1)}, bf16[128,512]{1,0:T(8,128)(2,1)S(1)}, u32[]{:S(2)}, u32[]{:S(2)}) collective-permute-start(bf16[128,512]{1,0:T(8,128)(2,1)} %get-tuple-element.33), channel_id=1, source_target_pairs={{0,16},{16,0},{32,48},{48,32},{64,80},{80,64},{96,112},{112,96},{1... | collective-permute-start | bytes 393224 | tf_op jit(solution)/shard_map/ppermute | solution.py:199
  59.1 1.0 copy-start
  60.1 0.9 copy-start.4
  61.0 39.0 %copy-start.2 = (bf16[512,256]{1,0:T(8,128)(2,1)S(1)}, bf16[512,256]{1,0:T(8,128)(2,1)}, u32[]{:S(2)}) copy-start(bf16[512,256]{1,0:T(8,128)(2,1)} %d_ref.3) | copy-start | bytes 786436
  61.0 39.0 %copy-start.3 = (bf16[512,256]{1,0:T(8,128)(2,1)S(1)}, bf16[512,256]{1,0:T(8,128)(2,1)}, u32[]{:S(2)}) copy-start(bf16[512,256]{1,0:T(8,128)(2,1)} %v_ref.1) | copy-start | bytes 786436
  105.8 19.5 %collective-permute-start.6 = (bf16[128,512]{1,0:T(8,128)(2,1)S(1)}, bf16[128,512]{1,0:T(8,128)(2,1)S(1)}, u32[]{:S(2)}, u32[]{:S(2)}) collective-permute-start(bf16[128,512]{1,0:T(8,128)(2,1)S(1)} %get-tuple-element.44), channel_id=1, source_target_pairs={{64,128},{128,64},{80,144},{144,80},{96,160},{160,96},{112,176},{1... | collective-permute-start | bytes 393224 | tf_op jit(solution)/shard_map/ppermute | solution.py:199
  111.9 17.4 %collective-permute-start.7 = (bf16[128,512]{1,0:T(8,128)(2,1)S(1)}, bf16[128,512]{1,0:T(8,128)(2,1)S(1)}, u32[]{:S(2)}, u32[]{:S(2)}) collective-permute-start(bf16[128,512]{1,0:T(8,128)(2,1)S(1)} %get-tuple-element.45), channel_id=1, source_target_pairs={{32,64},{64,32},{48,80},{80,48},{96,128},{128,96},{112,144},{144,1... | collective-permute-start | bytes 393224 | tf_op jit(solution)/shard_map/ppermute | solution.py:199
  117.3 15.3 %collective-permute-start.8 = (bf16[128,512]{1,0:T(8,128)(2,1)S(1)}, bf16[128,512]{1,0:T(8,128)(2,1)S(1)}, u32[]{:S(2)}, u32[]{:S(2)}) collective-permute-start(bf16[128,512]{1,0:T(8,128)(2,1)S(1)} %get-tuple-element.46), channel_id=1, source_target_pairs={{16,32},{32,16},{48,64},{64,48},{80,96},{96,80},{112,128},{128,112... | collective-permute-start | bytes 393224 | tf_op jit(solution)/shard_map/ppermute | solution.py:199
  121.4 11.2 %collective-permute-start.9 = (bf16[128,512]{1,0:T(8,128)(2,1)S(1)}, bf16[128,512]{1,0:T(8,128)(2,1)S(1)}, u32[]{:S(2)}, u32[]{:S(2)}) collective-permute-start(bf16[128,512]{1,0:T(8,128)(2,1)S(1)} %get-tuple-element.47), channel_id=1, source_target_pairs={{0,64},{64,0},{16,80},{80,16},{32,96},{96,32},{48,112},{112,48},{1... | collective-permute-start | bytes 393224 | tf_op jit(solution)/shard_map/ppermute | solution.py:199
  123.4 9.9 %collective-permute-start.10 = (bf16[128,512]{1,0:T(8,128)(2,1)S(1)}, bf16[128,512]{1,0:T(8,128)(2,1)S(1)}, u32[]{:S(2)}, u32[]{:S(2)}) collective-permute-start(bf16[128,512]{1,0:T(8,128)(2,1)S(1)} %get-tuple-element.48), channel_id=1, source_target_pairs={{0,32},{32,0},{16,48},{48,16},{64,96},{96,64},{80,112},{112,80},{1... | collective-permute-start | bytes 393224 | tf_op jit(solution)/shard_map/ppermute | solution.py:199
  125.3 8.0 %collective-permute-start.11 = (bf16[128,512]{1,0:T(8,128)(2,1)S(1)}, bf16[128,512]{1,0:T(8,128)(2,1)S(1)}, u32[]{:S(2)}, u32[]{:S(2)}) collective-permute-start(bf16[128,512]{1,0:T(8,128)(2,1)S(1)} %get-tuple-element.49), channel_id=1, source_target_pairs={{0,16},{16,0},{32,48},{48,32},{64,80},{80,64},{96,112},{112,96},{1... | collective-permute-start | bytes 393224 | tf_op jit(solution)/shard_map/ppermute | solution.py:199
  127.2 6.1 %copy-start.6 = (s32[64,6]{0,1:T(8,128)S(1)}, s32[64,6]{0,1:T(8,128)}, u32[]{:S(2)}) copy-start(s32[64,6]{0,1:T(8,128)} %param.9) | copy-start | bytes 4612

commit v6 on v2

--- a/solution.py
+++ b/solution.py
@@ -43,7 +43,7 @@
 def block_start(kept_ref, frame, frames, distance, shifted):
     offset, slot = partner(frame, distance, shifted)
     other = jnp.clip(frame + offset, 0, frames - 1)
-    return pl.multiple_of(kept_ref[other, slot] * BS, BS)
+    return pl.multiple_of(kept_ref[slot, other] * BS, BS)
 
 
 def is_live(frame, frames, distance, shifted):
@@ -56,8 +56,8 @@
     return ((frame % 2) ^ ((frame // 2) % 2)) == 1
 
 
-def prepare_kernel(frames, frame_ref, kept_ref, q_ref, k_ref, v_ref, sums_ref, *block_refs):
-    frame = frame_ref[0]
+def prepare_kernel(frames, kept_ref, q_ref, k_ref, v_ref, sums_ref, mask_ref, *block_refs):
+    frame = lax.axis_index("frame")
     width = k_ref.shape[1]
     rows = []
     for ref in (q_ref, k_ref):
@@ -70,6 +70,15 @@
     packed = jnp.concatenate(rows, axis=0)
     for copy in range(sums_ref.shape[0]):
         sums_ref[copy] = packed
+    mask_ref[...] = jnp.zeros_like(mask_ref)
+    for distance, shifted in EXCHANGES:
+        offset, _ = partner(frame, distance, shifted)
+        block = block_start(kept_ref, frame, frames, distance, shifted) // BS
+
+        @pl.when(is_live(frame, frames, distance, shifted))
+        def _():
+            mask_ref[frame + offset, pl.ds(block, 1), :] = jnp.ones((1, BS), jnp.float32)
+
     first = block_refs[0]
     targets = [first.at[:BS], *block_refs[1:], first.at[BS:]]
     for (distance, shifted), block in zip(EXCHANGES, targets):
@@ -86,24 +95,15 @@
     return (block.astype(jnp.float32) * scale).astype(jnp.bfloat16)
 
 
-def norm_kernel(frames, width_all, frame_ref, kept_ref, sums_ref, q_ref, k_ref, qn_ref, kn_ref, scale_ref, scale_rows):
-    frame = frame_ref[0]
+def norm_kernel(width_all, sums_ref, mask_ref, q_ref, k_ref, qn_ref, kn_ref, scale_ref):
     width = q_ref.shape[1]
     total = sums_ref[0]
     for part in range(1, sums_ref.shape[0]):
         total += sums_ref[part]
     scale = lax.rsqrt(total / width_all + norm_eps)
-    scale_rows[...] = scale
-    scale_ref[...] = jnp.zeros_like(scale_ref)
-    for distance, shifted in EXCHANGES:
-        offset, _ = partner(frame, distance, shifted)
-        block = block_start(kept_ref, frame, frames, distance, shifted) // BS
-        row = q_ref.shape[0] // BS + block
-
-        @pl.when(is_live(frame, frames, distance, shifted))
-        def _():
-            scale_ref[frame + offset] = scale_rows[pl.ds(row, 1), :]
-
+    key_scale = scale[q_ref.shape[0] // 128 :]
+    for frame in range(scale_ref.shape[0]):
+        scale_ref[frame] = jnp.sum(mask_ref[frame] * key_scale, axis=0, keepdims=True)
     row = 0
     for ref, out in ((q_ref, qn_ref), (k_ref, kn_ref)):
         for start in range(0, ref.shape[0], 128):
@@ -117,6 +117,7 @@
 CONTRACT_LAST = (((1,), (1,)), ((), ()))
 CONTRACT_FIRST = (((0,), (0,)), ((), ()))
 FACTOR = 1.0 / math.sqrt(HD)
+EXPONENT = FACTOR * math.log2(math.e)
 CHUNK = 256
 
 
@@ -124,12 +125,12 @@
     return lax.dot_general(left, right, dims, preferred_element_type=jnp.float32)
 
 
-def attend_kernel(frames, frame_ref, scale_ref, q_ref, k_ref, v_ref, d_ref, *refs):
+def attend_kernel(frames, scale_ref, q_ref, k_ref, v_ref, d_ref, *refs):
     far_refs = refs[:5]
     att_ref, p_own, s_own, s_far, k_far = refs[5:10]
     back_refs = refs[10:16]
     v_far, p_far = refs[16:]
-    frame = frame_ref[0]
+    frame = lax.axis_index("frame")
     tokens, width = q_ref.shape
     f32 = jnp.float32
 
@@ -166,23 +167,21 @@
         for first in range(0, tokens, CHUNK):
             rows = slice(first, first + CHUNK)
             grads = d_ref[rows, head]
-            own = dot(q_ref[rows, head], k_ref[:, head], CONTRACT_LAST) * FACTOR
-            far = jnp.where(allowed, dot(q_ref[rows, head], keys, CONTRACT_LAST) * FACTOR, masked_score)
+            own = dot(q_ref[rows, head], k_ref[:, head], CONTRACT_LAST)
+            far = jnp.where(allowed, dot(q_ref[rows, head], keys, CONTRACT_LAST), masked_score)
             top = jnp.maximum(jnp.max(own, axis=1, keepdims=True), jnp.max(far, axis=1, keepdims=True))
-            own = jnp.exp(own - top)
-            far = jnp.exp(far - top)
+            own = jnp.exp2((own - top) * EXPONENT)
+            far = jnp.exp2((far - top) * EXPONENT)
             share = 1.0 / (jnp.sum(own, axis=1, keepdims=True) + jnp.sum(far, axis=1, keepdims=True))
-            own = own * share
-            far = far * share
-            own_low = own.astype(jnp.bfloat16)
-            far_low = far.astype(jnp.bfloat16)
+            own_low = (own * share).astype(jnp.bfloat16)
+            far_low = (far * share).astype(jnp.bfloat16)
             p_own[index, rows, :] = own_low
             p_far[rows, :] = far_low
             attended = (dot(own_low, v_ref[:, head]) + dot(far_low, vals)).astype(jnp.bfloat16)
             att_ref[rows, head] = attended
             inner = jnp.sum(grads.astype(f32) * attended.astype(f32), axis=1, keepdims=True)
-            s_own[index, rows, :] = (own * (dot(grads, v_ref[:, head], CONTRACT_LAST) - inner)).astype(jnp.bfloat16)
-            s_far[index, rows, :] = (far * (dot(grads, vals, CONTRACT_LAST) - inner)).astype(jnp.bfloat16)
+            s_own[index, rows, :] = (own * ((dot(grads, v_ref[:, head], CONTRACT_LAST) - inner) * share)).astype(jnp.bfloat16)
+            s_far[index, rows, :] = (far * ((dot(grads, vals, CONTRACT_LAST) - inner) * share)).astype(jnp.bfloat16)
         grad_k = dot(s_far[index], q_ref[:, head], CONTRACT_FIRST) * FACTOR
         grad_v = dot(p_far[...], d_ref[:, head], CONTRACT_FIRST)
         for slot, back in zip(RETURN_ORDER, back_refs):
@@ -200,9 +199,9 @@
         gv_ref[:, head] = dot(p_own[index], d_ref[:, head], CONTRACT_FIRST)
 
 
-def collect_kernel(frames, frame_ref, kept_ref, gk_ref, gv_ref, *refs):
+def collect_kernel(frames, kept_ref, gk_ref, gv_ref, *refs):
     back_refs, (outk_ref, outv_ref, acc_k, acc_v) = refs[:6], refs[6:]
-    frame = frame_ref[0]
+    frame = lax.axis_index("frame")
     width = gk_ref.shape[1]
     acc_k[...] = gk_ref[...]
     acc_v[...] = gv_ref[...]
@@ -242,31 +241,35 @@
     frames = lax.axis_size("frame")
     heads = lax.axis_size("head")
     tokens, width = queries.shape
-    frame = lax.axis_index("frame").reshape(1)
+    kept = kept.T
     stat_rows = 2 * tokens // 128
     flat = jax.ShapeDtypeStruct((tokens, width), jnp.bfloat16)
     wide = jax.ShapeDtypeStruct((tokens, width), jnp.float32)
     block = jax.ShapeDtypeStruct((BS, 2 * width), jnp.bfloat16)
     pair = jax.ShapeDtypeStruct((2 * BS, 2 * width), jnp.bfloat16)
-    sums, *sent = pl.pallas_call(
+    sums, mask, *sent = pl.pallas_call(
         functools.partial(prepare_kernel, frames),
-        out_shape=[jax.ShapeDtypeStruct((heads, stat_rows, 128), jnp.float32), pair] + [block] * 4,
-        in_specs=[SMEM] * 2 + [VMEM] * 3,
-        out_specs=[VMEM] * 6,
+        out_shape=[
+            jax.ShapeDtypeStruct((heads, stat_rows, 128), jnp.float32),
+            jax.ShapeDtypeStruct((frames, tokens // BS, BS), jnp.float32),
+            pair,
+        ]
+        + [block] * 4,
+        in_specs=[SMEM] + [VMEM] * 3,
+        out_specs=[VMEM] * 7,
         compiler_params=params(8),
         name="prepare",
-    )(frame, kept, queries, keys, values)
+    )(kept, queries, keys, values)
     sums = lax.all_to_all(sums, "head", 0, 0)
     far = swap_relayed(sent, frames)
     q_norm, k_norm, scales = pl.pallas_call(
-        functools.partial(norm_kernel, frames, width * heads),
+        functools.partial(norm_kernel, width * heads),
         out_shape=[flat, flat, jax.ShapeDtypeStruct((frames, 1, BS), jnp.float32)],
-        in_specs=[SMEM] * 2 + [VMEM] * 3,
+        in_specs=[VMEM] * 4,
         out_specs=[VMEM] * 3,
-        scratch_shapes=[pltpu.VMEM((stat_rows, 128), jnp.float32)],
         compiler_params=params(8),
         name="normalize",
-    )(frame, kept, sums, queries, keys)
+    )(sums, mask, queries, keys)
     scales = lax.all_to_all(scales, "frame", 0, 0)
     heads_dev = width // HD
     own_shape = (heads_dev, tokens, tokens)
@@ -281,7 +284,7 @@
             jax.ShapeDtypeStruct((6 * BS, width), jnp.bfloat16),
         ]
         + [block] * 6,
-        in_specs=[SMEM] + [VMEM] * 10,
+        in_specs=[VMEM] * 10,
         out_specs=[VMEM] * 11,
         scratch_shapes=[
             pltpu.VMEM((6 * BS, width), jnp.bfloat16),
@@ -289,7 +292,7 @@
         ],
         compiler_params=params(20),
         name="attend",
-    )(frame, scales, q_norm, k_norm, values, cotangent, *far)
+    )(scales, q_norm, k_norm, values, cotangent, *far)
     grad_q, own_k, own_v = pl.pallas_call(
         rest_kernel,
         out_shape=[flat, wide, wide],
@@ -303,12 +306,12 @@
     grad_k, grad_v = pl.pallas_call(
         functools.partial(collect_kernel, frames),
         out_shape=[flat, flat],
-        in_specs=[SMEM] * 2 + [VMEM] * 8,
+        in_specs=[SMEM] + [VMEM] * 8,
         out_specs=[VMEM] * 2,
         scratch_shapes=[pltpu.VMEM((tokens, width), jnp.float32)] * 2,
         compiler_params=params(8),
         name="collect",
-    )(frame, kept, own_k, own_v, *back)
+    )(kept, own_k, own_v, *back)
     return attended, grad_q, grad_k, grad_v
 
 

time: 111 us -> 111 us (level)
  Pallas kernels: 14 us -> 12.2 us
    ppermute x11, waiting for transfers between devices: 7.15 us -> 8.37 us  [exchange(): return lax.ppermute(block, 'frame', route(*EXCHANGES[which], frames))]
    unnamed x15 -> x18, local copies, waits for them, and re-layouts: 3.68 us -> 3.55 us
  transfers between devices with their start and end apart: 13 -> 13, of which waited for: 5 -> 5; matrix products, arithmetic and copies ran while one was open for 0% -> 1% of each run, Pallas kernels for 4% -> 3%
where the time goes in v6:
time: 111 us; the launch traced here: 110 us
  starting transfers between devices  76.6 us (69%)
  waiting for transfers between devices  16.1 us (15%)
  Pallas kernels  12.2 us (11%)
  local copies, waits for them, and re-layouts  3.56 us (3%)
    ppermute x11, starting transfers between devices, exchange(): return lax.ppermute(block, 'frame', route(*EXCHANGES[which], frames))  38.3 us
    all_to_all x1, starting transfers between devices, on_device(): sums = lax.all_to_all(sums, 'head', 0, 0)  24.5 us
    all_to_all x1, starting transfers between devices, on_device(): scales = lax.all_to_all(scales, 'frame', 0, 0)  13.9 us
    ppermute x11, waiting for transfers between devices, exchange(): return lax.ppermute(block, 'frame', route(*EXCHANGES[which], frames))  8.37 us
    all_to_all x1, waiting for transfers between devices, on_device(): scales = lax.all_to_all(scales, 'frame', 0, 0)  7.58 us
    pallas_call x1, Pallas kernels, on_device(): pl.pallas_call(functools.partial(attend_kernel, frames), out_shape=[flat,...  5.87 us
    unnamed x18, local copies, waits for them, and re-layouts  3.55 us
  transfers between devices with their start and end apart: 13, of which 5 were waited for; matrix products, arithmetic and copies ran while one was open for 1% of the time, Pallas kernels for 3%

profile of v6, /device:TPU:10, one launch (start us, length us, event | category | flops | bytes accessed | tf_op | source)
XLA Modules:
  0.0 110.0 jit_solution(7100572651353253558)
XLA Ops:
  0.6 0.9 copy-done
  1.6 0.9 copy-done.2
  2.5 0.9 copy-done.4
  3.5 0.7 copy-done.7
  4.2 1.6 %prepare.1 = (f32[16,8,128]{2,1,0:T(8,128)}, f32[64,4,128]{2,1,0:T(4,128)S(1)}, bf16[256,512]{1,0:T(8,128)(2,1)S(1)}, bf16[128,512]{1,0:T(8,128)(2,1)S(1)}, bf16...) custom-call(s32[6,64]{1,0:T(8,128)S(1)} %bitcast.1, ...), custom_call_target="tpu_custom_call" | custom-call | tf_op jit(solution)/shard_map/prepare/pallas_call | solution.py:250
  5.8 1.9 %collective-permute-start = (bf16[256,512]{1,0:T(8,128)(2,1)S(1)}, bf16[256,512]{1,0:T(8,128)(2,1)S(1)}, u32[]{:S(2)}, u32[]{:S(2)}) collective-permute-start(bf16[256,512]{1,0:T(8,128)(2,1)S(1)} %get-tuple-element.35), channel_id=1, source_target_pairs={{0,16},{16,0},{32,48},{48,32},{64,80},{80,64},{96,112},{112,96},{1... | collective-permute-start | bytes 786440 | tf_op jit(solution)/shard_map/ppermute | solution.py:222
  7.7 24.5 %all-to-all-start = ((f32[16,8,128]{2,1,0:T(8,128)}), f32[16,8,128]{2,1,0:T(8,128)S(1)}, u32[]{:S(2)}, u32[]{:S(2)}) async-start(f32[16,8,128]{2,1,0:T(8,128)} %get-tuple-element.30), calls=%async_computation | async-start | bytes 131072 | tf_op jit(solution)/shard_map/all_to_all | solution.py:263
  32.2 0.0 collective-permute-done.refs_0_
  32.2 0.7 pad_maximum_fusion
  32.9 3.4 %collective-permute-start.4 = (bf16[256,512]{1,0:T(8,128)(2,1)}, bf16[256,512]{1,0:T(8,128)(2,1)S(1)}, u32[]{:S(2)}, u32[]{:S(2)}) collective-permute-start(bf16[256,512]{1,0:T(8,128)(2,1)} %get-tuple-element.56), channel_id=1, source_target_pairs={{0,32},{32,0},{16,48},{48,16},{64,96},{96,64},{80,112},{112,80},{1... | collective-permute-start | bytes 786440 | tf_op jit(solution)/shard_map/ppermute | solution.py:222
  36.3 7.9 %collective-permute-start.3 = (bf16[256,512]{1,0:T(8,128)(2,1)S(1)}, bf16[256,512]{1,0:T(8,128)(2,1)S(1)}, u32[]{:S(2)}, u32[]{:S(2)}) collective-permute-start(bf16[256,512]{1,0:T(8,128)(2,1)S(1)} %get-tuple-element.57), channel_id=1, source_target_pairs={{32,64},{64,32},{48,80},{80,48},{96,128},{128,96},{112,144},{144,1... | collective-permute-start | bytes 786440 | tf_op jit(solution)/shard_map/ppermute | solution.py:222
  44.2 1.9 %collective-permute-start.1 = (bf16[128,512]{1,0:T(8,128)(2,1)S(1)}, bf16[128,512]{1,0:T(8,128)(2,1)S(1)}, u32[]{:S(2)}, u32[]{:S(2)}) collective-permute-start(bf16[128,512]{1,0:T(8,128)(2,1)S(1)} %get-tuple-element.36), channel_id=1, source_target_pairs={{64,128},{128,64},{80,144},{144,80},{96,160},{160,96},{112,176},{1... | collective-permute-start | bytes 393224 | tf_op jit(solution)/shard_map/ppermute | solution.py:222
  46.1 1.9 %collective-permute-start.2 = (bf16[128,512]{1,0:T(8,128)(2,1)S(1)}, bf16[128,512]{1,0:T(8,128)(2,1)S(1)}, u32[]{:S(2)}, u32[]{:S(2)}) collective-permute-start(bf16[128,512]{1,0:T(8,128)(2,1)S(1)} %get-tuple-element.37), channel_id=1, source_target_pairs={{0,64},{64,0},{16,80},{80,16},{32,96},{96,32},{48,112},{112,48},{1... | collective-permute-start | bytes 393224 | tf_op jit(solution)/shard_map/ppermute | solution.py:222
  48.1 0.2 all-to-all-done.sums_ref
  48.3 0.9 normalize.1
  49.2 13.9 %all-to-all-start.1 = ((f32[64,1,128]{2,1,0:T(1,128)}), f32[64,1,128]{2,1,0:T(1,128)S(1)}, u32[]{:S(2)}, u32[]{:S(2)}) async-start(f32[64,1,128]{2,1,0:T(1,128)} %get-tuple-element.32), calls=%async_computation.1 | async-start | bytes 65536 | tf_op jit(solution)/shard_map/all_to_all | solution.py:273
  63.0 3.8 %collective-permute-done.1.refs_1_ = bf16[128,512]{1,0:T(8,128)(2,1)S(1)} collective-permute-done((bf16[128,512]{1,0:T(8,128)(2,1)S(1)}, bf16[128,512]{1,0:T(8,128)(2,1)S(1)}, u32[]{:S(2)}, u32[]{:S(2)}) %collective-permute-start.1) | collective-permute-done | bytes 131104 | tf_op jit(solution)/shard_map/ppermute | solution.py:222
  66.9 0.0 collective-permute-done.2.refs_2_
  66.9 7.6 %all-to-all-done.1.scale_ref = f32[64,1,128]{2,1,0:T(1,128)S(1)} async-done(((f32[64,1,128]{2,1,0:T(1,128)}), f32[64,1,128]{2,1,0:T(1,128)S(1)}, u32[]{:S(2)}, u32[]{:S(2)}) %all-to-all-start.1) | async-done | bytes 32800 | tf_op jit(solution)/shard_map/all_to_all | solution.py:273
  74.5 0.0 collective-permute-done.3.refs_3_
  74.5 5.9 %attend.1 = (bf16[512,256]{1,0:T(8,128)(2,1)}, bf16[2,512,512]{2,1,0:T(8,128)(2,1)S(1)}, bf16[2,512,512]{2,1,0:T(8,128)(2,1)S(1)}, bf16[2,512,768]{2,1,0:T(8,128...) custom-call(f32[64,1,128]{2,1,0:T(1,128)S(1)} %all-to-all-done.1.sca, ...), custom_call_target="tpu_custom_call" | custom-call | tf_op jit(solution)/shard_map/attend/pallas_call | solution.py:277
  80.4 3.3 %collective-permute-start.5 = (bf16[128,512]{1,0:T(8,128)(2,1)S(1)}, bf16[128,512]{1,0:T(8,128)(2,1)S(1)}, u32[]{:S(2)}, u32[]{:S(2)}) collective-permute-start(bf16[128,512]{1,0:T(8,128)(2,1)S(1)} %get-tuple-element.48), channel_id=1, source_target_pairs={{64,128},{128,64},{80,144},{144,80},{96,160},{160,96},{112,176},{1... | collective-permute-start | bytes 393224 | tf_op jit(solution)/shard_map/ppermute | solution.py:222
  83.6 8.9 %collective-permute-start.6 = (bf16[128,512]{1,0:T(8,128)(2,1)S(1)}, bf16[128,512]{1,0:T(8,128)(2,1)S(1)}, u32[]{:S(2)}, u32[]{:S(2)}) collective-permute-start(bf16[128,512]{1,0:T(8,128)(2,1)S(1)} %get-tuple-element.49), channel_id=1, source_target_pairs={{32,64},{64,32},{48,80},{80,48},{96,128},{128,96},{112,144},{144,1... | collective-permute-start | bytes 393224 | tf_op jit(solution)/shard_map/ppermute | solution.py:222
  92.5 3.4 %collective-permute-start.7 = (bf16[128,512]{1,0:T(8,128)(2,1)S(1)}, bf16[128,512]{1,0:T(8,128)(2,1)S(1)}, u32[]{:S(2)}, u32[]{:S(2)}) collective-permute-start(bf16[128,512]{1,0:T(8,128)(2,1)S(1)} %get-tuple-element.50), channel_id=1, source_target_pairs={{16,32},{32,16},{48,64},{64,48},{80,96},{96,80},{112,128},{128,112... | collective-permute-start | bytes 393224 | tf_op jit(solution)/shard_map/ppermute | solution.py:222
  95.9 1.9 %collective-permute-start.8 = (bf16[128,512]{1,0:T(8,128)(2,1)S(1)}, bf16[128,512]{1,0:T(8,128)(2,1)S(1)}, u32[]{:S(2)}, u32[]{:S(2)}) collective-permute-start(bf16[128,512]{1,0:T(8,128)(2,1)S(1)} %get-tuple-element.51), channel_id=1, source_target_pairs={{0,64},{64,0},{16,80},{80,16},{32,96},{96,32},{48,112},{112,48},{1... | collective-permute-start | bytes 393224 | tf_op jit(solution)/shard_map/ppermute | solution.py:222
  97.8 1.9 %collective-permute-start.9 = (bf16[128,512]{1,0:T(8,128)(2,1)S(1)}, bf16[128,512]{1,0:T(8,128)(2,1)S(1)}, u32[]{:S(2)}, u32[]{:S(2)}) collective-permute-start(bf16[128,512]{1,0:T(8,128)(2,1)S(1)} %get-tuple-element.52), channel_id=1, source_target_pairs={{0,32},{32,0},{16,48},{48,16},{64,96},{96,64},{80,112},{112,80},{1... | collective-permute-start | bytes 393224 | tf_op jit(solution)/shard_map/ppermute | solution.py:222
  99.8 1.9 %collective-permute-start.10 = (bf16[128,512]{1,0:T(8,128)(2,1)S(1)}, bf16[128,512]{1,0:T(8,128)(2,1)S(1)}, u32[]{:S(2)}, u32[]{:S(2)}) collective-permute-start(bf16[128,512]{1,0:T(8,128)(2,1)S(1)} %get-tuple-element.53), channel_id=1, source_target_pairs={{0,16},{16,0},{32,48},{48,32},{64,80},{80,64},{96,112},{112,96},{1... | collective-permute-start | bytes 393224 | tf_op jit(solution)/shard_map/ppermute | solution.py:222
  101.7 0.0 copy-start.8
  101.7 2.1 %rest.1 = (bf16[512,256]{1,0:T(8,128)(2,1)}, f32[512,256]{1,0:T(8,128)S(1)}, f32[512,256]{1,0:T(8,128)S(1)}) custom-call(bf16[2,512,512]{2,1,0:T(8,128)(2,1)S(1)} %get-tuple-element.41.p_own, bf16[2,512,512]{2,1,0:T(8,128)(2,1)S(1)} %get-tuple-element.42.s_own, bf16[2,512,768]{2,1,0:T(8,128)(2,1)S(1)} %get-tuple-element.43.s_far, ...), custom_call_target="tpu_custom_call" | custom-call | flops 536870912 | bytes 8388608 | tf_op jit(solution)/shard_map/rest/pallas_call | solution.py:296
  103.8 2.8 %collective-permute-done.7.refs_2_ = bf16[128,512]{1,0:T(8,128)(2,1)S(1)} collective-permute-done((bf16[128,512]{1,0:T(8,128)(2,1)S(1)}, bf16[128,512]{1,0:T(8,128)(2,1)S(1)}, u32[]{:S(2)}, u32[]{:S(2)}) %collective-permute-start.7) | collective-permute-done | bytes 131104 | tf_op jit(solution)/shard_map/ppermute | solution.py:222
  106.6 1.7 %collective-permute-done.8.refs_3_ = bf16[128,512]{1,0:T(8,128)(2,1)S(1)} collective-permute-done((bf16[128,512]{1,0:T(8,128)(2,1)S(1)}, bf16[128,512]{1,0:T(8,128)(2,1)S(1)}, u32[]{:S(2)}, u32[]{:S(2)}) %collective-permute-start.8) | collective-permute-done | bytes 131104 | tf_op jit(solution)/shard_map/ppermute | solution.py:222
  108.3 1.7 %collect.1 = (bf16[512,256]{1,0:T(8,128)(2,1)}, bf16[512,256]{1,0:T(8,128)(2,1)}) custom-call(s32[6,64]{1,0:T(8,128)S(1)} %bitcast.2, f32[512,256]{1,0:T(8,128)S(1)} %get-tuple-element.46.gk_ref, f32[512,256]{1,0:T(8,128)S(1)} %get-tuple-element.47.gv_ref, bf16[128,512]{1,0:T(8,128)(2,1)S(1)} %collective-permute-done.5.refs_0_, ...), custom_call_target="tpu_custom_call" | custom-call | tf_op jit(solution)/shard_map/collect/pallas_call | solution.py:306
  (19 shorter events, 0.0 us)
Async XLA Ops:
  0.6 1.0 copy-start
  1.6 0.9 copy-start.2
  2.5 0.9 copy-start.4
  3.5 0.7 copy-start.7
  4.2 44.1 %copy-start.1 = (bf16[512,256]{1,0:T(8,128)(2,1)S(1)}, bf16[512,256]{1,0:T(8,128)(2,1)}, u32[]{:S(2)}) copy-start(bf16[512,256]{1,0:T(8,128)(2,1)} %q_ref.3) | copy-start | bytes 786436
  4.2 44.1 %copy-start.3 = (bf16[512,256]{1,0:T(8,128)(2,1)S(1)}, bf16[512,256]{1,0:T(8,128)(2,1)}, u32[]{:S(2)}) copy-start(bf16[512,256]{1,0:T(8,128)(2,1)} %k_ref.3) | copy-start | bytes 786436
  4.2 70.3 %copy-start.5 = (bf16[512,256]{1,0:T(8,128)(2,1)S(1)}, bf16[512,256]{1,0:T(8,128)(2,1)}, u32[]{:S(2)}) copy-start(bf16[512,256]{1,0:T(8,128)(2,1)} %v_ref.3) | copy-start | bytes 786436
  4.2 70.3 %copy-start.6 = (bf16[512,256]{1,0:T(8,128)(2,1)S(1)}, bf16[512,256]{1,0:T(8,128)(2,1)}, u32[]{:S(2)}) copy-start(bf16[512,256]{1,0:T(8,128)(2,1)} %d_ref.3) | copy-start | bytes 786436
  5.8 26.4 %collective-permute-start = (bf16[256,512]{1,0:T(8,128)(2,1)S(1)}, bf16[256,512]{1,0:T(8,128)(2,1)S(1)}, u32[]{:S(2)}, u32[]{:S(2)}) collective-permute-start(bf16[256,512]{1,0:T(8,128)(2,1)S(1)} %get-tuple-element.35), channel_id=1, source_target_pairs={{0,16},{16,0},{32,48},{48,32},{64,80},{80,64},{96,112},{112,96},{1... | collective-permute-start | bytes 786440 | tf_op jit(solution)/shard_map/ppermute | solution.py:222
  7.7 40.6 %all-to-all-start = ((f32[16,8,128]{2,1,0:T(8,128)}), f32[16,8,128]{2,1,0:T(8,128)S(1)}, u32[]{:S(2)}, u32[]{:S(2)}) async-start(f32[16,8,128]{2,1,0:T(8,128)} %get-tuple-element.30), calls=%async_computation | async-start | bytes 131072 | tf_op jit(solution)/shard_map/all_to_all | solution.py:263
  32.9 41.6 %collective-permute-start.4 = (bf16[256,512]{1,0:T(8,128)(2,1)}, bf16[256,512]{1,0:T(8,128)(2,1)S(1)}, u32[]{:S(2)}, u32[]{:S(2)}) collective-permute-start(bf16[256,512]{1,0:T(8,128)(2,1)} %get-tuple-element.56), channel_id=1, source_target_pairs={{0,32},{32,0},{16,48},{48,16},{64,96},{96,64},{80,112},{112,80},{1... | collective-permute-start | bytes 786440 | tf_op jit(solution)/shard_map/ppermute | solution.py:222
  36.3 38.2 %collective-permute-start.3 = (bf16[256,512]{1,0:T(8,128)(2,1)S(1)}, bf16[256,512]{1,0:T(8,128)(2,1)S(1)}, u32[]{:S(2)}, u32[]{:S(2)}) collective-permute-start(bf16[256,512]{1,0:T(8,128)(2,1)S(1)} %get-tuple-element.57), channel_id=1, source_target_pairs={{32,64},{64,32},{48,80},{80,48},{96,128},{128,96},{112,144},{144,1... | collective-permute-start | bytes 786440 | tf_op jit(solution)/shard_map/ppermute | solution.py:222
  44.2 22.7 %collective-permute-start.1 = (bf16[128,512]{1,0:T(8,128)(2,1)S(1)}, bf16[128,512]{1,0:T(8,128)(2,1)S(1)}, u32[]{:S(2)}, u32[]{:S(2)}) collective-permute-start(bf16[128,512]{1,0:T(8,128)(2,1)S(1)} %get-tuple-element.36), channel_id=1, source_target_pairs={{64,128},{128,64},{80,144},{144,80},{96,160},{160,96},{112,176},{1... | collective-permute-start | bytes 393224 | tf_op jit(solution)/shard_map/ppermute | solution.py:222
  46.1 20.8 %collective-permute-start.2 = (bf16[128,512]{1,0:T(8,128)(2,1)S(1)}, bf16[128,512]{1,0:T(8,128)(2,1)S(1)}, u32[]{:S(2)}, u32[]{:S(2)}) collective-permute-start(bf16[128,512]{1,0:T(8,128)(2,1)S(1)} %get-tuple-element.37), channel_id=1, source_target_pairs={{0,64},{64,0},{16,80},{80,16},{32,96},{96,32},{48,112},{112,48},{1... | collective-permute-start | bytes 393224 | tf_op jit(solution)/shard_map/ppermute | solution.py:222
  49.2 25.3 %all-to-all-start.1 = ((f32[64,1,128]{2,1,0:T(1,128)}), f32[64,1,128]{2,1,0:T(1,128)S(1)}, u32[]{:S(2)}, u32[]{:S(2)}) async-start(f32[64,1,128]{2,1,0:T(1,128)} %get-tuple-element.32), calls=%async_computation.1 | async-start | bytes 65536 | tf_op jit(solution)/shard_map/all_to_all | solution.py:273
  80.4 19.4 %collective-permute-start.5 = (bf16[128,512]{1,0:T(8,128)(2,1)S(1)}, bf16[128,512]{1,0:T(8,128)(2,1)S(1)}, u32[]{:S(2)}, u32[]{:S(2)}) collective-permute-start(bf16[128,512]{1,0:T(8,128)(2,1)S(1)} %get-tuple-element.48), channel_id=1, source_target_pairs={{64,128},{128,64},{80,144},{144,80},{96,160},{160,96},{112,176},{1... | collective-permute-start | bytes 393224 | tf_op jit(solution)/shard_map/ppermute | solution.py:222
  83.6 20.2 %collective-permute-start.6 = (bf16[128,512]{1,0:T(8,128)(2,1)S(1)}, bf16[128,512]{1,0:T(8,128)(2,1)S(1)}, u32[]{:S(2)}, u32[]{:S(2)}) collective-permute-start(bf16[128,512]{1,0:T(8,128)(2,1)S(1)} %get-tuple-element.49), channel_id=1, source_target_pairs={{32,64},{64,32},{48,80},{80,48},{96,128},{128,96},{112,144},{144,1... | collective-permute-start | bytes 393224 | tf_op jit(solution)/shard_map/ppermute | solution.py:222
  92.5 14.1 %collective-permute-start.7 = (bf16[128,512]{1,0:T(8,128)(2,1)S(1)}, bf16[128,512]{1,0:T(8,128)(2,1)S(1)}, u32[]{:S(2)}, u32[]{:S(2)}) collective-permute-start(bf16[128,512]{1,0:T(8,128)(2,1)S(1)} %get-tuple-element.50), channel_id=1, source_target_pairs={{16,32},{32,16},{48,64},{64,48},{80,96},{96,80},{112,128},{128,112... | collective-permute-start | bytes 393224 | tf_op jit(solution)/shard_map/ppermute | solution.py:222
  95.9 12.4 %collective-permute-start.8 = (bf16[128,512]{1,0:T(8,128)(2,1)S(1)}, bf16[128,512]{1,0:T(8,128)(2,1)S(1)}, u32[]{:S(2)}, u32[]{:S(2)}) collective-permute-start(bf16[128,512]{1,0:T(8,128)(2,1)S(1)} %get-tuple-element.51), channel_id=1, source_target_pairs={{0,64},{64,0},{16,80},{80,16},{32,96},{96,32},{48,112},{112,48},{1... | collective-permute-start | bytes 393224 | tf_op jit(solution)/shard_map/ppermute | solution.py:222
  97.8 10.5 %collective-permute-start.9 = (bf16[128,512]{1,0:T(8,128)(2,1)S(1)}, bf16[128,512]{1,0:T(8,128)(2,1)S(1)}, u32[]{:S(2)}, u32[]{:S(2)}) collective-permute-start(bf16[128,512]{1,0:T(8,128)(2,1)S(1)} %get-tuple-element.52), channel_id=1, source_target_pairs={{0,32},{32,0},{16,48},{48,16},{64,96},{96,64},{80,112},{112,80},{1... | collective-permute-start | bytes 393224 | tf_op jit(solution)/shard_map/ppermute | solution.py:222
  99.8 8.5 %collective-permute-start.10 = (bf16[128,512]{1,0:T(8,128)(2,1)S(1)}, bf16[128,512]{1,0:T(8,128)(2,1)S(1)}, u32[]{:S(2)}, u32[]{:S(2)}) collective-permute-start(bf16[128,512]{1,0:T(8,128)(2,1)S(1)} %get-tuple-element.53), channel_id=1, source_target_pairs={{0,16},{16,0},{32,48},{48,32},{64,80},{80,64},{96,112},{112,96},{1... | collective-permute-start | bytes 393224 | tf_op jit(solution)/shard_map/ppermute | solution.py:222
  101.7 6.6 %copy-start.8 = (s32[64,6]{0,1:T(8,128)S(1)}, s32[64,6]{0,1:T(8,128)}, u32[]{:S(2)}) copy-start(s32[64,6]{0,1:T(8,128)} %param.9) | copy-start | bytes 4612

commit v7 on v6

--- a/solution.py
+++ b/solution.py
@@ -17,6 +17,8 @@
 norm_eps = 1e-06
 
 VMEM = pl.BlockSpec(memory_space=pltpu.VMEM)
+PREPARE_MIB = 53
+ANY = pl.BlockSpec(memory_space=pl.ANY)
 SMEM = pl.BlockSpec(memory_space=pltpu.SMEM)
 
 
@@ -56,11 +58,19 @@
     return ((frame % 2) ^ ((frame // 2) % 2)) == 1
 
 
-def prepare_kernel(frames, kept_ref, q_ref, k_ref, v_ref, sums_ref, mask_ref, *block_refs):
+def prepare_kernel(frames, kept_ref, q_hbm, k_hbm, v_hbm, sums_ref, wanted_ref, *refs):
+    block_refs, (q_ref, k_ref, v_ref, sems) = refs[:5], refs[5:]
+    copies = [
+        pltpu.make_async_copy(source, target, sems.at[index])
+        for index, (source, target) in enumerate(((q_hbm, q_ref), (k_hbm, k_ref), (v_hbm, v_ref)))
+    ]
+    for copy in copies:
+        copy.start()
     frame = lax.axis_index("frame")
     width = k_ref.shape[1]
     rows = []
-    for ref in (q_ref, k_ref):
+    for copy, ref in zip(copies, (q_ref, k_ref)):
+        copy.wait()
         for start in range(0, ref.shape[0], 128):
             total = jnp.zeros((128, 128), jnp.float32)
             for column in range(0, width, 128):
@@ -70,15 +80,12 @@
     packed = jnp.concatenate(rows, axis=0)
     for copy in range(sums_ref.shape[0]):
         sums_ref[copy] = packed
-    mask_ref[...] = jnp.zeros_like(mask_ref)
+    wanted = []
     for distance, shifted in EXCHANGES:
-        offset, _ = partner(frame, distance, shifted)
         block = block_start(kept_ref, frame, frames, distance, shifted) // BS
-
-        @pl.when(is_live(frame, frames, distance, shifted))
-        def _():
-            mask_ref[frame + offset, pl.ds(block, 1), :] = jnp.ones((1, BS), jnp.float32)
-
+        wanted.append(jnp.full((1, BS), block, jnp.int32))
+    wanted_ref[...] = jnp.concatenate(wanted + [jnp.zeros((2, BS), jnp.int32)], axis=0)
+    copies[2].wait()
     first = block_refs[0]
     targets = [first.at[:BS], *block_refs[1:], first.at[BS:]]
     for (distance, shifted), block in zip(EXCHANGES, targets):
@@ -95,15 +102,26 @@
     return (block.astype(jnp.float32) * scale).astype(jnp.bfloat16)
 
 
-def norm_kernel(width_all, sums_ref, mask_ref, q_ref, k_ref, qn_ref, kn_ref, scale_ref):
+def norm_kernel(frames, width_all, sums_ref, wanted_ref, q_ref, k_ref, qn_ref, kn_ref, scale_ref):
     width = q_ref.shape[1]
     total = sums_ref[0]
     for part in range(1, sums_ref.shape[0]):
         total += sums_ref[part]
     scale = lax.rsqrt(total / width_all + norm_eps)
     key_scale = scale[q_ref.shape[0] // 128 :]
-    for frame in range(scale_ref.shape[0]):
-        scale_ref[frame] = jnp.sum(mask_ref[frame] * key_scale, axis=0, keepdims=True)
+    scale_ref[...] = jnp.zeros_like(scale_ref)
+    frame = lax.axis_index("frame")
+    for slot, (distance, shifted) in enumerate(EXCHANGES):
+        offset, _ = partner(frame, distance, shifted)
+        wanted = wanted_ref[slot : slot + 1, :]
+        chosen = key_scale[:1]
+        for row in range(1, key_scale.shape[0]):
+            chosen = jnp.where(wanted == row, key_scale[row : row + 1], chosen)
+
+        @pl.when(is_live(frame, frames, distance, shifted))
+        def _():
+            scale_ref[frame + offset] = chosen
+
     row = 0
     for ref, out in ((q_ref, qn_ref), (k_ref, kn_ref)):
         for start in range(0, ref.shape[0], 128):
@@ -127,7 +145,7 @@
 
 def attend_kernel(frames, scale_ref, q_ref, k_ref, v_ref, d_ref, *refs):
     far_refs = refs[:5]
-    att_ref, p_own, s_own, s_far, k_far = refs[5:10]
+    att_ref, w_own, stats, s_far, k_far = refs[5:10]
     back_refs = refs[10:16]
     v_far, p_far = refs[16:]
     frame = lax.axis_index("frame")
@@ -171,16 +189,17 @@
             far = jnp.where(allowed, dot(q_ref[rows, head], keys, CONTRACT_LAST), masked_score)
             top = jnp.maximum(jnp.max(own, axis=1, keepdims=True), jnp.max(far, axis=1, keepdims=True))
             own = jnp.exp2((own - top) * EXPONENT)
+            w_own[index, rows, :] = own
             far = jnp.exp2((far - top) * EXPONENT)
             share = 1.0 / (jnp.sum(own, axis=1, keepdims=True) + jnp.sum(far, axis=1, keepdims=True))
             own_low = (own * share).astype(jnp.bfloat16)
             far_low = (far * share).astype(jnp.bfloat16)
-            p_own[index, rows, :] = own_low
             p_far[rows, :] = far_low
             attended = (dot(own_low, v_ref[:, head]) + dot(far_low, vals)).astype(jnp.bfloat16)
             att_ref[rows, head] = attended
             inner = jnp.sum(grads.astype(f32) * attended.astype(f32), axis=1, keepdims=True)
-            s_own[index, rows, :] = (own * ((dot(grads, v_ref[:, head], CONTRACT_LAST) - inner) * share)).astype(jnp.bfloat16)
+            stats[rows, 2 * index : 2 * index + 1] = share
+            stats[rows, 2 * index + 1 : 2 * index + 2] = inner
             s_far[index, rows, :] = (far * ((dot(grads, vals, CONTRACT_LAST) - inner) * share)).astype(jnp.bfloat16)
         grad_k = dot(s_far[index], q_ref[:, head], CONTRACT_FIRST) * FACTOR
         grad_v = dot(p_far[...], d_ref[:, head], CONTRACT_FIRST)
@@ -190,13 +209,19 @@
             back[:, width + index * HD : width + (index + 1) * HD] = grad_v[rows].astype(jnp.bfloat16)
 
 
-def rest_kernel(p_own, s_own, s_far, k_far, q_ref, k_ref, d_ref, gq_ref, gk_ref, gv_ref):
+def rest_kernel(w_own, stats, s_far, k_far, q_ref, k_ref, v_ref, d_ref, gq_ref, gk_ref, gv_ref):
     for index in range(q_ref.shape[1] // HD):
         head = slice(index * HD, (index + 1) * HD)
-        grad_q = dot(s_own[index], k_ref[:, head]) + dot(s_far[index], k_far[:, head])
+        share = stats[:, 2 * index : 2 * index + 1]
+        inner = stats[:, 2 * index + 1 : 2 * index + 2]
+        weights = w_own[index]
+        probs = (weights * share).astype(jnp.bfloat16)
+        dprobs = dot(d_ref[:, head], v_ref[:, head], CONTRACT_LAST)
+        dscores = (weights * ((dprobs - inner) * share)).astype(jnp.bfloat16)
+        grad_q = dot(dscores, k_ref[:, head]) + dot(s_far[index], k_far[:, head])
         gq_ref[:, head] = (grad_q * FACTOR).astype(jnp.bfloat16)
-        gk_ref[:, head] = dot(s_own[index], q_ref[:, head], CONTRACT_FIRST) * FACTOR
-        gv_ref[:, head] = dot(p_own[index], d_ref[:, head], CONTRACT_FIRST)
+        gk_ref[:, head] = dot(dscores, q_ref[:, head], CONTRACT_FIRST) * FACTOR
+        gv_ref[:, head] = dot(probs, d_ref[:, head], CONTRACT_FIRST)
 
 
 def collect_kernel(frames, kept_ref, gk_ref, gv_ref, *refs):
@@ -247,39 +272,40 @@
     wide = jax.ShapeDtypeStruct((tokens, width), jnp.float32)
     block = jax.ShapeDtypeStruct((BS, 2 * width), jnp.bfloat16)
     pair = jax.ShapeDtypeStruct((2 * BS, 2 * width), jnp.bfloat16)
-    sums, mask, *sent = pl.pallas_call(
+    sums, wanted, *sent = pl.pallas_call(
         functools.partial(prepare_kernel, frames),
         out_shape=[
             jax.ShapeDtypeStruct((heads, stat_rows, 128), jnp.float32),
-            jax.ShapeDtypeStruct((frames, tokens // BS, BS), jnp.float32),
+            jax.ShapeDtypeStruct((8, BS), jnp.int32),
             pair,
         ]
         + [block] * 4,
-        in_specs=[SMEM] + [VMEM] * 3,
+        in_specs=[SMEM] + [ANY] * 3,
         out_specs=[VMEM] * 7,
-        compiler_params=params(8),
+        scratch_shapes=[pltpu.VMEM((tokens, width), jnp.bfloat16)] * 3 + [pltpu.SemaphoreType.DMA((3,))],
+        compiler_params=params(PREPARE_MIB),
         name="prepare",
     )(kept, queries, keys, values)
     sums = lax.all_to_all(sums, "head", 0, 0)
     far = swap_relayed(sent, frames)
     q_norm, k_norm, scales = pl.pallas_call(
-        functools.partial(norm_kernel, width * heads),
+        functools.partial(norm_kernel, frames, width * heads),
         out_shape=[flat, flat, jax.ShapeDtypeStruct((frames, 1, BS), jnp.float32)],
         in_specs=[VMEM] * 4,
         out_specs=[VMEM] * 3,
         compiler_params=params(8),
         name="normalize",
-    )(sums, mask, queries, keys)
+    )(sums, wanted, queries, keys)
     scales = lax.all_to_all(scales, "frame", 0, 0)
     heads_dev = width // HD
     own_shape = (heads_dev, tokens, tokens)
     own_flops = 2 * tokens * tokens * width
-    attended, own_p, own_s, far_s, far_k, *back = pl.pallas_call(
+    attended, own_w, stats, far_s, far_k, *back = pl.pallas_call(
         functools.partial(attend_kernel, frames),
         out_shape=[
             flat,
-            jax.ShapeDtypeStruct(own_shape, jnp.bfloat16),
-            jax.ShapeDtypeStruct(own_shape, jnp.bfloat16),
+            jax.ShapeDtypeStruct(own_shape, jnp.float32),
+            jax.ShapeDtypeStruct((tokens, 128), jnp.float32),
             jax.ShapeDtypeStruct((heads_dev, tokens, 6 * BS), jnp.bfloat16),
             jax.ShapeDtypeStruct((6 * BS, width), jnp.bfloat16),
         ]
@@ -296,12 +322,12 @@
     grad_q, own_k, own_v = pl.pallas_call(
         rest_kernel,
         out_shape=[flat, wide, wide],
-        in_specs=[VMEM] * 7,
+        in_specs=[VMEM] * 8,
         out_specs=[VMEM] * 3,
         compiler_params=params(8),
-        cost_estimate=pl.CostEstimate(flops=4 * own_flops, bytes_accessed=8 << 20, transcendentals=0),
+        cost_estimate=pl.CostEstimate(flops=6 * own_flops, bytes_accessed=8 << 20, transcendentals=0),
         name="rest",
-    )(own_p, own_s, far_s, far_k, q_norm, k_norm, cotangent)
+    )(own_w, stats, far_s, far_k, q_norm, k_norm, values, cotangent)
     back = swap(back, frames)
     grad_k, grad_v = pl.pallas_call(
         functools.partial(collect_kernel, frames),

time: 111 us -> 107 us (0.964)
  local copies, waits for them, and re-layouts: 3.56 us -> 0.8 us
    unnamed x18 -> x12, local copies, waits for them, and re-layouts: 3.55 us -> 0.79 us
  transfers between devices with their start and end apart: 13 -> 13, of which waited for: 5 -> 5; matrix products, arithmetic and copies ran while one was open for 1% -> 0% of each run, Pallas kernels for 3% -> 3%
where the time goes in v7:
time: 107 us
  starting transfers between devices  76.2 us (71%)
  waiting for transfers between devices  16.4 us (15%)
  Pallas kernels  12.6 us (12%)
    ppermute x11, starting transfers between devices, exchange(): return lax.ppermute(block, 'frame', route(*EXCHANGES[which], frames))  38.5 us
    all_to_all x1, starting transfers between devices, on_device(): sums = lax.all_to_all(sums, 'head', 0, 0)  24.5 us
    all_to_all x1, starting transfers between devices, on_device(): scales = lax.all_to_all(scales, 'frame', 0, 0)  13.2 us
    ppermute x11, waiting for transfers between devices, exchange(): return lax.ppermute(block, 'frame', route(*EXCHANGES[which], frames))  8.42 us
    all_to_all x1, waiting for transfers between devices, on_device(): scales = lax.all_to_all(scales, 'frame', 0, 0)  7.14 us
    pallas_call x1, Pallas kernels, on_device(): pl.pallas_call(functools.partial(attend_kernel, frames), out_shape=[flat,...  5.23 us
    pallas_call x1, Pallas kernels, on_device(): pl.pallas_call(rest_kernel, out_shape=[flat, wide, wide], in_specs=[VMEM]...  2.51 us
    pallas_call x1, Pallas kernels, on_device(): pl.pallas_call(functools.partial(prepare_kernel, frames), out_shape=[jax....  2.5 us
  transfers between devices with their start and end apart: 13, of which 5 were waited for; matrix products, arithmetic and copies ran while one was open for 0% of the time, Pallas kernels for 3%

profile of v7, /device:TPU:10, one launch (start us, length us, event | category | flops | bytes accessed | tf_op | source)
XLA Modules:
  0.0 106.9 jit_solution(3541613954827877201)
XLA Ops:
  0.7 0.0 copy-start.4
  0.7 0.8 copy-done.4
  1.4 2.5 %prepare.1 = (f32[16,8,128]{2,1,0:T(8,128)}, s32[8,128]{1,0:T(8,128)S(1)}, bf16[256,512]{1,0:T(8,128)(2,1)S(1)}, bf16[128,512]{1,0:T(8,128)(2,1)S(1)}, bf16[128,...) custom-call(s32[6,64]{1,0:T(8,128)S(1)} %bitcast.1, bf16[512,256]{1,0:T(8,128)(2,1)} %q_ref.1, ...), custom_call_target="tpu_custom_call" | custom-call | tf_op jit(solution)/shard_map/prepare/pallas_call | solution.py:275
  3.9 1.9 %collective-permute-start = (bf16[256,512]{1,0:T(8,128)(2,1)S(1)}, bf16[256,512]{1,0:T(8,128)(2,1)S(1)}, u32[]{:S(2)}, u32[]{:S(2)}) collective-permute-start(bf16[256,512]{1,0:T(8,128)(2,1)S(1)} %get-tuple-element.35), channel_id=1, source_target_pairs={{0,16},{16,0},{32,48},{48,32},{64,80},{80,64},{96,112},{112,96},{1... | collective-permute-start | bytes 786440 | tf_op jit(solution)/shard_map/ppermute | solution.py:247
  5.9 24.5 %all-to-all-start = ((f32[16,8,128]{2,1,0:T(8,128)}), f32[16,8,128]{2,1,0:T(8,128)S(1)}, u32[]{:S(2)}, u32[]{:S(2)}) async-start(f32[16,8,128]{2,1,0:T(8,128)} %get-tuple-element.30), calls=%async_computation | async-start | bytes 131072 | tf_op jit(solution)/shard_map/all_to_all | solution.py:289
  30.4 3.4 %collective-permute-start.4 = (bf16[256,512]{1,0:T(8,128)(2,1)S(1)}, bf16[256,512]{1,0:T(8,128)(2,1)S(1)}, u32[]{:S(2)}, u32[]{:S(2)}) collective-permute-start(bf16[256,512]{1,0:T(8,128)(2,1)S(1)} %get-tuple-element.56), channel_id=1, source_target_pairs={{0,32},{32,0},{16,48},{48,16},{64,96},{96,64},{80,112},{112,80},{1... | collective-permute-start | bytes 786440 | tf_op jit(solution)/shard_map/ppermute | solution.py:247
  33.8 7.9 %collective-permute-start.3 = (bf16[256,512]{1,0:T(8,128)(2,1)S(1)}, bf16[256,512]{1,0:T(8,128)(2,1)S(1)}, u32[]{:S(2)}, u32[]{:S(2)}) collective-permute-start(bf16[256,512]{1,0:T(8,128)(2,1)S(1)} %get-tuple-element.57), channel_id=1, source_target_pairs={{32,64},{64,32},{48,80},{80,48},{96,128},{128,96},{112,144},{144,1... | collective-permute-start | bytes 786440 | tf_op jit(solution)/shard_map/ppermute | solution.py:247
  41.7 1.9 %collective-permute-start.1 = (bf16[128,512]{1,0:T(8,128)(2,1)S(1)}, bf16[128,512]{1,0:T(8,128)(2,1)S(1)}, u32[]{:S(2)}, u32[]{:S(2)}) collective-permute-start(bf16[128,512]{1,0:T(8,128)(2,1)S(1)} %get-tuple-element.36), channel_id=1, source_target_pairs={{64,128},{128,64},{80,144},{144,80},{96,160},{160,96},{112,176},{1... | collective-permute-start | bytes 393224 | tf_op jit(solution)/shard_map/ppermute | solution.py:247
  43.6 1.9 %collective-permute-start.2 = (bf16[128,512]{1,0:T(8,128)(2,1)S(1)}, bf16[128,512]{1,0:T(8,128)(2,1)S(1)}, u32[]{:S(2)}, u32[]{:S(2)}) collective-permute-start(bf16[128,512]{1,0:T(8,128)(2,1)S(1)} %get-tuple-element.37), channel_id=1, source_target_pairs={{0,64},{64,0},{16,80},{80,16},{32,96},{96,32},{48,112},{112,48},{1... | collective-permute-start | bytes 393224 | tf_op jit(solution)/shard_map/ppermute | solution.py:247
  45.6 0.9 all-to-all-done.sums_ref
  46.4 0.7 normalize.1
  47.1 13.2 %all-to-all-start.1 = ((f32[64,1,128]{2,1,0:T(1,128)}), f32[64,1,128]{2,1,0:T(1,128)S(1)}, u32[]{:S(2)}, u32[]{:S(2)}) async-start(f32[64,1,128]{2,1,0:T(1,128)} %get-tuple-element.32), calls=%async_computation.1 | async-start | bytes 65536 | tf_op jit(solution)/shard_map/all_to_all | solution.py:299
  60.3 4.3 %collective-permute-done.1.refs_1_ = bf16[128,512]{1,0:T(8,128)(2,1)S(1)} collective-permute-done((bf16[128,512]{1,0:T(8,128)(2,1)S(1)}, bf16[128,512]{1,0:T(8,128)(2,1)S(1)}, u32[]{:S(2)}, u32[]{:S(2)}) %collective-permute-start.1) | collective-permute-done | bytes 131104 | tf_op jit(solution)/shard_map/ppermute | solution.py:247
  64.6 0.0 collective-permute-done.2.refs_2_
  64.6 7.1 %all-to-all-done.1.scale_ref = f32[64,1,128]{2,1,0:T(1,128)S(1)} async-done(((f32[64,1,128]{2,1,0:T(1,128)}), f32[64,1,128]{2,1,0:T(1,128)S(1)}, u32[]{:S(2)}, u32[]{:S(2)}) %all-to-all-start.1) | async-done | bytes 32800 | tf_op jit(solution)/shard_map/all_to_all | solution.py:299
  71.8 0.0 collective-permute-done.4.refs_4_
  71.8 0.0 collective-permute-done.3.refs_3_
  71.8 5.2 %attend.1 = (bf16[512,256]{1,0:T(8,128)(2,1)}, f32[2,512,512]{2,1,0:T(8,128)S(1)}, f32[512,128]{1,0:T(8,128)S(1)}, bf16[2,512,768]{2,1,0:T(8,128)(2,1)S(1)}, bf1...) custom-call(f32[64,1,128]{2,1,0:T(1,128)S(1)} %all-to-all-done.1.sca, ...), custom_call_target="tpu_custom_call" | custom-call | tf_op jit(solution)/shard_map/attend/pallas_call | solution.py:303
  77.0 3.5 %collective-permute-start.5 = (bf16[128,512]{1,0:T(8,128)(2,1)S(1)}, bf16[128,512]{1,0:T(8,128)(2,1)S(1)}, u32[]{:S(2)}, u32[]{:S(2)}) collective-permute-start(bf16[128,512]{1,0:T(8,128)(2,1)S(1)} %get-tuple-element.48), channel_id=1, source_target_pairs={{64,128},{128,64},{80,144},{144,80},{96,160},{160,96},{112,176},{1... | collective-permute-start | bytes 393224 | tf_op jit(solution)/shard_map/ppermute | solution.py:247
  80.5 8.7 %collective-permute-start.6 = (bf16[128,512]{1,0:T(8,128)(2,1)S(1)}, bf16[128,512]{1,0:T(8,128)(2,1)S(1)}, u32[]{:S(2)}, u32[]{:S(2)}) collective-permute-start(bf16[128,512]{1,0:T(8,128)(2,1)S(1)} %get-tuple-element.49), channel_id=1, source_target_pairs={{32,64},{64,32},{48,80},{80,48},{96,128},{128,96},{112,144},{144,1... | collective-permute-start | bytes 393224 | tf_op jit(solution)/shard_map/ppermute | solution.py:247
  89.2 3.6 %collective-permute-start.7 = (bf16[128,512]{1,0:T(8,128)(2,1)S(1)}, bf16[128,512]{1,0:T(8,128)(2,1)S(1)}, u32[]{:S(2)}, u32[]{:S(2)}) collective-permute-start(bf16[128,512]{1,0:T(8,128)(2,1)S(1)} %get-tuple-element.50), channel_id=1, source_target_pairs={{16,32},{32,16},{48,64},{64,48},{80,96},{96,80},{112,128},{128,112... | collective-permute-start | bytes 393224 | tf_op jit(solution)/shard_map/ppermute | solution.py:247
  92.7 1.9 %collective-permute-start.8 = (bf16[128,512]{1,0:T(8,128)(2,1)S(1)}, bf16[128,512]{1,0:T(8,128)(2,1)S(1)}, u32[]{:S(2)}, u32[]{:S(2)}) collective-permute-start(bf16[128,512]{1,0:T(8,128)(2,1)S(1)} %get-tuple-element.51), channel_id=1, source_target_pairs={{0,64},{64,0},{16,80},{80,16},{32,96},{96,32},{48,112},{112,48},{1... | collective-permute-start | bytes 393224 | tf_op jit(solution)/shard_map/ppermute | solution.py:247
  94.7 1.9 %collective-permute-start.9 = (bf16[128,512]{1,0:T(8,128)(2,1)S(1)}, bf16[128,512]{1,0:T(8,128)(2,1)S(1)}, u32[]{:S(2)}, u32[]{:S(2)}) collective-permute-start(bf16[128,512]{1,0:T(8,128)(2,1)S(1)} %get-tuple-element.52), channel_id=1, source_target_pairs={{0,32},{32,0},{16,48},{48,16},{64,96},{96,64},{80,112},{112,80},{1... | collective-permute-start | bytes 393224 | tf_op jit(solution)/shard_map/ppermute | solution.py:247
  96.6 1.9 %collective-permute-start.10 = (bf16[128,512]{1,0:T(8,128)(2,1)S(1)}, bf16[128,512]{1,0:T(8,128)(2,1)S(1)}, u32[]{:S(2)}, u32[]{:S(2)}) collective-permute-start(bf16[128,512]{1,0:T(8,128)(2,1)S(1)} %get-tuple-element.53), channel_id=1, source_target_pairs={{0,16},{16,0},{32,48},{48,32},{64,80},{80,64},{96,112},{112,96},{1... | collective-permute-start | bytes 393224 | tf_op jit(solution)/shard_map/ppermute | solution.py:247
  98.5 0.0 copy-start.5
  98.5 2.5 %rest.1 = (bf16[512,256]{1,0:T(8,128)(2,1)}, f32[512,256]{1,0:T(8,128)S(1)}, f32[512,256]{1,0:T(8,128)S(1)}) custom-call(f32[2,512,512]{2,1,0:T(8,128)S(1)} %get-tuple-element.41.w_own, f32[512,128]{1,0:T(8,128)S(1)} %get-tuple-element.42.stats, bf16[2,512,768]{2,1,0:T(8,128)(2,1)S(1)} %get-tuple-element.43.s_far, ...), custom_call_target="tpu_custom_call" | custom-call | flops 805306368 | bytes 8388608 | tf_op jit(solution)/shard_map/rest/pallas_call | solution.py:322
  101.1 0.0 collective-permute-done.6.refs_1_
  101.1 2.2 %collective-permute-done.7.refs_2_ = bf16[128,512]{1,0:T(8,128)(2,1)S(1)} collective-permute-done((bf16[128,512]{1,0:T(8,128)(2,1)S(1)}, bf16[128,512]{1,0:T(8,128)(2,1)S(1)}, u32[]{:S(2)}, u32[]{:S(2)}) %collective-permute-start.7) | collective-permute-done | bytes 131104 | tf_op jit(solution)/shard_map/ppermute | solution.py:247
  103.3 1.9 %collective-permute-done.8.refs_3_ = bf16[128,512]{1,0:T(8,128)(2,1)S(1)} collective-permute-done((bf16[128,512]{1,0:T(8,128)(2,1)S(1)}, bf16[128,512]{1,0:T(8,128)(2,1)S(1)}, u32[]{:S(2)}, u32[]{:S(2)}) %collective-permute-start.8) | collective-permute-done | bytes 131104 | tf_op jit(solution)/shard_map/ppermute | solution.py:247
  105.2 0.0 collective-permute-done.9.refs_4_
  105.2 0.0 collective-permute-done.10.refs_5_
  105.2 1.7 %collect.1 = (bf16[512,256]{1,0:T(8,128)(2,1)}, bf16[512,256]{1,0:T(8,128)(2,1)}) custom-call(s32[6,64]{1,0:T(8,128)S(1)} %bitcast.2, f32[512,256]{1,0:T(8,128)S(1)} %get-tuple-element.46.gk_ref, f32[512,256]{1,0:T(8,128)S(1)} %get-tuple-element.47.gv_ref, bf16[128,512]{1,0:T(8,128)(2,1)S(1)} %collective-permute-done.5.refs_0_, ...), custom_call_target="tpu_custom_call" | custom-call | tf_op jit(solution)/shard_map/collect/pallas_call | solution.py:332
  (13 shorter events, 0.1 us)
Async XLA Ops:
  0.6 71.1 %copy-start = (bf16[512,256]{1,0:T(8,128)(2,1)S(1)}, bf16[512,256]{1,0:T(8,128)(2,1)}, u32[]{:S(2)}) copy-start(bf16[512,256]{1,0:T(8,128)(2,1)} %v_ref.3) | copy-start | bytes 786436
  0.6 45.8 %copy-start.2 = (bf16[512,256]{1,0:T(8,128)(2,1)S(1)}, bf16[512,256]{1,0:T(8,128)(2,1)}, u32[]{:S(2)}) copy-start(bf16[512,256]{1,0:T(8,128)(2,1)} %k_ref.1) | copy-start | bytes 786436
  0.7 45.8 %copy-start.1 = (bf16[512,256]{1,0:T(8,128)(2,1)S(1)}, bf16[512,256]{1,0:T(8,128)(2,1)}, u32[]{:S(2)}) copy-start(bf16[512,256]{1,0:T(8,128)(2,1)} %q_ref.1) | copy-start | bytes 786436
  0.7 71.1 %copy-start.3 = (bf16[512,256]{1,0:T(8,128)(2,1)S(1)}, bf16[512,256]{1,0:T(8,128)(2,1)}, u32[]{:S(2)}) copy-start(bf16[512,256]{1,0:T(8,128)(2,1)} %d_ref.3) | copy-start | bytes 786436
  0.7 0.8 copy-start.4
  3.9 26.4 %collective-permute-start = (bf16[256,512]{1,0:T(8,128)(2,1)S(1)}, bf16[256,512]{1,0:T(8,128)(2,1)S(1)}, u32[]{:S(2)}, u32[]{:S(2)}) collective-permute-start(bf16[256,512]{1,0:T(8,128)(2,1)S(1)} %get-tuple-element.35), channel_id=1, source_target_pairs={{0,16},{16,0},{32,48},{48,32},{64,80},{80,64},{96,112},{112,96},{1... | collective-permute-start | bytes 786440 | tf_op jit(solution)/shard_map/ppermute | solution.py:247
  5.9 40.6 %all-to-all-start = ((f32[16,8,128]{2,1,0:T(8,128)}), f32[16,8,128]{2,1,0:T(8,128)S(1)}, u32[]{:S(2)}, u32[]{:S(2)}) async-start(f32[16,8,128]{2,1,0:T(8,128)} %get-tuple-element.30), calls=%async_computation | async-start | bytes 131072 | tf_op jit(solution)/shard_map/all_to_all | solution.py:289
  30.4 41.4 %collective-permute-start.4 = (bf16[256,512]{1,0:T(8,128)(2,1)S(1)}, bf16[256,512]{1,0:T(8,128)(2,1)S(1)}, u32[]{:S(2)}, u32[]{:S(2)}) collective-permute-start(bf16[256,512]{1,0:T(8,128)(2,1)S(1)} %get-tuple-element.56), channel_id=1, source_target_pairs={{0,32},{32,0},{16,48},{48,16},{64,96},{96,64},{80,112},{112,80},{1... | collective-permute-start | bytes 786440 | tf_op jit(solution)/shard_map/ppermute | solution.py:247
  33.8 38.0 %collective-permute-start.3 = (bf16[256,512]{1,0:T(8,128)(2,1)S(1)}, bf16[256,512]{1,0:T(8,128)(2,1)S(1)}, u32[]{:S(2)}, u32[]{:S(2)}) collective-permute-start(bf16[256,512]{1,0:T(8,128)(2,1)S(1)} %get-tuple-element.57), channel_id=1, source_target_pairs={{32,64},{64,32},{48,80},{80,48},{96,128},{128,96},{112,144},{144,1... | collective-permute-start | bytes 786440 | tf_op jit(solution)/shard_map/ppermute | solution.py:247
  41.7 22.9 %collective-permute-start.1 = (bf16[128,512]{1,0:T(8,128)(2,1)S(1)}, bf16[128,512]{1,0:T(8,128)(2,1)S(1)}, u32[]{:S(2)}, u32[]{:S(2)}) collective-permute-start(bf16[128,512]{1,0:T(8,128)(2,1)S(1)} %get-tuple-element.36), channel_id=1, source_target_pairs={{64,128},{128,64},{80,144},{144,80},{96,160},{160,96},{112,176},{1... | collective-permute-start | bytes 393224 | tf_op jit(solution)/shard_map/ppermute | solution.py:247
  43.6 21.0 %collective-permute-start.2 = (bf16[128,512]{1,0:T(8,128)(2,1)S(1)}, bf16[128,512]{1,0:T(8,128)(2,1)S(1)}, u32[]{:S(2)}, u32[]{:S(2)}) collective-permute-start(bf16[128,512]{1,0:T(8,128)(2,1)S(1)} %get-tuple-element.37), channel_id=1, source_target_pairs={{0,64},{64,0},{16,80},{80,16},{32,96},{96,32},{48,112},{112,48},{1... | collective-permute-start | bytes 393224 | tf_op jit(solution)/shard_map/ppermute | solution.py:247
  47.1 24.6 %all-to-all-start.1 = ((f32[64,1,128]{2,1,0:T(1,128)}), f32[64,1,128]{2,1,0:T(1,128)S(1)}, u32[]{:S(2)}, u32[]{:S(2)}) async-start(f32[64,1,128]{2,1,0:T(1,128)} %get-tuple-element.32), calls=%async_computation.1 | async-start | bytes 65536 | tf_op jit(solution)/shard_map/all_to_all | solution.py:299
  77.0 19.6 %collective-permute-start.5 = (bf16[128,512]{1,0:T(8,128)(2,1)S(1)}, bf16[128,512]{1,0:T(8,128)(2,1)S(1)}, u32[]{:S(2)}, u32[]{:S(2)}) collective-permute-start(bf16[128,512]{1,0:T(8,128)(2,1)S(1)} %get-tuple-element.48), channel_id=1, source_target_pairs={{64,128},{128,64},{80,144},{144,80},{96,160},{160,96},{112,176},{1... | collective-permute-start | bytes 393224 | tf_op jit(solution)/shard_map/ppermute | solution.py:247
  80.5 20.6 %collective-permute-start.6 = (bf16[128,512]{1,0:T(8,128)(2,1)S(1)}, bf16[128,512]{1,0:T(8,128)(2,1)S(1)}, u32[]{:S(2)}, u32[]{:S(2)}) collective-permute-start(bf16[128,512]{1,0:T(8,128)(2,1)S(1)} %get-tuple-element.49), channel_id=1, source_target_pairs={{32,64},{64,32},{48,80},{80,48},{96,128},{128,96},{112,144},{144,1... | collective-permute-start | bytes 393224 | tf_op jit(solution)/shard_map/ppermute | solution.py:247
  89.2 14.1 %collective-permute-start.7 = (bf16[128,512]{1,0:T(8,128)(2,1)S(1)}, bf16[128,512]{1,0:T(8,128)(2,1)S(1)}, u32[]{:S(2)}, u32[]{:S(2)}) collective-permute-start(bf16[128,512]{1,0:T(8,128)(2,1)S(1)} %get-tuple-element.50), channel_id=1, source_target_pairs={{16,32},{32,16},{48,64},{64,48},{80,96},{96,80},{112,128},{128,112... | collective-permute-start | bytes 393224 | tf_op jit(solution)/shard_map/ppermute | solution.py:247
  92.7 12.4 %collective-permute-start.8 = (bf16[128,512]{1,0:T(8,128)(2,1)S(1)}, bf16[128,512]{1,0:T(8,128)(2,1)S(1)}, u32[]{:S(2)}, u32[]{:S(2)}) collective-permute-start(bf16[128,512]{1,0:T(8,128)(2,1)S(1)} %get-tuple-element.51), channel_id=1, source_target_pairs={{0,64},{64,0},{16,80},{80,16},{32,96},{96,32},{48,112},{112,48},{1... | collective-permute-start | bytes 393224 | tf_op jit(solution)/shard_map/ppermute | solution.py:247
  94.7 10.5 %collective-permute-start.9 = (bf16[128,512]{1,0:T(8,128)(2,1)S(1)}, bf16[128,512]{1,0:T(8,128)(2,1)S(1)}, u32[]{:S(2)}, u32[]{:S(2)}) collective-permute-start(bf16[128,512]{1,0:T(8,128)(2,1)S(1)} %get-tuple-element.52), channel_id=1, source_target_pairs={{0,32},{32,0},{16,48},{48,16},{64,96},{96,64},{80,112},{112,80},{1... | collective-permute-start | bytes 393224 | tf_op jit(solution)/shard_map/ppermute | solution.py:247
  96.6 8.6 %collective-permute-start.10 = (bf16[128,512]{1,0:T(8,128)(2,1)S(1)}, bf16[128,512]{1,0:T(8,128)(2,1)S(1)}, u32[]{:S(2)}, u32[]{:S(2)}) collective-permute-start(bf16[128,512]{1,0:T(8,128)(2,1)S(1)} %get-tuple-element.53), channel_id=1, source_target_pairs={{0,16},{16,0},{32,48},{48,32},{64,80},{80,64},{96,112},{112,96},{1... | collective-permute-start | bytes 393224 | tf_op jit(solution)/shard_map/ppermute | solution.py:247
  98.5 6.6 %copy-start.5 = (s32[64,6]{0,1:T(8,128)S(1)}, s32[64,6]{0,1:T(8,128)}, u32[]{:S(2)}) copy-start(s32[64,6]{0,1:T(8,128)} %param.9) | copy-start | bytes 4612

commit v8 on v7

--- a/solution.py
+++ b/solution.py
@@ -136,7 +136,7 @@
 CONTRACT_FIRST = (((0,), (0,)), ((), ()))
 FACTOR = 1.0 / math.sqrt(HD)
 EXPONENT = FACTOR * math.log2(math.e)
-CHUNK = 256
+CHUNK = 512
 
 
 def dot(left, right, dims=(((1,), (0,)), ((), ()))):
@@ -201,8 +201,8 @@
             stats[rows, 2 * index : 2 * index + 1] = share
             stats[rows, 2 * index + 1 : 2 * index + 2] = inner
             s_far[index, rows, :] = (far * ((dot(grads, vals, CONTRACT_LAST) - inner) * share)).astype(jnp.bfloat16)
-        grad_k = dot(s_far[index], q_ref[:, head], CONTRACT_FIRST) * FACTOR
-        grad_v = dot(p_far[...], d_ref[:, head], CONTRACT_FIRST)
+        grad_k = dot(q_ref[:, head].T, s_far[index]).T * FACTOR
+        grad_v = dot(d_ref[:, head].T, p_far[...]).T
         for slot, back in zip(RETURN_ORDER, back_refs):
             rows = slice(slot * BS, (slot + 1) * BS)
             back[:, index * HD : (index + 1) * HD] = grad_k[rows].astype(jnp.bfloat16)
@@ -252,7 +252,7 @@
     got_first = exchange(first, frames, 0)
     got_wide_far = exchange(wide_far, frames, 1)
     got_near_far = exchange(near_far, frames, 2)
-    relay = got_first[BS:]
+    relay, got_near_far, got_wide_far = lax.optimization_barrier((got_first[BS:], got_near_far, got_wide_far))
     got_wide_two = exchange(jnp.concatenate([wide_two, relay]), frames, 3)
     got_near_two = exchange(jnp.concatenate([near_two, relay]), frames, 4)
     return got_first, got_wide_far, got_near_far, got_wide_two, got_near_two

time: 107 us -> 114 us (1.065)
  the two profiles are of different devices: /device:TPU:10 before, /device:TPU:2 now
where the time goes in v8:
time: 114 us; the launch traced here: 113 us
  starting transfers between devices  67.4 us (59%)
  blocking collectives  21.3 us (19%)
  Pallas kernels  11.9 us (10%)
  waiting for transfers between devices  11 us (10%)
    ppermute x11, starting transfers between devices, exchange(): return lax.ppermute(block, 'frame', route(*EXCHANGES[which], frames))  49.3 us
    all_to_all x1, blocking collectives, on_device(): scales = lax.all_to_all(scales, 'frame', 0, 0)  21.3 us
    all_to_all x1, starting transfers between devices, on_device(): sums = lax.all_to_all(sums, 'head', 0, 0)  18 us
    all_to_all x1, waiting for transfers between devices, on_device(): sums = lax.all_to_all(sums, 'head', 0, 0)  7.47 us
    pallas_call x1, Pallas kernels, on_device(): pl.pallas_call(functools.partial(attend_kernel, frames), out_shape=[flat,...  4.98 us
    ppermute x11, waiting for transfers between devices, exchange(): return lax.ppermute(block, 'frame', route(*EXCHANGES[which], frames))  3.57 us
    pallas_call x1, Pallas kernels, on_device(): pl.pallas_call(rest_kernel, out_shape=[flat, wide, wide], in_specs=[VMEM]...  2.51 us
    pallas_call x1, Pallas kernels, on_device(): pl.pallas_call(functools.partial(prepare_kernel, frames), out_shape=[jax....  2.5 us
  transfers between devices with their start and end apart: 12, of which 3 were waited for; matrix products, arithmetic and copies ran while one was open for 0% of the time, Pallas kernels for 2%

profile of v8, /device:TPU:2, one launch (start us, length us, event | category | flops | bytes accessed | tf_op | source)
XLA Modules:
  0.0 113.3 jit_solution(6256766376975123098)
XLA Ops:
  0.7 0.0 copy-start.4
  0.7 0.8 copy-done.4
  1.4 2.5 %prepare.1 = (f32[16,8,128]{2,1,0:T(8,128)}, s32[8,128]{1,0:T(8,128)S(1)}, bf16[256,512]{1,0:T(8,128)(2,1)S(1)}, bf16[128,512]{1,0:T(8,128)(2,1)S(1)}, bf16[128,...) custom-call(s32[6,64]{1,0:T(8,128)S(1)} %bitcast.1, bf16[512,256]{1,0:T(8,128)(2,1)} %q_ref.1, ...), custom_call_target="tpu_custom_call" | custom-call | tf_op jit(solution)/shard_map/prepare/pallas_call | solution.py:275
  3.9 1.9 %collective-permute-start = (bf16[256,512]{1,0:T(8,128)(2,1)S(1)}, bf16[256,512]{1,0:T(8,128)(2,1)S(1)}, u32[]{:S(2)}, u32[]{:S(2)}) collective-permute-start(bf16[256,512]{1,0:T(8,128)(2,1)S(1)} %get-tuple-element.38), channel_id=1, source_target_pairs={{0,16},{16,0},{32,48},{48,32},{64,80},{80,64},{96,112},{112,96},{1... | collective-permute-start | bytes 786440 | tf_op jit(solution)/shard_map/ppermute | solution.py:247
  5.9 6.1 %collective-permute-start.1 = (bf16[128,512]{1,0:T(8,128)(2,1)S(1)}, bf16[128,512]{1,0:T(8,128)(2,1)S(1)}, u32[]{:S(2)}, u32[]{:S(2)}) collective-permute-start(bf16[128,512]{1,0:T(8,128)(2,1)S(1)} %get-tuple-element.39), channel_id=1, source_target_pairs={{0,64},{64,0},{16,80},{80,16},{32,96},{96,32},{48,112},{112,48},{1... | collective-permute-start | bytes 393224 | tf_op jit(solution)/shard_map/ppermute | solution.py:247
  12.0 10.3 %collective-permute-start.2 = (bf16[128,512]{1,0:T(8,128)(2,1)S(1)}, bf16[128,512]{1,0:T(8,128)(2,1)S(1)}, u32[]{:S(2)}, u32[]{:S(2)}) collective-permute-start(bf16[128,512]{1,0:T(8,128)(2,1)S(1)} %get-tuple-element.40), channel_id=1, source_target_pairs={{64,128},{128,64},{80,144},{144,80},{96,160},{160,96},{112,176},{1... | collective-permute-start | bytes 393224 | tf_op jit(solution)/shard_map/ppermute | solution.py:247
  22.3 18.0 %all-to-all-start = ((f32[16,8,128]{2,1,0:T(8,128)}), f32[16,8,128]{2,1,0:T(8,128)S(1)}, u32[]{:S(2)}, u32[]{:S(2)}) async-start(f32[16,8,128]{2,1,0:T(8,128)} %get-tuple-element.33), calls=%async_computation | async-start | bytes 131072 | tf_op jit(solution)/shard_map/all_to_all | solution.py:289
  40.4 0.0 collective-permute-done.refs_0_
  40.4 0.0 collective-permute-done.1.refs_2_
  40.4 0.0 collective-permute-done.2.refs_1_
  40.5 3.4 %collective-permute-start.4 = (bf16[256,512]{1,0:T(8,128)(2,1)S(1)}, bf16[256,512]{1,0:T(8,128)(2,1)S(1)}, u32[]{:S(2)}, u32[]{:S(2)}) collective-permute-start(bf16[256,512]{1,0:T(8,128)(2,1)S(1)} %get-tuple-element.62), channel_id=1, source_target_pairs={{0,32},{32,0},{16,48},{48,16},{64,96},{96,64},{80,112},{112,80},{1... | collective-permute-start | bytes 786440 | tf_op jit(solution)/shard_map/ppermute | solution.py:247
  43.8 6.4 %collective-permute-start.3 = (bf16[256,512]{1,0:T(8,128)(2,1)S(1)}, bf16[256,512]{1,0:T(8,128)(2,1)S(1)}, u32[]{:S(2)}, u32[]{:S(2)}) collective-permute-start(bf16[256,512]{1,0:T(8,128)(2,1)S(1)} %get-tuple-element.63), channel_id=1, source_target_pairs={{32,64},{64,32},{48,80},{80,48},{96,128},{128,96},{112,144},{144,1... | collective-permute-start | bytes 786440 | tf_op jit(solution)/shard_map/ppermute | solution.py:247
  50.2 7.5 %all-to-all-done.sums_ref = f32[16,8,128]{2,1,0:T(8,128)S(1)} async-done(((f32[16,8,128]{2,1,0:T(8,128)}), f32[16,8,128]{2,1,0:T(8,128)S(1)}, u32[]{:S(2)}, u32[]{:S(2)}) %all-to-all-start) | async-done | bytes 65568 | tf_op jit(solution)/shard_map/all_to_all | solution.py:289
  57.7 0.3 normalize.1
  58.0 21.3 %all_to_all.10.scale_ref = f32[64,1,128]{2,1,0:T(1,128)S(1)} all-to-all(f32[64,1,128]{2,1,0:T(1,128)S(1)} %get-tuple-element.35), channel_id=1, replica_groups=mesh['frame'=64,'head'=16] {'frame'}, dimensions={0} | all-to-all | bytes 65536 | tf_op jit(solution)/shard_map/all_to_all | solution.py:299
  79.3 0.0 collective-permute-done.4.refs_4_
  79.3 0.0 collective-permute-done.3.refs_3_
  79.3 5.0 %attend.1 = (bf16[512,256]{1,0:T(8,128)(2,1)}, f32[2,512,512]{2,1,0:T(8,128)S(1)}, f32[512,128]{1,0:T(8,128)S(1)}, bf16[2,512,768]{2,1,0:T(8,128)(2,1)S(1)}, bf1...) custom-call(f32[64,1,128]{2,1,0:T(1,128)S(1)} %all_to_all.10.scale_r, ...), custom_call_target="tpu_custom_call" | custom-call | tf_op jit(solution)/shard_map/attend/pallas_call | solution.py:303
  84.3 3.2 %collective-permute-start.5 = (bf16[128,512]{1,0:T(8,128)(2,1)S(1)}, bf16[128,512]{1,0:T(8,128)(2,1)S(1)}, u32[]{:S(2)}, u32[]{:S(2)}) collective-permute-start(bf16[128,512]{1,0:T(8,128)(2,1)S(1)} %get-tuple-element.54), channel_id=1, source_target_pairs={{64,128},{128,64},{80,144},{144,80},{96,160},{160,96},{112,176},{1... | collective-permute-start | bytes 393224 | tf_op jit(solution)/shard_map/ppermute | solution.py:247
  87.5 8.9 %collective-permute-start.6 = (bf16[128,512]{1,0:T(8,128)(2,1)S(1)}, bf16[128,512]{1,0:T(8,128)(2,1)S(1)}, u32[]{:S(2)}, u32[]{:S(2)}) collective-permute-start(bf16[128,512]{1,0:T(8,128)(2,1)S(1)} %get-tuple-element.55), channel_id=1, source_target_pairs={{32,64},{64,32},{48,80},{80,48},{96,128},{128,96},{112,144},{144,1... | collective-permute-start | bytes 393224 | tf_op jit(solution)/shard_map/ppermute | solution.py:247
  96.4 3.3 %collective-permute-start.7 = (bf16[128,512]{1,0:T(8,128)(2,1)S(1)}, bf16[128,512]{1,0:T(8,128)(2,1)S(1)}, u32[]{:S(2)}, u32[]{:S(2)}) collective-permute-start(bf16[128,512]{1,0:T(8,128)(2,1)S(1)} %get-tuple-element.56), channel_id=1, source_target_pairs={{16,32},{32,16},{48,64},{64,48},{80,96},{96,80},{112,128},{128,112... | collective-permute-start | bytes 393224 | tf_op jit(solution)/shard_map/ppermute | solution.py:247
  99.8 1.9 %collective-permute-start.8 = (bf16[128,512]{1,0:T(8,128)(2,1)S(1)}, bf16[128,512]{1,0:T(8,128)(2,1)S(1)}, u32[]{:S(2)}, u32[]{:S(2)}) collective-permute-start(bf16[128,512]{1,0:T(8,128)(2,1)S(1)} %get-tuple-element.57), channel_id=1, source_target_pairs={{0,64},{64,0},{16,80},{80,16},{32,96},{96,32},{48,112},{112,48},{1... | collective-permute-start | bytes 393224 | tf_op jit(solution)/shard_map/ppermute | solution.py:247
  101.7 1.9 %collective-permute-start.9 = (bf16[128,512]{1,0:T(8,128)(2,1)S(1)}, bf16[128,512]{1,0:T(8,128)(2,1)S(1)}, u32[]{:S(2)}, u32[]{:S(2)}) collective-permute-start(bf16[128,512]{1,0:T(8,128)(2,1)S(1)} %get-tuple-element.58), channel_id=1, source_target_pairs={{0,32},{32,0},{16,48},{48,16},{64,96},{96,64},{80,112},{112,80},{1... | collective-permute-start | bytes 393224 | tf_op jit(solution)/shard_map/ppermute | solution.py:247
  103.6 0.0 collective-permute-done.5.refs_0_
  103.6 1.9 %collective-permute-start.10 = (bf16[128,512]{1,0:T(8,128)(2,1)S(1)}, bf16[128,512]{1,0:T(8,128)(2,1)S(1)}, u32[]{:S(2)}, u32[]{:S(2)}) collective-permute-start(bf16[128,512]{1,0:T(8,128)(2,1)S(1)} %get-tuple-element.59), channel_id=1, source_target_pairs={{0,16},{16,0},{32,48},{48,32},{64,80},{80,64},{96,112},{112,96},{1... | collective-permute-start | bytes 393224 | tf_op jit(solution)/shard_map/ppermute | solution.py:247
  105.5 0.0 copy-start.5
  105.6 2.5 %rest.1 = (bf16[512,256]{1,0:T(8,128)(2,1)}, f32[512,256]{1,0:T(8,128)S(1)}, f32[512,256]{1,0:T(8,128)S(1)}) custom-call(f32[2,512,512]{2,1,0:T(8,128)S(1)} %get-tuple-element.47.w_own, f32[512,128]{1,0:T(8,128)S(1)} %get-tuple-element.48.stats, bf16[2,512,768]{2,1,0:T(8,128)(2,1)S(1)} %get-tuple-element.49.s_far, ...), custom_call_target="tpu_custom_call" | custom-call | flops 805306368 | bytes 8388608 | tf_op jit(solution)/shard_map/rest/pallas_call | solution.py:322
  108.1 0.0 collective-permute-done.6.refs_1_
  108.1 2.4 %collective-permute-done.7.refs_2_ = bf16[128,512]{1,0:T(8,128)(2,1)S(1)} collective-permute-done((bf16[128,512]{1,0:T(8,128)(2,1)S(1)}, bf16[128,512]{1,0:T(8,128)(2,1)S(1)}, u32[]{:S(2)}, u32[]{:S(2)}) %collective-permute-start.7) | collective-permute-done | bytes 131104 | tf_op jit(solution)/shard_map/ppermute | solution.py:247
  110.5 1.2 %collective-permute-done.8.refs_3_ = bf16[128,512]{1,0:T(8,128)(2,1)S(1)} collective-permute-done((bf16[128,512]{1,0:T(8,128)(2,1)S(1)}, bf16[128,512]{1,0:T(8,128)(2,1)S(1)}, u32[]{:S(2)}, u32[]{:S(2)}) %collective-permute-start.8) | collective-permute-done | bytes 131104 | tf_op jit(solution)/shard_map/ppermute | solution.py:247
  111.6 0.0 collective-permute-done.9.refs_4_
  111.6 1.7 %collect.1 = (bf16[512,256]{1,0:T(8,128)(2,1)}, bf16[512,256]{1,0:T(8,128)(2,1)}) custom-call(s32[6,64]{1,0:T(8,128)S(1)} %bitcast.2, f32[512,256]{1,0:T(8,128)S(1)} %get-tuple-element.52.gk_ref, f32[512,256]{1,0:T(8,128)S(1)} %get-tuple-element.53.gv_ref, bf16[128,512]{1,0:T(8,128)(2,1)S(1)} %collective-permute-done.5.refs_0_, ...), custom_call_target="tpu_custom_call" | custom-call | tf_op jit(solution)/shard_map/collect/pallas_call | solution.py:332
  (12 shorter events, 0.1 us)
Async XLA Ops:
  0.6 78.6 %copy-start = (bf16[512,256]{1,0:T(8,128)(2,1)S(1)}, bf16[512,256]{1,0:T(8,128)(2,1)}, u32[]{:S(2)}) copy-start(bf16[512,256]{1,0:T(8,128)(2,1)} %v_ref.3) | copy-start | bytes 786436
  0.6 57.1 %copy-start.2 = (bf16[512,256]{1,0:T(8,128)(2,1)S(1)}, bf16[512,256]{1,0:T(8,128)(2,1)}, u32[]{:S(2)}) copy-start(bf16[512,256]{1,0:T(8,128)(2,1)} %k_ref.1) | copy-start | bytes 786436
  0.7 57.0 %copy-start.1 = (bf16[512,256]{1,0:T(8,128)(2,1)S(1)}, bf16[512,256]{1,0:T(8,128)(2,1)}, u32[]{:S(2)}) copy-start(bf16[512,256]{1,0:T(8,128)(2,1)} %q_ref.1) | copy-start | bytes 786436
  0.7 78.6 %copy-start.3 = (bf16[512,256]{1,0:T(8,128)(2,1)S(1)}, bf16[512,256]{1,0:T(8,128)(2,1)}, u32[]{:S(2)}) copy-start(bf16[512,256]{1,0:T(8,128)(2,1)} %d_ref.3) | copy-start | bytes 786436
  0.7 0.8 copy-start.4
  3.9 36.4 %collective-permute-start = (bf16[256,512]{1,0:T(8,128)(2,1)S(1)}, bf16[256,512]{1,0:T(8,128)(2,1)S(1)}, u32[]{:S(2)}, u32[]{:S(2)}) collective-permute-start(bf16[256,512]{1,0:T(8,128)(2,1)S(1)} %get-tuple-element.38), channel_id=1, source_target_pairs={{0,16},{16,0},{32,48},{48,32},{64,80},{80,64},{96,112},{112,96},{1... | collective-permute-start | bytes 786440 | tf_op jit(solution)/shard_map/ppermute | solution.py:247
  5.9 34.5 %collective-permute-start.1 = (bf16[128,512]{1,0:T(8,128)(2,1)S(1)}, bf16[128,512]{1,0:T(8,128)(2,1)S(1)}, u32[]{:S(2)}, u32[]{:S(2)}) collective-permute-start(bf16[128,512]{1,0:T(8,128)(2,1)S(1)} %get-tuple-element.39), channel_id=1, source_target_pairs={{0,64},{64,0},{16,80},{80,16},{32,96},{96,32},{48,112},{112,48},{1... | collective-permute-start | bytes 393224 | tf_op jit(solution)/shard_map/ppermute | solution.py:247
  12.0 28.4 %collective-permute-start.2 = (bf16[128,512]{1,0:T(8,128)(2,1)S(1)}, bf16[128,512]{1,0:T(8,128)(2,1)S(1)}, u32[]{:S(2)}, u32[]{:S(2)}) collective-permute-start(bf16[128,512]{1,0:T(8,128)(2,1)S(1)} %get-tuple-element.40), channel_id=1, source_target_pairs={{64,128},{128,64},{80,144},{144,80},{96,160},{160,96},{112,176},{1... | collective-permute-start | bytes 393224 | tf_op jit(solution)/shard_map/ppermute | solution.py:247
  22.3 35.4 %all-to-all-start = ((f32[16,8,128]{2,1,0:T(8,128)}), f32[16,8,128]{2,1,0:T(8,128)S(1)}, u32[]{:S(2)}, u32[]{:S(2)}) async-start(f32[16,8,128]{2,1,0:T(8,128)} %get-tuple-element.33), calls=%async_computation | async-start | bytes 131072 | tf_op jit(solution)/shard_map/all_to_all | solution.py:289
  40.5 38.8 %collective-permute-start.4 = (bf16[256,512]{1,0:T(8,128)(2,1)S(1)}, bf16[256,512]{1,0:T(8,128)(2,1)S(1)}, u32[]{:S(2)}, u32[]{:S(2)}) collective-permute-start(bf16[256,512]{1,0:T(8,128)(2,1)S(1)} %get-tuple-element.62), channel_id=1, source_target_pairs={{0,32},{32,0},{16,48},{48,16},{64,96},{96,64},{80,112},{112,80},{1... | collective-permute-start | bytes 786440 | tf_op jit(solution)/shard_map/ppermute | solution.py:247
  43.8 35.4 %collective-permute-start.3 = (bf16[256,512]{1,0:T(8,128)(2,1)S(1)}, bf16[256,512]{1,0:T(8,128)(2,1)S(1)}, u32[]{:S(2)}, u32[]{:S(2)}) collective-permute-start(bf16[256,512]{1,0:T(8,128)(2,1)S(1)} %get-tuple-element.63), channel_id=1, source_target_pairs={{32,64},{64,32},{48,80},{80,48},{96,128},{128,96},{112,144},{144,1... | collective-permute-start | bytes 786440 | tf_op jit(solution)/shard_map/ppermute | solution.py:247
  84.3 19.4 %collective-permute-start.5 = (bf16[128,512]{1,0:T(8,128)(2,1)S(1)}, bf16[128,512]{1,0:T(8,128)(2,1)S(1)}, u32[]{:S(2)}, u32[]{:S(2)}) collective-permute-start(bf16[128,512]{1,0:T(8,128)(2,1)S(1)} %get-tuple-element.54), channel_id=1, source_target_pairs={{64,128},{128,64},{80,144},{144,80},{96,160},{160,96},{112,176},{1... | collective-permute-start | bytes 393224 | tf_op jit(solution)/shard_map/ppermute | solution.py:247
  87.5 20.6 %collective-permute-start.6 = (bf16[128,512]{1,0:T(8,128)(2,1)S(1)}, bf16[128,512]{1,0:T(8,128)(2,1)S(1)}, u32[]{:S(2)}, u32[]{:S(2)}) collective-permute-start(bf16[128,512]{1,0:T(8,128)(2,1)S(1)} %get-tuple-element.55), channel_id=1, source_target_pairs={{32,64},{64,32},{48,80},{80,48},{96,128},{128,96},{112,144},{144,1... | collective-permute-start | bytes 393224 | tf_op jit(solution)/shard_map/ppermute | solution.py:247
  96.4 14.1 %collective-permute-start.7 = (bf16[128,512]{1,0:T(8,128)(2,1)S(1)}, bf16[128,512]{1,0:T(8,128)(2,1)S(1)}, u32[]{:S(2)}, u32[]{:S(2)}) collective-permute-start(bf16[128,512]{1,0:T(8,128)(2,1)S(1)} %get-tuple-element.56), channel_id=1, source_target_pairs={{16,32},{32,16},{48,64},{64,48},{80,96},{96,80},{112,128},{128,112... | collective-permute-start | bytes 393224 | tf_op jit(solution)/shard_map/ppermute | solution.py:247
  99.8 11.9 %collective-permute-start.8 = (bf16[128,512]{1,0:T(8,128)(2,1)S(1)}, bf16[128,512]{1,0:T(8,128)(2,1)S(1)}, u32[]{:S(2)}, u32[]{:S(2)}) collective-permute-start(bf16[128,512]{1,0:T(8,128)(2,1)S(1)} %get-tuple-element.57), channel_id=1, source_target_pairs={{0,64},{64,0},{16,80},{80,16},{32,96},{96,32},{48,112},{112,48},{1... | collective-permute-start | bytes 393224 | tf_op jit(solution)/shard_map/ppermute | solution.py:247
  101.7 9.9 %collective-permute-start.9 = (bf16[128,512]{1,0:T(8,128)(2,1)S(1)}, bf16[128,512]{1,0:T(8,128)(2,1)S(1)}, u32[]{:S(2)}, u32[]{:S(2)}) collective-permute-start(bf16[128,512]{1,0:T(8,128)(2,1)S(1)} %get-tuple-element.58), channel_id=1, source_target_pairs={{0,32},{32,0},{16,48},{48,16},{64,96},{96,64},{80,112},{112,80},{1... | collective-permute-start | bytes 393224 | tf_op jit(solution)/shard_map/ppermute | solution.py:247
  103.6 8.0 %collective-permute-start.10 = (bf16[128,512]{1,0:T(8,128)(2,1)S(1)}, bf16[128,512]{1,0:T(8,128)(2,1)S(1)}, u32[]{:S(2)}, u32[]{:S(2)}) collective-permute-start(bf16[128,512]{1,0:T(8,128)(2,1)S(1)} %get-tuple-element.59), channel_id=1, source_target_pairs={{0,16},{16,0},{32,48},{48,32},{64,80},{80,64},{96,112},{112,96},{1... | collective-permute-start | bytes 393224 | tf_op jit(solution)/shard_map/ppermute | solution.py:247
  105.5 6.1 %copy-start.5 = (s32[64,6]{0,1:T(8,128)S(1)}, s32[64,6]{0,1:T(8,128)}, u32[]{:S(2)}) copy-start(s32[64,6]{0,1:T(8,128)} %param.9) | copy-start | bytes 4612

commit v9 on v8

--- a/solution.py
+++ b/solution.py
@@ -11,6 +11,7 @@
 HD = 128
 BS = 128
 EXCHANGES = ((1, False), (4, True), (4, False), (2, True), (2, False), (1, True))
+FAR_ORDER = (0, 4, 3, 1, 2)
 RETURN_ORDER = (1, 3, 5, 2, 4, 0)
 
 masked_score = -1e30
@@ -162,16 +163,16 @@
             k_far[start : start + BS, column : column + 128] = scaled(part, scale)
         v_far[start : start + BS] = far[:BS, width:]
 
-    for slot, far in enumerate(far_refs):
+    for slot, far in zip(FAR_ORDER, far_refs):
         place(slot, far)
 
     @pl.when(via_near(frame))
     def _():
-        place(5, far_refs[4].at[BS:])
+        place(5, far_refs[1].at[BS:])
 
     @pl.when(jnp.logical_not(via_near(frame)))
     def _():
-        place(5, far_refs[3].at[BS:])
+        place(5, far_refs[2].at[BS:])
 
     column = lax.broadcasted_iota(jnp.int32, (1, 6 * BS), 1)
     allowed = column < 0
@@ -252,10 +253,10 @@
     got_first = exchange(first, frames, 0)
     got_wide_far = exchange(wide_far, frames, 1)
     got_near_far = exchange(near_far, frames, 2)
-    relay, got_near_far, got_wide_far = lax.optimization_barrier((got_first[BS:], got_near_far, got_wide_far))
+    relay = got_first[BS:]
     got_wide_two = exchange(jnp.concatenate([wide_two, relay]), frames, 3)
     got_near_two = exchange(jnp.concatenate([near_two, relay]), frames, 4)
-    return got_first, got_wide_far, got_near_far, got_wide_two, got_near_two
+    return got_first, got_near_two, got_wide_two, got_wide_far, got_near_far
 
 
 def swap(blocks, frames):

time: 114 us -> 107 us (0.939)
  the two profiles are of different devices: /device:TPU:2 before, /device:TPU:10 now
where the time goes in v9:
time: 107 us
  starting transfers between devices  77.7 us (73%)
  waiting for transfers between devices  15 us (14%)
  Pallas kernels  12.4 us (12%)
    ppermute x11, starting transfers between devices, exchange(): return lax.ppermute(block, 'frame', route(*EXCHANGES[which], frames))  40.9 us
    all_to_all x1, starting transfers between devices, on_device(): sums = lax.all_to_all(sums, 'head', 0, 0)  24.5 us
    all_to_all x1, starting transfers between devices, on_device(): scales = lax.all_to_all(scales, 'frame', 0, 0)  12.3 us
    all_to_all x1, waiting for transfers between devices, on_device(): scales = lax.all_to_all(scales, 'frame', 0, 0)  10.7 us
    pallas_call x1, Pallas kernels, on_device(): pl.pallas_call(functools.partial(attend_kernel, frames), out_shape=[flat,...  4.97 us
    ppermute x11, waiting for transfers between devices, exchange(): return lax.ppermute(block, 'frame', route(*EXCHANGES[which], frames))  4.35 us
    pallas_call x1, Pallas kernels, on_device(): pl.pallas_call(rest_kernel, out_shape=[flat, wide, wide], in_specs=[VMEM]...  2.51 us
    pallas_call x1, Pallas kernels, on_device(): pl.pallas_call(functools.partial(prepare_kernel, frames), out_shape=[jax....  2.5 us
  transfers between devices with their start and end apart: 13, of which 4 were waited for; matrix products, arithmetic and copies ran while one was open for 0% of the time, Pallas kernels for 3%

profile of v9, /device:TPU:10, one launch (start us, length us, event | category | flops | bytes accessed | tf_op | source)
XLA Modules:
  0.0 106.7 jit_solution(8822548892940961774)
XLA Ops:
  0.7 0.0 copy-start.4
  0.7 0.8 copy-done.4
  1.4 2.5 %prepare.1 = (f32[16,8,128]{2,1,0:T(8,128)}, s32[8,128]{1,0:T(8,128)S(1)}, bf16[256,512]{1,0:T(8,128)(2,1)S(1)}, bf16[128,512]{1,0:T(8,128)(2,1)S(1)}, bf16[128,...) custom-call(s32[6,64]{1,0:T(8,128)S(1)} %bitcast.1, bf16[512,256]{1,0:T(8,128)(2,1)} %q_ref.1, ...), custom_call_target="tpu_custom_call" | custom-call | tf_op jit(solution)/shard_map/prepare/pallas_call | solution.py:276
  3.9 1.9 %collective-permute-start = (bf16[256,512]{1,0:T(8,128)(2,1)S(1)}, bf16[256,512]{1,0:T(8,128)(2,1)S(1)}, u32[]{:S(2)}, u32[]{:S(2)}) collective-permute-start(bf16[256,512]{1,0:T(8,128)(2,1)S(1)} %get-tuple-element.35), channel_id=1, source_target_pairs={{0,16},{16,0},{32,48},{48,32},{64,80},{80,64},{96,112},{112,96},{1... | collective-permute-start | bytes 786440 | tf_op jit(solution)/shard_map/ppermute | solution.py:248
  5.9 24.5 %all-to-all-start = ((f32[16,8,128]{2,1,0:T(8,128)}), f32[16,8,128]{2,1,0:T(8,128)S(1)}, u32[]{:S(2)}, u32[]{:S(2)}) async-start(f32[16,8,128]{2,1,0:T(8,128)} %get-tuple-element.30), calls=%async_computation | async-start | bytes 131072 | tf_op jit(solution)/shard_map/all_to_all | solution.py:290
  30.3 0.0 collective-permute-done.refs_0_
  30.4 8.8 %collective-permute-start.2 = (bf16[256,512]{1,0:T(8,128)(2,1)S(1)}, bf16[256,512]{1,0:T(8,128)(2,1)S(1)}, u32[]{:S(2)}, u32[]{:S(2)}) collective-permute-start(bf16[256,512]{1,0:T(8,128)(2,1)S(1)} %get-tuple-element.56), channel_id=1, source_target_pairs={{32,64},{64,32},{48,80},{80,48},{96,128},{128,96},{112,144},{144,1... | collective-permute-start | bytes 786440 | tf_op jit(solution)/shard_map/ppermute | solution.py:248
  39.2 1.9 %collective-permute-start.1 = (bf16[256,512]{1,0:T(8,128)(2,1)S(1)}, bf16[256,512]{1,0:T(8,128)(2,1)S(1)}, u32[]{:S(2)}, u32[]{:S(2)}) collective-permute-start(bf16[256,512]{1,0:T(8,128)(2,1)S(1)} %get-tuple-element.57), channel_id=1, source_target_pairs={{0,32},{32,0},{16,48},{48,16},{64,96},{96,64},{80,112},{112,80},{1... | collective-permute-start | bytes 786440 | tf_op jit(solution)/shard_map/ppermute | solution.py:248
  41.2 5.1 %collective-permute-start.3 = (bf16[128,512]{1,0:T(8,128)(2,1)S(1)}, bf16[128,512]{1,0:T(8,128)(2,1)S(1)}, u32[]{:S(2)}, u32[]{:S(2)}) collective-permute-start(bf16[128,512]{1,0:T(8,128)(2,1)S(1)} %get-tuple-element.38), channel_id=1, source_target_pairs={{64,128},{128,64},{80,144},{144,80},{96,160},{160,96},{112,176},{1... | collective-permute-start | bytes 393224 | tf_op jit(solution)/shard_map/ppermute | solution.py:248
  46.3 1.9 %collective-permute-start.4 = (bf16[128,512]{1,0:T(8,128)(2,1)S(1)}, bf16[128,512]{1,0:T(8,128)(2,1)S(1)}, u32[]{:S(2)}, u32[]{:S(2)}) collective-permute-start(bf16[128,512]{1,0:T(8,128)(2,1)S(1)} %get-tuple-element.39), channel_id=1, source_target_pairs={{0,64},{64,0},{16,80},{80,16},{32,96},{96,32},{48,112},{112,48},{1... | collective-permute-start | bytes 393224 | tf_op jit(solution)/shard_map/ppermute | solution.py:248
  48.2 0.0 all-to-all-done.sums_ref
  48.2 0.7 normalize.1
  48.9 12.3 %all-to-all-start.1 = ((f32[64,1,128]{2,1,0:T(1,128)}), f32[64,1,128]{2,1,0:T(1,128)S(1)}, u32[]{:S(2)}, u32[]{:S(2)}) async-start(f32[64,1,128]{2,1,0:T(1,128)} %get-tuple-element.32), calls=%async_computation.1 | async-start | bytes 65536 | tf_op jit(solution)/shard_map/all_to_all | solution.py:300
  61.2 0.8 collective-permute-done.3.refs_3_
  62.0 0.0 collective-permute-done.4.refs_4_
  62.0 10.7 %all-to-all-done.1.scale_ref = f32[64,1,128]{2,1,0:T(1,128)S(1)} async-done(((f32[64,1,128]{2,1,0:T(1,128)}), f32[64,1,128]{2,1,0:T(1,128)S(1)}, u32[]{:S(2)}, u32[]{:S(2)}) %all-to-all-start.1) | async-done | bytes 32800 | tf_op jit(solution)/shard_map/all_to_all | solution.py:300
  72.7 0.0 collective-permute-done.2.refs_2_
  72.7 5.0 %attend.1 = (bf16[512,256]{1,0:T(8,128)(2,1)}, f32[2,512,512]{2,1,0:T(8,128)S(1)}, f32[512,128]{1,0:T(8,128)S(1)}, bf16[2,512,768]{2,1,0:T(8,128)(2,1)S(1)}, bf1...) custom-call(f32[64,1,128]{2,1,0:T(1,128)S(1)} %all-to-all-done.1.sca, ...), custom_call_target="tpu_custom_call" | custom-call | tf_op jit(solution)/shard_map/attend/pallas_call | solution.py:304
  77.7 3.2 %collective-permute-start.5 = (bf16[128,512]{1,0:T(8,128)(2,1)S(1)}, bf16[128,512]{1,0:T(8,128)(2,1)S(1)}, u32[]{:S(2)}, u32[]{:S(2)}) collective-permute-start(bf16[128,512]{1,0:T(8,128)(2,1)S(1)} %get-tuple-element.48), channel_id=1, source_target_pairs={{64,128},{128,64},{80,144},{144,80},{96,160},{160,96},{112,176},{1... | collective-permute-start | bytes 393224 | tf_op jit(solution)/shard_map/ppermute | solution.py:248
  80.9 8.9 %collective-permute-start.6 = (bf16[128,512]{1,0:T(8,128)(2,1)S(1)}, bf16[128,512]{1,0:T(8,128)(2,1)S(1)}, u32[]{:S(2)}, u32[]{:S(2)}) collective-permute-start(bf16[128,512]{1,0:T(8,128)(2,1)S(1)} %get-tuple-element.49), channel_id=1, source_target_pairs={{32,64},{64,32},{48,80},{80,48},{96,128},{128,96},{112,144},{144,1... | collective-permute-start | bytes 393224 | tf_op jit(solution)/shard_map/ppermute | solution.py:248
  89.8 3.3 %collective-permute-start.7 = (bf16[128,512]{1,0:T(8,128)(2,1)S(1)}, bf16[128,512]{1,0:T(8,128)(2,1)S(1)}, u32[]{:S(2)}, u32[]{:S(2)}) collective-permute-start(bf16[128,512]{1,0:T(8,128)(2,1)S(1)} %get-tuple-element.50), channel_id=1, source_target_pairs={{16,32},{32,16},{48,64},{64,48},{80,96},{96,80},{112,128},{128,112... | collective-permute-start | bytes 393224 | tf_op jit(solution)/shard_map/ppermute | solution.py:248
  93.2 1.9 %collective-permute-start.8 = (bf16[128,512]{1,0:T(8,128)(2,1)S(1)}, bf16[128,512]{1,0:T(8,128)(2,1)S(1)}, u32[]{:S(2)}, u32[]{:S(2)}) collective-permute-start(bf16[128,512]{1,0:T(8,128)(2,1)S(1)} %get-tuple-element.51), channel_id=1, source_target_pairs={{0,64},{64,0},{16,80},{80,16},{32,96},{96,32},{48,112},{112,48},{1... | collective-permute-start | bytes 393224 | tf_op jit(solution)/shard_map/ppermute | solution.py:248
  95.1 1.9 %collective-permute-start.9 = (bf16[128,512]{1,0:T(8,128)(2,1)S(1)}, bf16[128,512]{1,0:T(8,128)(2,1)S(1)}, u32[]{:S(2)}, u32[]{:S(2)}) collective-permute-start(bf16[128,512]{1,0:T(8,128)(2,1)S(1)} %get-tuple-element.52), channel_id=1, source_target_pairs={{0,32},{32,0},{16,48},{48,16},{64,96},{96,64},{80,112},{112,80},{1... | collective-permute-start | bytes 393224 | tf_op jit(solution)/shard_map/ppermute | solution.py:248
  97.0 0.0 collective-permute-done.5.refs_0_
  97.0 1.9 %collective-permute-start.10 = (bf16[128,512]{1,0:T(8,128)(2,1)S(1)}, bf16[128,512]{1,0:T(8,128)(2,1)S(1)}, u32[]{:S(2)}, u32[]{:S(2)}) collective-permute-start(bf16[128,512]{1,0:T(8,128)(2,1)S(1)} %get-tuple-element.53), channel_id=1, source_target_pairs={{0,16},{16,0},{32,48},{48,32},{64,80},{80,64},{96,112},{112,96},{1... | collective-permute-start | bytes 393224 | tf_op jit(solution)/shard_map/ppermute | solution.py:248
  99.0 0.0 copy-start.5
  99.0 2.5 %rest.1 = (bf16[512,256]{1,0:T(8,128)(2,1)}, f32[512,256]{1,0:T(8,128)S(1)}, f32[512,256]{1,0:T(8,128)S(1)}) custom-call(f32[2,512,512]{2,1,0:T(8,128)S(1)} %get-tuple-element.41.w_own, f32[512,128]{1,0:T(8,128)S(1)} %get-tuple-element.42.stats, bf16[2,512,768]{2,1,0:T(8,128)(2,1)S(1)} %get-tuple-element.43.s_far, ...), custom_call_target="tpu_custom_call" | custom-call | flops 805306368 | bytes 8388608 | tf_op jit(solution)/shard_map/rest/pallas_call | solution.py:323
  101.5 2.4 %collective-permute-done.7.refs_2_ = bf16[128,512]{1,0:T(8,128)(2,1)S(1)} collective-permute-done((bf16[128,512]{1,0:T(8,128)(2,1)S(1)}, bf16[128,512]{1,0:T(8,128)(2,1)S(1)}, u32[]{:S(2)}, u32[]{:S(2)}) %collective-permute-start.7) | collective-permute-done | bytes 131104 | tf_op jit(solution)/shard_map/ppermute | solution.py:248
  103.9 1.1 %collective-permute-done.8.refs_3_ = bf16[128,512]{1,0:T(8,128)(2,1)S(1)} collective-permute-done((bf16[128,512]{1,0:T(8,128)(2,1)S(1)}, bf16[128,512]{1,0:T(8,128)(2,1)S(1)}, u32[]{:S(2)}, u32[]{:S(2)}) %collective-permute-start.8) | collective-permute-done | bytes 131104 | tf_op jit(solution)/shard_map/ppermute | solution.py:248
  105.0 0.0 collective-permute-done.9.refs_4_
  105.0 0.0 collective-permute-done.10.refs_5_
  105.0 1.7 %collect.1 = (bf16[512,256]{1,0:T(8,128)(2,1)}, bf16[512,256]{1,0:T(8,128)(2,1)}) custom-call(s32[6,64]{1,0:T(8,128)S(1)} %bitcast.2, f32[512,256]{1,0:T(8,128)S(1)} %get-tuple-element.46.gk_ref, f32[512,256]{1,0:T(8,128)S(1)} %get-tuple-element.47.gv_ref, bf16[128,512]{1,0:T(8,128)(2,1)S(1)} %collective-permute-done.5.refs_0_, ...), custom_call_target="tpu_custom_call" | custom-call | tf_op jit(solution)/shard_map/collect/pallas_call | solution.py:333
  (13 shorter events, 0.1 us)
Async XLA Ops:
  0.6 72.0 %copy-start = (bf16[512,256]{1,0:T(8,128)(2,1)S(1)}, bf16[512,256]{1,0:T(8,128)(2,1)}, u32[]{:S(2)}) copy-start(bf16[512,256]{1,0:T(8,128)(2,1)} %v_ref.3) | copy-start | bytes 786436
  0.6 47.6 %copy-start.2 = (bf16[512,256]{1,0:T(8,128)(2,1)S(1)}, bf16[512,256]{1,0:T(8,128)(2,1)}, u32[]{:S(2)}) copy-start(bf16[512,256]{1,0:T(8,128)(2,1)} %k_ref.1) | copy-start | bytes 786436
  0.7 47.6 %copy-start.1 = (bf16[512,256]{1,0:T(8,128)(2,1)S(1)}, bf16[512,256]{1,0:T(8,128)(2,1)}, u32[]{:S(2)}) copy-start(bf16[512,256]{1,0:T(8,128)(2,1)} %q_ref.1) | copy-start | bytes 786436
  0.7 72.0 %copy-start.3 = (bf16[512,256]{1,0:T(8,128)(2,1)S(1)}, bf16[512,256]{1,0:T(8,128)(2,1)}, u32[]{:S(2)}) copy-start(bf16[512,256]{1,0:T(8,128)(2,1)} %d_ref.3) | copy-start | bytes 786436
  0.7 0.8 copy-start.4
  3.9 26.4 %collective-permute-start = (bf16[256,512]{1,0:T(8,128)(2,1)S(1)}, bf16[256,512]{1,0:T(8,128)(2,1)S(1)}, u32[]{:S(2)}, u32[]{:S(2)}) collective-permute-start(bf16[256,512]{1,0:T(8,128)(2,1)S(1)} %get-tuple-element.35), channel_id=1, source_target_pairs={{0,16},{16,0},{32,48},{48,32},{64,80},{80,64},{96,112},{112,96},{1... | collective-permute-start | bytes 786440 | tf_op jit(solution)/shard_map/ppermute | solution.py:248
  5.9 42.3 %all-to-all-start = ((f32[16,8,128]{2,1,0:T(8,128)}), f32[16,8,128]{2,1,0:T(8,128)S(1)}, u32[]{:S(2)}, u32[]{:S(2)}) async-start(f32[16,8,128]{2,1,0:T(8,128)} %get-tuple-element.30), calls=%async_computation | async-start | bytes 131072 | tf_op jit(solution)/shard_map/all_to_all | solution.py:290
  30.4 42.3 %collective-permute-start.2 = (bf16[256,512]{1,0:T(8,128)(2,1)S(1)}, bf16[256,512]{1,0:T(8,128)(2,1)S(1)}, u32[]{:S(2)}, u32[]{:S(2)}) collective-permute-start(bf16[256,512]{1,0:T(8,128)(2,1)S(1)} %get-tuple-element.56), channel_id=1, source_target_pairs={{32,64},{64,32},{48,80},{80,48},{96,128},{128,96},{112,144},{144,1... | collective-permute-start | bytes 786440 | tf_op jit(solution)/shard_map/ppermute | solution.py:248
  39.2 33.5 %collective-permute-start.1 = (bf16[256,512]{1,0:T(8,128)(2,1)S(1)}, bf16[256,512]{1,0:T(8,128)(2,1)S(1)}, u32[]{:S(2)}, u32[]{:S(2)}) collective-permute-start(bf16[256,512]{1,0:T(8,128)(2,1)S(1)} %get-tuple-element.57), channel_id=1, source_target_pairs={{0,32},{32,0},{16,48},{48,16},{64,96},{96,64},{80,112},{112,80},{1... | collective-permute-start | bytes 786440 | tf_op jit(solution)/shard_map/ppermute | solution.py:248
  41.2 20.8 %collective-permute-start.3 = (bf16[128,512]{1,0:T(8,128)(2,1)S(1)}, bf16[128,512]{1,0:T(8,128)(2,1)S(1)}, u32[]{:S(2)}, u32[]{:S(2)}) collective-permute-start(bf16[128,512]{1,0:T(8,128)(2,1)S(1)} %get-tuple-element.38), channel_id=1, source_target_pairs={{64,128},{128,64},{80,144},{144,80},{96,160},{160,96},{112,176},{1... | collective-permute-start | bytes 393224 | tf_op jit(solution)/shard_map/ppermute | solution.py:248
  46.3 15.7 %collective-permute-start.4 = (bf16[128,512]{1,0:T(8,128)(2,1)S(1)}, bf16[128,512]{1,0:T(8,128)(2,1)S(1)}, u32[]{:S(2)}, u32[]{:S(2)}) collective-permute-start(bf16[128,512]{1,0:T(8,128)(2,1)S(1)} %get-tuple-element.39), channel_id=1, source_target_pairs={{0,64},{64,0},{16,80},{80,16},{32,96},{96,32},{48,112},{112,48},{1... | collective-permute-start | bytes 393224 | tf_op jit(solution)/shard_map/ppermute | solution.py:248
  48.9 23.8 %all-to-all-start.1 = ((f32[64,1,128]{2,1,0:T(1,128)}), f32[64,1,128]{2,1,0:T(1,128)S(1)}, u32[]{:S(2)}, u32[]{:S(2)}) async-start(f32[64,1,128]{2,1,0:T(1,128)} %get-tuple-element.32), calls=%async_computation.1 | async-start | bytes 65536 | tf_op jit(solution)/shard_map/all_to_all | solution.py:300
  77.7 19.4 %collective-permute-start.5 = (bf16[128,512]{1,0:T(8,128)(2,1)S(1)}, bf16[128,512]{1,0:T(8,128)(2,1)S(1)}, u32[]{:S(2)}, u32[]{:S(2)}) collective-permute-start(bf16[128,512]{1,0:T(8,128)(2,1)S(1)} %get-tuple-element.48), channel_id=1, source_target_pairs={{64,128},{128,64},{80,144},{144,80},{96,160},{160,96},{112,176},{1... | collective-permute-start | bytes 393224 | tf_op jit(solution)/shard_map/ppermute | solution.py:248
  80.9 20.6 %collective-permute-start.6 = (bf16[128,512]{1,0:T(8,128)(2,1)S(1)}, bf16[128,512]{1,0:T(8,128)(2,1)S(1)}, u32[]{:S(2)}, u32[]{:S(2)}) collective-permute-start(bf16[128,512]{1,0:T(8,128)(2,1)S(1)} %get-tuple-element.49), channel_id=1, source_target_pairs={{32,64},{64,32},{48,80},{80,48},{96,128},{128,96},{112,144},{144,1... | collective-permute-start | bytes 393224 | tf_op jit(solution)/shard_map/ppermute | solution.py:248
  89.8 14.1 %collective-permute-start.7 = (bf16[128,512]{1,0:T(8,128)(2,1)S(1)}, bf16[128,512]{1,0:T(8,128)(2,1)S(1)}, u32[]{:S(2)}, u32[]{:S(2)}) collective-permute-start(bf16[128,512]{1,0:T(8,128)(2,1)S(1)} %get-tuple-element.50), channel_id=1, source_target_pairs={{16,32},{32,16},{48,64},{64,48},{80,96},{96,80},{112,128},{128,112... | collective-permute-start | bytes 393224 | tf_op jit(solution)/shard_map/ppermute | solution.py:248
  93.2 11.9 %collective-permute-start.8 = (bf16[128,512]{1,0:T(8,128)(2,1)S(1)}, bf16[128,512]{1,0:T(8,128)(2,1)S(1)}, u32[]{:S(2)}, u32[]{:S(2)}) collective-permute-start(bf16[128,512]{1,0:T(8,128)(2,1)S(1)} %get-tuple-element.51), channel_id=1, source_target_pairs={{0,64},{64,0},{16,80},{80,16},{32,96},{96,32},{48,112},{112,48},{1... | collective-permute-start | bytes 393224 | tf_op jit(solution)/shard_map/ppermute | solution.py:248
  95.1 9.9 %collective-permute-start.9 = (bf16[128,512]{1,0:T(8,128)(2,1)S(1)}, bf16[128,512]{1,0:T(8,128)(2,1)S(1)}, u32[]{:S(2)}, u32[]{:S(2)}) collective-permute-start(bf16[128,512]{1,0:T(8,128)(2,1)S(1)} %get-tuple-element.52), channel_id=1, source_target_pairs={{0,32},{32,0},{16,48},{48,16},{64,96},{96,64},{80,112},{112,80},{1... | collective-permute-start | bytes 393224 | tf_op jit(solution)/shard_map/ppermute | solution.py:248
  97.0 8.0 %collective-permute-start.10 = (bf16[128,512]{1,0:T(8,128)(2,1)S(1)}, bf16[128,512]{1,0:T(8,128)(2,1)S(1)}, u32[]{:S(2)}, u32[]{:S(2)}) collective-permute-start(bf16[128,512]{1,0:T(8,128)(2,1)S(1)} %get-tuple-element.53), channel_id=1, source_target_pairs={{0,16},{16,0},{32,48},{48,32},{64,80},{80,64},{96,112},{112,96},{1... | collective-permute-start | bytes 393224 | tf_op jit(solution)/shard_map/ppermute | solution.py:248
  99.0 6.1 %copy-start.5 = (s32[64,6]{0,1:T(8,128)S(1)}, s32[64,6]{0,1:T(8,128)}, u32[]{:S(2)}) copy-start(s32[64,6]{0,1:T(8,128)} %param.9) | copy-start | bytes 4612

commit v10 on v8

--- a/solution.py
+++ b/solution.py
@@ -252,7 +252,7 @@
     got_first = exchange(first, frames, 0)
     got_wide_far = exchange(wide_far, frames, 1)
     got_near_far = exchange(near_far, frames, 2)
-    relay, got_near_far, got_wide_far = lax.optimization_barrier((got_first[BS:], got_near_far, got_wide_far))
+    relay = got_first[BS:]
     got_wide_two = exchange(jnp.concatenate([wide_two, relay]), frames, 3)
     got_near_two = exchange(jnp.concatenate([near_two, relay]), frames, 4)
     return got_first, got_wide_far, got_near_far, got_wide_two, got_near_two

time: 114 us -> 107 us (0.939)
  the two profiles are of different devices: /device:TPU:2 before, /device:TPU:10 now
where the time goes in v10:
time: 107 us
  starting transfers between devices  76.2 us (71%)
  waiting for transfers between devices  16.4 us (15%)
  Pallas kernels  12.4 us (12%)
    ppermute x11, starting transfers between devices, exchange(): return lax.ppermute(block, 'frame', route(*EXCHANGES[which], frames))  38.5 us
    all_to_all x1, starting transfers between devices, on_device(): sums = lax.all_to_all(sums, 'head', 0, 0)  24.5 us
    all_to_all x1, starting transfers between devices, on_device(): scales = lax.all_to_all(scales, 'frame', 0, 0)  13.2 us
    ppermute x11, waiting for transfers between devices, exchange(): return lax.ppermute(block, 'frame', route(*EXCHANGES[which], frames))  8.41 us
    all_to_all x1, waiting for transfers between devices, on_device(): scales = lax.all_to_all(scales, 'frame', 0, 0)  7.14 us
    pallas_call x1, Pallas kernels, on_device(): pl.pallas_call(functools.partial(attend_kernel, frames), out_shape=[flat,...  4.97 us
    pallas_call x1, Pallas kernels, on_device(): pl.pallas_call(rest_kernel, out_shape=[flat, wide, wide], in_specs=[VMEM]...  2.52 us
    pallas_call x1, Pallas kernels, on_device(): pl.pallas_call(functools.partial(prepare_kernel, frames), out_shape=[jax....  2.5 us
  transfers between devices with their start and end apart: 13, of which 5 were waited for; matrix products, arithmetic and copies ran while one was open for 0% of the time, Pallas kernels for 3%

profile of v10, /device:TPU:10, one launch (start us, length us, event | category | flops | bytes accessed | tf_op | source)
XLA Modules:
  0.0 106.6 jit_solution(12550907687319784976)
XLA Ops:
  0.7 0.0 copy-start.4
  0.7 0.8 copy-done.4
  1.4 2.5 %prepare.1 = (f32[16,8,128]{2,1,0:T(8,128)}, s32[8,128]{1,0:T(8,128)S(1)}, bf16[256,512]{1,0:T(8,128)(2,1)S(1)}, bf16[128,512]{1,0:T(8,128)(2,1)S(1)}, bf16[128,...) custom-call(s32[6,64]{1,0:T(8,128)S(1)} %bitcast.1, bf16[512,256]{1,0:T(8,128)(2,1)} %q_ref.1, ...), custom_call_target="tpu_custom_call" | custom-call | tf_op jit(solution)/shard_map/prepare/pallas_call | solution.py:275
  3.9 1.9 %collective-permute-start = (bf16[256,512]{1,0:T(8,128)(2,1)S(1)}, bf16[256,512]{1,0:T(8,128)(2,1)S(1)}, u32[]{:S(2)}, u32[]{:S(2)}) collective-permute-start(bf16[256,512]{1,0:T(8,128)(2,1)S(1)} %get-tuple-element.35), channel_id=1, source_target_pairs={{0,16},{16,0},{32,48},{48,32},{64,80},{80,64},{96,112},{112,96},{1... | collective-permute-start | bytes 786440 | tf_op jit(solution)/shard_map/ppermute | solution.py:247
  5.9 24.5 %all-to-all-start = ((f32[16,8,128]{2,1,0:T(8,128)}), f32[16,8,128]{2,1,0:T(8,128)S(1)}, u32[]{:S(2)}, u32[]{:S(2)}) async-start(f32[16,8,128]{2,1,0:T(8,128)} %get-tuple-element.30), calls=%async_computation | async-start | bytes 131072 | tf_op jit(solution)/shard_map/all_to_all | solution.py:289
  30.3 0.0 collective-permute-done.refs_0_
  30.4 3.4 %collective-permute-start.4 = (bf16[256,512]{1,0:T(8,128)(2,1)S(1)}, bf16[256,512]{1,0:T(8,128)(2,1)S(1)}, u32[]{:S(2)}, u32[]{:S(2)}) collective-permute-start(bf16[256,512]{1,0:T(8,128)(2,1)S(1)} %get-tuple-element.56), channel_id=1, source_target_pairs={{0,32},{32,0},{16,48},{48,16},{64,96},{96,64},{80,112},{112,80},{1... | collective-permute-start | bytes 786440 | tf_op jit(solution)/shard_map/ppermute | solution.py:247
  33.8 7.9 %collective-permute-start.3 = (bf16[256,512]{1,0:T(8,128)(2,1)S(1)}, bf16[256,512]{1,0:T(8,128)(2,1)S(1)}, u32[]{:S(2)}, u32[]{:S(2)}) collective-permute-start(bf16[256,512]{1,0:T(8,128)(2,1)S(1)} %get-tuple-element.57), channel_id=1, source_target_pairs={{32,64},{64,32},{48,80},{80,48},{96,128},{128,96},{112,144},{144,1... | collective-permute-start | bytes 786440 | tf_op jit(solution)/shard_map/ppermute | solution.py:247
  41.7 1.9 %collective-permute-start.1 = (bf16[128,512]{1,0:T(8,128)(2,1)S(1)}, bf16[128,512]{1,0:T(8,128)(2,1)S(1)}, u32[]{:S(2)}, u32[]{:S(2)}) collective-permute-start(bf16[128,512]{1,0:T(8,128)(2,1)S(1)} %get-tuple-element.36), channel_id=1, source_target_pairs={{64,128},{128,64},{80,144},{144,80},{96,160},{160,96},{112,176},{1... | collective-permute-start | bytes 393224 | tf_op jit(solution)/shard_map/ppermute | solution.py:247
  43.6 1.9 %collective-permute-start.2 = (bf16[128,512]{1,0:T(8,128)(2,1)S(1)}, bf16[128,512]{1,0:T(8,128)(2,1)S(1)}, u32[]{:S(2)}, u32[]{:S(2)}) collective-permute-start(bf16[128,512]{1,0:T(8,128)(2,1)S(1)} %get-tuple-element.37), channel_id=1, source_target_pairs={{0,64},{64,0},{16,80},{80,16},{32,96},{96,32},{48,112},{112,48},{1... | collective-permute-start | bytes 393224 | tf_op jit(solution)/shard_map/ppermute | solution.py:247
  45.6 0.9 all-to-all-done.sums_ref
  46.4 0.7 normalize.1
  47.1 13.2 %all-to-all-start.1 = ((f32[64,1,128]{2,1,0:T(1,128)}), f32[64,1,128]{2,1,0:T(1,128)S(1)}, u32[]{:S(2)}, u32[]{:S(2)}) async-start(f32[64,1,128]{2,1,0:T(1,128)} %get-tuple-element.32), calls=%async_computation.1 | async-start | bytes 65536 | tf_op jit(solution)/shard_map/all_to_all | solution.py:299
  60.3 4.3 %collective-permute-done.1.refs_1_ = bf16[128,512]{1,0:T(8,128)(2,1)S(1)} collective-permute-done((bf16[128,512]{1,0:T(8,128)(2,1)S(1)}, bf16[128,512]{1,0:T(8,128)(2,1)S(1)}, u32[]{:S(2)}, u32[]{:S(2)}) %collective-permute-start.1) | collective-permute-done | bytes 131104 | tf_op jit(solution)/shard_map/ppermute | solution.py:247
  64.6 0.0 collective-permute-done.2.refs_2_
  64.6 7.1 %all-to-all-done.1.scale_ref = f32[64,1,128]{2,1,0:T(1,128)S(1)} async-done(((f32[64,1,128]{2,1,0:T(1,128)}), f32[64,1,128]{2,1,0:T(1,128)S(1)}, u32[]{:S(2)}, u32[]{:S(2)}) %all-to-all-start.1) | async-done | bytes 32800 | tf_op jit(solution)/shard_map/all_to_all | solution.py:299
  71.8 0.0 collective-permute-done.4.refs_4_
  71.8 0.0 collective-permute-done.3.refs_3_
  71.8 5.0 %attend.1 = (bf16[512,256]{1,0:T(8,128)(2,1)}, f32[2,512,512]{2,1,0:T(8,128)S(1)}, f32[512,128]{1,0:T(8,128)S(1)}, bf16[2,512,768]{2,1,0:T(8,128)(2,1)S(1)}, bf1...) custom-call(f32[64,1,128]{2,1,0:T(1,128)S(1)} %all-to-all-done.1.sca, ...), custom_call_target="tpu_custom_call" | custom-call | tf_op jit(solution)/shard_map/attend/pallas_call | solution.py:303
  76.8 3.5 %collective-permute-start.5 = (bf16[128,512]{1,0:T(8,128)(2,1)S(1)}, bf16[128,512]{1,0:T(8,128)(2,1)S(1)}, u32[]{:S(2)}, u32[]{:S(2)}) collective-permute-start(bf16[128,512]{1,0:T(8,128)(2,1)S(1)} %get-tuple-element.48), channel_id=1, source_target_pairs={{64,128},{128,64},{80,144},{144,80},{96,160},{160,96},{112,176},{1... | collective-permute-start | bytes 393224 | tf_op jit(solution)/shard_map/ppermute | solution.py:247
  80.2 8.7 %collective-permute-start.6 = (bf16[128,512]{1,0:T(8,128)(2,1)S(1)}, bf16[128,512]{1,0:T(8,128)(2,1)S(1)}, u32[]{:S(2)}, u32[]{:S(2)}) collective-permute-start(bf16[128,512]{1,0:T(8,128)(2,1)S(1)} %get-tuple-element.49), channel_id=1, source_target_pairs={{32,64},{64,32},{48,80},{80,48},{96,128},{128,96},{112,144},{144,1... | collective-permute-start | bytes 393224 | tf_op jit(solution)/shard_map/ppermute | solution.py:247
  88.9 3.6 %collective-permute-start.7 = (bf16[128,512]{1,0:T(8,128)(2,1)S(1)}, bf16[128,512]{1,0:T(8,128)(2,1)S(1)}, u32[]{:S(2)}, u32[]{:S(2)}) collective-permute-start(bf16[128,512]{1,0:T(8,128)(2,1)S(1)} %get-tuple-element.50), channel_id=1, source_target_pairs={{16,32},{32,16},{48,64},{64,48},{80,96},{96,80},{112,128},{128,112... | collective-permute-start | bytes 393224 | tf_op jit(solution)/shard_map/ppermute | solution.py:247
  92.5 1.9 %collective-permute-start.8 = (bf16[128,512]{1,0:T(8,128)(2,1)S(1)}, bf16[128,512]{1,0:T(8,128)(2,1)S(1)}, u32[]{:S(2)}, u32[]{:S(2)}) collective-permute-start(bf16[128,512]{1,0:T(8,128)(2,1)S(1)} %get-tuple-element.51), channel_id=1, source_target_pairs={{0,64},{64,0},{16,80},{80,16},{32,96},{96,32},{48,112},{112,48},{1... | collective-permute-start | bytes 393224 | tf_op jit(solution)/shard_map/ppermute | solution.py:247
  94.4 1.9 %collective-permute-start.9 = (bf16[128,512]{1,0:T(8,128)(2,1)S(1)}, bf16[128,512]{1,0:T(8,128)(2,1)S(1)}, u32[]{:S(2)}, u32[]{:S(2)}) collective-permute-start(bf16[128,512]{1,0:T(8,128)(2,1)S(1)} %get-tuple-element.52), channel_id=1, source_target_pairs={{0,32},{32,0},{16,48},{48,16},{64,96},{96,64},{80,112},{112,80},{1... | collective-permute-start | bytes 393224 | tf_op jit(solution)/shard_map/ppermute | solution.py:247
  96.4 1.9 %collective-permute-start.10 = (bf16[128,512]{1,0:T(8,128)(2,1)S(1)}, bf16[128,512]{1,0:T(8,128)(2,1)S(1)}, u32[]{:S(2)}, u32[]{:S(2)}) collective-permute-start(bf16[128,512]{1,0:T(8,128)(2,1)S(1)} %get-tuple-element.53), channel_id=1, source_target_pairs={{0,16},{16,0},{32,48},{48,32},{64,80},{80,64},{96,112},{112,96},{1... | collective-permute-start | bytes 393224 | tf_op jit(solution)/shard_map/ppermute | solution.py:247
  98.3 0.0 copy-start.5
  98.3 2.5 %rest.1 = (bf16[512,256]{1,0:T(8,128)(2,1)}, f32[512,256]{1,0:T(8,128)S(1)}, f32[512,256]{1,0:T(8,128)S(1)}) custom-call(f32[2,512,512]{2,1,0:T(8,128)S(1)} %get-tuple-element.41.w_own, f32[512,128]{1,0:T(8,128)S(1)} %get-tuple-element.42.stats, bf16[2,512,768]{2,1,0:T(8,128)(2,1)S(1)} %get-tuple-element.43.s_far, ...), custom_call_target="tpu_custom_call" | custom-call | flops 805306368 | bytes 8388608 | tf_op jit(solution)/shard_map/rest/pallas_call | solution.py:322
  100.8 0.0 collective-permute-done.6.refs_1_
  100.8 2.2 %collective-permute-done.7.refs_2_ = bf16[128,512]{1,0:T(8,128)(2,1)S(1)} collective-permute-done((bf16[128,512]{1,0:T(8,128)(2,1)S(1)}, bf16[128,512]{1,0:T(8,128)(2,1)S(1)}, u32[]{:S(2)}, u32[]{:S(2)}) %collective-permute-start.7) | collective-permute-done | bytes 131104 | tf_op jit(solution)/shard_map/ppermute | solution.py:247
  103.0 1.9 %collective-permute-done.8.refs_3_ = bf16[128,512]{1,0:T(8,128)(2,1)S(1)} collective-permute-done((bf16[128,512]{1,0:T(8,128)(2,1)S(1)}, bf16[128,512]{1,0:T(8,128)(2,1)S(1)}, u32[]{:S(2)}, u32[]{:S(2)}) %collective-permute-start.8) | collective-permute-done | bytes 131104 | tf_op jit(solution)/shard_map/ppermute | solution.py:247
  104.9 0.0 collective-permute-done.10.refs_5_
  104.9 1.7 %collect.1 = (bf16[512,256]{1,0:T(8,128)(2,1)}, bf16[512,256]{1,0:T(8,128)(2,1)}) custom-call(s32[6,64]{1,0:T(8,128)S(1)} %bitcast.2, f32[512,256]{1,0:T(8,128)S(1)} %get-tuple-element.46.gk_ref, f32[512,256]{1,0:T(8,128)S(1)} %get-tuple-element.47.gv_ref, bf16[128,512]{1,0:T(8,128)(2,1)S(1)} %collective-permute-done.5.refs_0_, ...), custom_call_target="tpu_custom_call" | custom-call | tf_op jit(solution)/shard_map/collect/pallas_call | solution.py:332
  (13 shorter events, 0.1 us)
Async XLA Ops:
  0.6 71.1 %copy-start = (bf16[512,256]{1,0:T(8,128)(2,1)S(1)}, bf16[512,256]{1,0:T(8,128)(2,1)}, u32[]{:S(2)}) copy-start(bf16[512,256]{1,0:T(8,128)(2,1)} %v_ref.3) | copy-start | bytes 786436
  0.6 45.8 %copy-start.2 = (bf16[512,256]{1,0:T(8,128)(2,1)S(1)}, bf16[512,256]{1,0:T(8,128)(2,1)}, u32[]{:S(2)}) copy-start(bf16[512,256]{1,0:T(8,128)(2,1)} %k_ref.1) | copy-start | bytes 786436
  0.7 45.8 %copy-start.1 = (bf16[512,256]{1,0:T(8,128)(2,1)S(1)}, bf16[512,256]{1,0:T(8,128)(2,1)}, u32[]{:S(2)}) copy-start(bf16[512,256]{1,0:T(8,128)(2,1)} %q_ref.1) | copy-start | bytes 786436
  0.7 71.1 %copy-start.3 = (bf16[512,256]{1,0:T(8,128)(2,1)S(1)}, bf16[512,256]{1,0:T(8,128)(2,1)}, u32[]{:S(2)}) copy-start(bf16[512,256]{1,0:T(8,128)(2,1)} %d_ref.3) | copy-start | bytes 786436
  0.7 0.8 copy-start.4
  3.9 26.4 %collective-permute-start = (bf16[256,512]{1,0:T(8,128)(2,1)S(1)}, bf16[256,512]{1,0:T(8,128)(2,1)S(1)}, u32[]{:S(2)}, u32[]{:S(2)}) collective-permute-start(bf16[256,512]{1,0:T(8,128)(2,1)S(1)} %get-tuple-element.35), channel_id=1, source_target_pairs={{0,16},{16,0},{32,48},{48,32},{64,80},{80,64},{96,112},{112,96},{1... | collective-permute-start | bytes 786440 | tf_op jit(solution)/shard_map/ppermute | solution.py:247
  5.9 40.6 %all-to-all-start = ((f32[16,8,128]{2,1,0:T(8,128)}), f32[16,8,128]{2,1,0:T(8,128)S(1)}, u32[]{:S(2)}, u32[]{:S(2)}) async-start(f32[16,8,128]{2,1,0:T(8,128)} %get-tuple-element.30), calls=%async_computation | async-start | bytes 131072 | tf_op jit(solution)/shard_map/all_to_all | solution.py:289
  30.4 41.4 %collective-permute-start.4 = (bf16[256,512]{1,0:T(8,128)(2,1)S(1)}, bf16[256,512]{1,0:T(8,128)(2,1)S(1)}, u32[]{:S(2)}, u32[]{:S(2)}) collective-permute-start(bf16[256,512]{1,0:T(8,128)(2,1)S(1)} %get-tuple-element.56), channel_id=1, source_target_pairs={{0,32},{32,0},{16,48},{48,16},{64,96},{96,64},{80,112},{112,80},{1... | collective-permute-start | bytes 786440 | tf_op jit(solution)/shard_map/ppermute | solution.py:247
  33.8 38.0 %collective-permute-start.3 = (bf16[256,512]{1,0:T(8,128)(2,1)S(1)}, bf16[256,512]{1,0:T(8,128)(2,1)S(1)}, u32[]{:S(2)}, u32[]{:S(2)}) collective-permute-start(bf16[256,512]{1,0:T(8,128)(2,1)S(1)} %get-tuple-element.57), channel_id=1, source_target_pairs={{32,64},{64,32},{48,80},{80,48},{96,128},{128,96},{112,144},{144,1... | collective-permute-start | bytes 786440 | tf_op jit(solution)/shard_map/ppermute | solution.py:247
  41.7 22.9 %collective-permute-start.1 = (bf16[128,512]{1,0:T(8,128)(2,1)S(1)}, bf16[128,512]{1,0:T(8,128)(2,1)S(1)}, u32[]{:S(2)}, u32[]{:S(2)}) collective-permute-start(bf16[128,512]{1,0:T(8,128)(2,1)S(1)} %get-tuple-element.36), channel_id=1, source_target_pairs={{64,128},{128,64},{80,144},{144,80},{96,160},{160,96},{112,176},{1... | collective-permute-start | bytes 393224 | tf_op jit(solution)/shard_map/ppermute | solution.py:247
  43.6 21.0 %collective-permute-start.2 = (bf16[128,512]{1,0:T(8,128)(2,1)S(1)}, bf16[128,512]{1,0:T(8,128)(2,1)S(1)}, u32[]{:S(2)}, u32[]{:S(2)}) collective-permute-start(bf16[128,512]{1,0:T(8,128)(2,1)S(1)} %get-tuple-element.37), channel_id=1, source_target_pairs={{0,64},{64,0},{16,80},{80,16},{32,96},{96,32},{48,112},{112,48},{1... | collective-permute-start | bytes 393224 | tf_op jit(solution)/shard_map/ppermute | solution.py:247
  47.1 24.6 %all-to-all-start.1 = ((f32[64,1,128]{2,1,0:T(1,128)}), f32[64,1,128]{2,1,0:T(1,128)S(1)}, u32[]{:S(2)}, u32[]{:S(2)}) async-start(f32[64,1,128]{2,1,0:T(1,128)} %get-tuple-element.32), calls=%async_computation.1 | async-start | bytes 65536 | tf_op jit(solution)/shard_map/all_to_all | solution.py:299
  76.8 19.6 %collective-permute-start.5 = (bf16[128,512]{1,0:T(8,128)(2,1)S(1)}, bf16[128,512]{1,0:T(8,128)(2,1)S(1)}, u32[]{:S(2)}, u32[]{:S(2)}) collective-permute-start(bf16[128,512]{1,0:T(8,128)(2,1)S(1)} %get-tuple-element.48), channel_id=1, source_target_pairs={{64,128},{128,64},{80,144},{144,80},{96,160},{160,96},{112,176},{1... | collective-permute-start | bytes 393224 | tf_op jit(solution)/shard_map/ppermute | solution.py:247
  80.2 20.6 %collective-permute-start.6 = (bf16[128,512]{1,0:T(8,128)(2,1)S(1)}, bf16[128,512]{1,0:T(8,128)(2,1)S(1)}, u32[]{:S(2)}, u32[]{:S(2)}) collective-permute-start(bf16[128,512]{1,0:T(8,128)(2,1)S(1)} %get-tuple-element.49), channel_id=1, source_target_pairs={{32,64},{64,32},{48,80},{80,48},{96,128},{128,96},{112,144},{144,1... | collective-permute-start | bytes 393224 | tf_op jit(solution)/shard_map/ppermute | solution.py:247
  88.9 14.1 %collective-permute-start.7 = (bf16[128,512]{1,0:T(8,128)(2,1)S(1)}, bf16[128,512]{1,0:T(8,128)(2,1)S(1)}, u32[]{:S(2)}, u32[]{:S(2)}) collective-permute-start(bf16[128,512]{1,0:T(8,128)(2,1)S(1)} %get-tuple-element.50), channel_id=1, source_target_pairs={{16,32},{32,16},{48,64},{64,48},{80,96},{96,80},{112,128},{128,112... | collective-permute-start | bytes 393224 | tf_op jit(solution)/shard_map/ppermute | solution.py:247
  92.5 12.4 %collective-permute-start.8 = (bf16[128,512]{1,0:T(8,128)(2,1)S(1)}, bf16[128,512]{1,0:T(8,128)(2,1)S(1)}, u32[]{:S(2)}, u32[]{:S(2)}) collective-permute-start(bf16[128,512]{1,0:T(8,128)(2,1)S(1)} %get-tuple-element.51), channel_id=1, source_target_pairs={{0,64},{64,0},{16,80},{80,16},{32,96},{96,32},{48,112},{112,48},{1... | collective-permute-start | bytes 393224 | tf_op jit(solution)/shard_map/ppermute | solution.py:247
  94.4 10.5 %collective-permute-start.9 = (bf16[128,512]{1,0:T(8,128)(2,1)S(1)}, bf16[128,512]{1,0:T(8,128)(2,1)S(1)}, u32[]{:S(2)}, u32[]{:S(2)}) collective-permute-start(bf16[128,512]{1,0:T(8,128)(2,1)S(1)} %get-tuple-element.52), channel_id=1, source_target_pairs={{0,32},{32,0},{16,48},{48,16},{64,96},{96,64},{80,112},{112,80},{1... | collective-permute-start | bytes 393224 | tf_op jit(solution)/shard_map/ppermute | solution.py:247
  96.4 8.5 %collective-permute-start.10 = (bf16[128,512]{1,0:T(8,128)(2,1)S(1)}, bf16[128,512]{1,0:T(8,128)(2,1)S(1)}, u32[]{:S(2)}, u32[]{:S(2)}) collective-permute-start(bf16[128,512]{1,0:T(8,128)(2,1)S(1)} %get-tuple-element.53), channel_id=1, source_target_pairs={{0,16},{16,0},{32,48},{48,32},{64,80},{80,64},{96,112},{112,96},{1... | collective-permute-start | bytes 393224 | tf_op jit(solution)/shard_map/ppermute | solution.py:247
  98.3 6.6 %copy-start.5 = (s32[64,6]{0,1:T(8,128)S(1)}, s32[64,6]{0,1:T(8,128)}, u32[]{:S(2)}) copy-start(s32[64,6]{0,1:T(8,128)} %param.9) | copy-start | bytes 4612
